TPU v7x, 512 devices: a whole 4x4x16 slice. The times are simulated.
512 devices in a mesh: cluster: 64 (over y, z), member: 8 (over x, core).
Axes of the slice: x: 4, y: 4, z: 16, core: 2. Of those that a mesh axis runs over, the one named last changes fastest.
Arguments:
- leaf_centers: float32 [3, 512], replicated, may hold values from 0 to 1
- source_coords: float32 [3, 65536], P(None, ('cluster', 'member')), may hold values from -1 to 1
- target_points: float32 [3, 65536], P(None, ('cluster', 'member')), may hold values from 0 to 1
- charges: float32 [8, 65536], P(None, ('cluster', 'member')), may hold values from -6 to 6
- boundary_data: float32 [8, 65536], P(None, ('cluster', 'member')), may hold values from -6 to 6
- step_sizes: float32 [8], replicated, may hold values from 0.2 to 1
- valid_count: int32 [512], P(('cluster', 'member')), may hold values from 64 to 128, as said below
- near_lists: int32 [64, 26], replicated, may hold values from 0 to 63, as said below
Outputs:
- new_charges: float32 [8, 65536], P(None, ('cluster', 'member'))
- residual: float32 [8, 65536], P(None, ('cluster', 'member'))
Inputs may be any that keep to these rules, and one draw needn't show every extreme that they name: `valid_count`: some leaf has 128 live slots and some has half of 128. `near_lists`: row c names 26 different clusters, none of them c.
All inputs are finite; a program needn't handle non-finite values.
Results may differ from a plain program's by a relative error of at most 0.0003.
Values sent between devices are 32-bit elements; how exact they have to be, the bound alone decides.
No kernel may reach another device: no remote copies, remote signals or barrier semaphores. Data moves between devices by JAX's collectives and lax.ppermute only.
A program may use at most 64 MiB of HBM per device.

v0:
```python
import math

import jax
import jax.numpy as jnp
import numpy as np
from jax import lax
from jax.sharding import PartitionSpec as P

ITERS = 2


HALF_SIDE = 0.08
SOFTENING = 0.0025


def cheby_nodes(number):
    return np.cos(np.pi * (2 * np.arange(number) + 1) / (2 * number))


def basis_line(coord, number):
    nodes = cheby_nodes(number)
    factors = []
    for first in range(number):
        factor = jnp.ones_like(coord)
        for other in range(number):
            if other != first:
                factor = factor * (coord - nodes[other]) / (nodes[first] - nodes[other])
        factors.append(factor)
    return jnp.stack(factors, 0)


def lagrange(coords):
    along_x = basis_line(coords[0], 2)
    along_y = basis_line(coords[1], 4)
    along_z = basis_line(coords[2], 4)
    joined = along_x[:, None, None, :] * along_y[None, :, None, :] * along_z[None, None, :, :]
    return joined.reshape(32, coords.shape[1])


def proxy_grid():
    grid_x, grid_y, grid_z = np.meshgrid(
        cheby_nodes(2), cheby_nodes(4), cheby_nodes(4), indexing="ij"
    )
    return jnp.asarray(
        np.stack([grid_x.reshape(-1), grid_y.reshape(-1), grid_z.reshape(-1)], 0), jnp.float32
    )


def potential(targets, sources, weights):
    target_count = targets.shape[1]
    source_count = sources.shape[1]
    limit = max(128, (1 << 20) // target_count)
    src_block = math.gcd(source_count, limit)

    def advance(turn, running):
        pts = lax.dynamic_slice_in_dim(sources, turn * src_block, src_block, 1)
        wts = lax.dynamic_slice_in_dim(weights, turn * src_block, src_block, 1)
        distance = (pts[0][:, None] - targets[0][None, :]) ** 2
        distance = distance + (pts[1][:, None] - targets[1][None, :]) ** 2
        distance = distance + (pts[2][:, None] - targets[2][None, :]) ** 2
        kernel = lax.rsqrt(distance + SOFTENING)
        return running + jnp.dot(
            wts, kernel, precision=lax.Precision.HIGHEST, preferred_element_type=jnp.float32
        )

    start_value = jnp.zeros((weights.shape[0], target_count), jnp.float32)
    return lax.fori_loop(0, source_count // src_block, advance, start_value)


def flatten_packets(packets):
    return jnp.moveaxis(packets, 1, 0).reshape(packets.shape[1], -1)


def body(
    leaf_centers,
    source_coords,
    target_points,
    charges,
    boundary_data,
    step_sizes,
    valid_count,
    near_lists,
):
    clusters = lax.axis_size("cluster")
    members = lax.axis_size("member")
    leaf_size = source_coords.shape[1]
    proxies = 32
    cluster_index = lax.axis_index("cluster")
    member_index = lax.axis_index("member")
    leaf_index = cluster_index * members + member_index
    center = lax.dynamic_slice_in_dim(leaf_centers, leaf_index, 1, 1)
    source_points = center + HALF_SIDE * source_coords
    live = (jnp.arange(leaf_size, dtype=jnp.int32) < valid_count[0]).astype(jnp.float32)
    interp = lagrange(source_coords)
    offsets = proxy_grid()
    proxy_points = leaf_centers[:, :, None] + HALF_SIDE * offsets[:, None, :]
    my_near = lax.dynamic_index_in_dim(near_lists, cluster_index, 0, keepdims=False)
    listed = jnp.any(near_lists == cluster_index, axis=1)
    own_near = jnp.concatenate([jnp.reshape(cluster_index, (1,)), my_near])
    cluster_ids = jnp.arange(clusters, dtype=jnp.int32)
    far_cluster = jnp.all(cluster_ids[:, None] != own_near[None, :], axis=1).astype(jnp.float32)
    scale = 1.0 / math.sqrt(clusters * members * leaf_size)

    def outgoing(packet):
        return jnp.where(listed[:, None, None], packet[None], jnp.zeros_like(packet)[None])

    def select(received, own_piece):
        return jnp.concatenate([own_piece[None], jnp.take(received, my_near, axis=0)], 0)

    arrived_points = lax.all_to_all(
        outgoing(source_points), "cluster", split_axis=0, concat_axis=0, tiled=True
    )
    near_points = select(arrived_points, source_points)
    all_near_points = lax.all_gather(near_points, "member", axis=0, tiled=True)
    every_far = jnp.repeat(far_cluster, members * proxies)
    every_proxy = proxy_points.reshape(3, -1)
    current = charges * live
    residual = current
    for turn in range(ITERS):
        proxy_charges = jnp.einsum("fj,pj->fp", current, interp, precision=lax.Precision.HIGHEST)
        arrived_charges = lax.all_to_all(
            outgoing(current), "cluster", split_axis=0, concat_axis=0, tiled=True
        )
        near_charges = select(arrived_charges, current)
        near_sum = potential(
            target_points,
            flatten_packets(all_near_points),
            flatten_packets(lax.all_gather(near_charges, "member", axis=0, tiled=True)),
        )
        piece = lax.all_gather(proxy_charges, ("cluster", "member"), axis=1, tiled=True)
        positions = lax.slice_in_dim(every_proxy, 0, piece.shape[1], axis=1)
        far_sum = potential(target_points, positions, piece * every_far[None, :])
        field_sum = near_sum + far_sum
        residual = live * (boundary_data - scale * field_sum)
        current = live * (current + step_sizes[:, None] * residual / (1.0 + jnp.abs(residual)))
    return (current, residual)


def solution(mesh):
    in_specs = (
        P(),
        P(None, ("cluster", "member")),
        P(None, ("cluster", "member")),
        P(None, ("cluster", "member")),
        P(None, ("cluster", "member")),
        P(),
        P(("cluster", "member")),
        P(),
    )
    out_specs = (P(None, ("cluster", "member")), P(None, ("cluster", "member")))
    return jax.shard_map(body, mesh=mesh, in_specs=in_specs, out_specs=out_specs, check_vma=False)
```

profile of v0, /device:TPU:1, one launch (start us, length us, event | category | flops | bytes accessed | tf_op | source)
XLA Modules:
  0.0 408.0 jit_solution(5029262380854414042)
XLA Ops:
  1.4 0.9 dynamic-slice_reduce_fusion.1
  3.0 0.8 broadcast_select_fusion.2
  3.8 19.3 %all-to-all-start.1 = ((f32[64,3,128]{2,1,0:T(4,128)}), f32[64,3,128]{2,1,0:T(4,128)S(1)}, u32[]{:S(2)}, u32[]{:S(2)}) async-start(f32[64,3,128]{2,1,0:T(4,128)} %broadcast_select_fusion.2), calls=%async_computation.1 | async-start | bytes 262144 | tf_op jit(solution)/shard_map/all_to_all | solution.py:110
  23.1 0.9 dynamic-slice_reduce_fusion
  24.0 0.8 add_multiply_fusion.3
  26.4 117.8 %all-gather = f32[512,32,8]{1,2,0:T(8,128)S(1)} all-gather(f32[1,32,8]{1,2,0:T(8,128)S(1)} %convolution_bitcast_fusion.1), channel_id=1, replica_groups=mesh['cluster'=64,'member'=8] {'cluster','member'}, dimensions={0}, use_global_device_ids=true | all-gather | bytes 525312 | tf_op jit(solution)/shard_map/all_gather | solution.py:130
  144.5 1.0 reshape.131
  146.6 10.0 %while.57 = (s32[]{:T(128)}, f32[8,128]{1,0:T(8,128)S(1)}, f32[8,16384]{1,0:T(8,128)S(1)}, f32[3,16384]{1,0:T(4,128)S(1)}, f32[3,128]{1,0:T(4,128)S(1)}, /*index...) while((s32[]{:T(128)}, f32[8,128]{1,0:T(8,128)S(1)}, ...), condition=%wide.region_5.7_spmd.clone, body=%wide.region_4.6_spmd.clone.sunk | while | flops 110102536 | bytes 570069 | solution.py:67
  146.9 4.8 %fusion.110 = f32[8,128]{1,0:T(8,128)S(1)} fusion(f32[128]{0:T(128)S(1)} %get-tuple-element.677, f32[8192]{0:T(1024)S(1)} %bitcast.113, f32[128]{0:T(128)S(1)} %get-tuple-element.679, f32[8192]{0:T(1024)S(1)} %bitcast.112, f32[128]{0:T(128)S(1)} %get-tuple-element.681, f32[8192]{0:T(1024)S(1)} %bitcast.111, f32[8,16384]{1,0:T(8,128)S(1)} %get-tuple-element.762, ...), kind=kOutput, calls=%fused_computation.46.clone.1 | convolution fusion | flops 110102528 | bytes 370181 | tf_op jit(solution)/shard_map/while/body/eval_jaxpr/dot_general | solution.py:62
  151.9 4.8 %fusion.110 = f32[8,128]{1,0:T(8,128)S(1)} fusion(f32[128]{0:T(128)S(1)} %get-tuple-element.677, f32[8192]{0:T(1024)S(1)} %bitcast.113, f32[128]{0:T(128)S(1)} %get-tuple-element.679, f32[8192]{0:T(1024)S(1)} %bitcast.112, f32[128]{0:T(128)S(1)} %get-tuple-element.681, f32[8192]{0:T(1024)S(1)} %bitcast.111, f32[8,16384]{1,0:T(8,128)S(1)} %get-tuple-element.762, ...), kind=kOutput, calls=%fused_computation.46.clone.1 | convolution fusion | flops 110102528 | bytes 370181 | tf_op jit(solution)/shard_map/while/body/eval_jaxpr/dot_general | solution.py:62
  156.7 0.8 broadcast_select_fusion.1
  157.6 11.6 %all-to-all-start = ((f32[64,8,128]{2,1,0:T(8,128)}), f32[64,8,128]{2,1,0:T(8,128)S(1)}, u32[]{:S(2)}, u32[]{:S(2)}) async-start(f32[64,8,128]{2,1,0:T(8,128)} %broadcast_select_fusion.1), calls=%async_computation | async-start | bytes 524288 | tf_op jit(solution)/shard_map/all_to_all | solution.py:121
  170.0 13.3 %all_gather.16 = f32[216,3,128]{2,1,0:T(4,128)S(1)} all-gather(f32[27,3,128]{2,1,0:T(4,128)S(1)} %pad_maximum_fusion.2), channel_id=1, replica_groups=mesh['cluster'=64,'member'=8] {'member'}, dimensions={0}, use_global_device_ids=true | all-gather | bytes 373248 | tf_op jit(solution)/shard_map/all_gather | solution.py:114
  183.3 5.9 %all-to-all-done = f32[64,8,128]{2,1,0:T(8,128)S(1)} async-done(((f32[64,8,128]{2,1,0:T(8,128)}), f32[64,8,128]{2,1,0:T(8,128)S(1)}, u32[]{:S(2)}, u32[]{:S(2)}) %all-to-all-start) | async-done | bytes 262176 | tf_op jit(solution)/shard_map/all_to_all | solution.py:121
  189.9 15.3 %all_gather.15 = f32[216,8,128]{2,1,0:T(8,128)S(1)} all-gather(f32[27,8,128]{2,1,0:T(8,128)S(1)} %pad_maximum_fusion), channel_id=1, replica_groups=mesh['cluster'=64,'member'=8] {'member'}, dimensions={0}, use_global_device_ids=true | all-gather | bytes 995328 | tf_op jit(solution)/shard_map/all_gather | solution.py:128
  205.2 23.9 %while.56 = (s32[]{:T(128)}, f32[8,128]{1,0:T(8,128)S(1)}, f32[8,27648]{1,0:T(8,128)S(1)}, f32[3,27648]{1,0:T(4,128)S(1)}, f32[3,128]{1,0:T(4,128)S(1)}, /*index...) while((s32[]{:T(128)}, f32[8,128]{1,0:T(8,128)S(1)}, ...), condition=%wide.region_2.4_spmd.clone, body=%wide.region_1.0_spmd.clone.sunk | while | flops 13764617 | bytes 82645 | solution.py:67
  207.0 0.8 convolution_add_fusion.4
  207.9 0.8 convolution_add_fusion.4
  208.8 0.8 convolution_add_fusion.4
  213.2 0.8 convolution_add_fusion.4
  214.1 0.8 convolution_add_fusion.4
  218.5 0.8 convolution_add_fusion.4
  229.1 0.8 broadcast_select_fusion
  230.1 7.5 %all-to-all-start.2 = ((f32[64,8,128]{2,1,0:T(8,128)}), f32[64,8,128]{2,1,0:T(8,128)}, u32[]{:S(2)}, u32[]{:S(2)}) async-start(f32[64,8,128]{2,1,0:T(8,128)} %broadcast_select_fusion), calls=%async_computation.2 | async-start | bytes 524288 | tf_op jit(solution)/shard_map/all_to_all | solution.py:121
  237.6 119.2 %all-gather.1 = f32[512,32,8]{1,2,0:T(8,128)S(1)} all-gather(f32[1,32,8]{1,2,0:T(8,128)S(1)} %convolution_bitcast_fusion), channel_id=1, replica_groups=mesh['cluster'=64,'member'=8] {'cluster','member'}, dimensions={0}, use_global_device_ids=true | all-gather | bytes 525312 | tf_op jit(solution)/shard_map/all_gather | solution.py:130
  357.2 1.0 reshape.133
  358.2 10.0 %while.59 = (s32[]{:T(128)}, f32[8,128]{1,0:T(8,128)S(1)}, f32[8,16384]{1,0:T(8,128)S(1)}, f32[3,16384]{1,0:T(4,128)S(1)}, f32[3,128]{1,0:T(4,128)S(1)}, /*index...) while((s32[]{:T(128)}, f32[8,128]{1,0:T(8,128)S(1)}, ...), condition=%wide.region_9.11_spmd.clone, body=%wide.region_8.10_spmd.clone.sunk | while | flops 110102536 | bytes 570069 | solution.py:67
  358.5 4.8 %fusion.115 = f32[8,128]{1,0:T(8,128)S(1)} fusion(f32[128]{0:T(128)S(1)} %get-tuple-element.699, f32[8192]{0:T(1024)S(1)} %bitcast.116, f32[128]{0:T(128)S(1)} %get-tuple-element.701, f32[8192]{0:T(1024)S(1)} %bitcast.115, f32[128]{0:T(128)S(1)} %get-tuple-element.703, f32[8192]{0:T(1024)S(1)} %bitcast.114, f32[8,16384]{1,0:T(8,128)S(1)} %get-tuple-element.828, ...), kind=kOutput, calls=%fused_computation.97.clone.1 | convolution fusion | flops 110102528 | bytes 370181 | tf_op jit(solution)/shard_map/while/body/eval_jaxpr/dot_general | solution.py:62
  363.5 4.8 %fusion.115 = f32[8,128]{1,0:T(8,128)S(1)} fusion(f32[128]{0:T(128)S(1)} %get-tuple-element.699, f32[8192]{0:T(1024)S(1)} %bitcast.116, f32[128]{0:T(128)S(1)} %get-tuple-element.701, f32[8192]{0:T(1024)S(1)} %bitcast.115, f32[128]{0:T(128)S(1)} %get-tuple-element.703, f32[8192]{0:T(1024)S(1)} %bitcast.114, f32[8,16384]{1,0:T(8,128)S(1)} %get-tuple-element.828, ...), kind=kOutput, calls=%fused_computation.97.clone.1 | convolution fusion | flops 110102528 | bytes 370181 | tf_op jit(solution)/shard_map/while/body/eval_jaxpr/dot_general | solution.py:62
  368.3 1.5 gather_fusion.2
  369.9 13.5 %all_gather.18 = f32[216,8,128]{2,1,0:T(8,128)S(1)} all-gather(f32[27,8,128]{2,1,0:T(8,128)S(1)} %pad_maximum_fusion.1), channel_id=1, replica_groups=mesh['cluster'=64,'member'=8] {'member'}, dimensions={0}, use_global_device_ids=true | all-gather | bytes 995328 | tf_op jit(solution)/shard_map/all_gather | solution.py:128
  383.4 23.9 %while.58 = (s32[]{:T(128)}, f32[8,128]{1,0:T(8,128)S(1)}, f32[8,27648]{1,0:T(8,128)S(1)}, f32[3,27648]{1,0:T(4,128)S(1)}, f32[3,128]{1,0:T(4,128)S(1)}, /*index...) while((s32[]{:T(128)}, f32[8,128]{1,0:T(8,128)S(1)}, ...), condition=%wide.region_7.9_spmd.clone, body=%wide.region_6.8_spmd.clone.sunk | while | flops 13764617 | bytes 82645 | solution.py:67
  (222 shorter events, 49.0 us)
Async XLA Ops:
  3.8 153.8 %all-to-all-start.1 = ((f32[64,3,128]{2,1,0:T(4,128)}), f32[64,3,128]{2,1,0:T(4,128)S(1)}, u32[]{:S(2)}, u32[]{:S(2)}) async-start(f32[64,3,128]{2,1,0:T(4,128)} %broadcast_select_fusion.2), calls=%async_computation.1 | async-start | bytes 262144 | tf_op jit(solution)/shard_map/all_to_all | solution.py:110
  144.5 1.3 copy-start.4
  144.5 1.3 copy-start.5
  145.5 1.1 copy-start
  146.6 22.6 %copy-start.3 = (f32[3,128]{1,0:T(4,128)S(1)}, f32[3,128]{1,0:T(4,128)}, u32[]{:S(2)}) copy-start(f32[3,128]{1,0:T(4,128)} %param.20) | copy-start | bytes 4612
  146.6 22.6 %copy-start.1 = (f32[8,128]{1,0:T(8,128)S(1)}, f32[8,128]{1,0:T(8,128)}, u32[]{:S(2)}) copy-start(f32[8,128]{1,0:T(8,128)} %param.22) | copy-start | bytes 12292
  157.6 31.7 %all-to-all-start = ((f32[64,8,128]{2,1,0:T(8,128)}), f32[64,8,128]{2,1,0:T(8,128)S(1)}, u32[]{:S(2)}, u32[]{:S(2)}) async-start(f32[64,8,128]{2,1,0:T(8,128)} %broadcast_select_fusion.1), calls=%async_computation | async-start | bytes 524288 | tf_op jit(solution)/shard_map/all_to_all | solution.py:121
  205.2 23.9 %copy-start.2 = (f32[8,128]{1,0:T(8,128)S(1)}, f32[8,128]{1,0:T(8,128)}, u32[]{:S(2)}) copy-start(f32[8,128]{1,0:T(8,128)} %param.23) | copy-start | bytes 12292
  205.2 23.9 %copy-start.6 = (f32[8]{0:T(128)S(1)}, f32[8]{0:T(128)}, u32[]{:S(2)}) copy-start(f32[8]{0:T(128)} %param.24) | copy-start | bytes 100
  230.1 138.2 %all-to-all-start.2 = ((f32[64,8,128]{2,1,0:T(8,128)}), f32[64,8,128]{2,1,0:T(8,128)}, u32[]{:S(2)}, u32[]{:S(2)}) async-start(f32[64,8,128]{2,1,0:T(8,128)} %broadcast_select_fusion), calls=%async_computation.2 | async-start | bytes 524288 | tf_op jit(solution)/shard_map/all_to_all | solution.py:121
where the time goes:
time: 409 us; the launch traced here: 408 us
  blocking collectives  279 us (68%)
  matrix products  60.2 us (15%)
  starting transfers between devices  38.4 us (9%)
  local copies, waits for them, and re-layouts  13.7 us (3%)
  other arithmetic  7.24 us (2%)
  waiting for transfers between devices  5.93 us (1%)
    all_gather x2, blocking collectives, body(): lax.all_gather(proxy_charges, ('cluster', 'member'), axis=1, tiled=True)  237 us
    dot_general x58, matrix products, advance(): jnp.dot(wts, kernel, precision=lax.Precision.HIGHEST, preferred_element_t...  60 us
    all_gather x2, blocking collectives, body(): lax.all_gather(near_charges, 'member', axis=0, tiled=True)  28.7 us
    all_to_all x1, starting transfers between devices, body(): lax.all_to_all(outgoing(source_points), 'cluster', split_axis=0, concat_a...  19.3 us
    all_to_all x2, starting transfers between devices, body(): lax.all_to_all(outgoing(current), 'cluster', split_axis=0, concat_axis=0,...  19.1 us
    all_gather x1, blocking collectives, body(): all_near_points = lax.all_gather(near_points, 'member', axis=0, tiled=True)  13.3 us
  transfers between devices with their start and end apart: 3, of which 1 were waited for; matrix products, arithmetic and copies ran while one was open for 7% of the time, Pallas kernels for 0%

commit v1 on v0

v1 whole, which is shorter than its diff:
```python
import functools
import math

import jax
import jax.numpy as jnp
import numpy as np
from jax import lax
from jax.experimental import pallas as pl
from jax.experimental.pallas import tpu as pltpu
from jax.sharding import Mesh
from jax.sharding import PartitionSpec as P

HALF_SIDE = 0.08
SOFTENING = 0.0025
NY, NZ, NX, NC = 4, 16, 4, 2
MEMBERS = NX * NC
PLANE = NY * MEMBERS
NEAR = 26
DEPTH = 48
ZERO_BLOCK = NZ
FAR_A = NZ + 1
A_BLOCKS = FAR_A + 4
FAR_Q = NZ + 1
Q_BLOCKS = FAR_Q + 4 * NY
SLOTS = 32
bf16, f32 = jnp.bfloat16, jnp.float32


def cheby_nodes(number):
    return np.cos(np.pi * (2 * np.arange(number) + 1) / (2 * number))


def pick(index, values):
    out = jnp.full(index.shape, float(values[0]), f32)
    for k in range(1, len(values)):
        out = jnp.where(index == k, float(values[k]), out)
    return out


def iota(shape, dim):
    return lax.broadcasted_iota(jnp.int32, shape, dim)


def split3(v):
    h = v.astype(bf16).astype(f32)
    r = v - h
    m = r.astype(bf16).astype(f32)
    low = (r - m).astype(bf16).astype(f32)
    return h, m, low


def split2(v):
    h = v.astype(bf16)
    return h, (v - h.astype(f32)).astype(bf16)


def source_rows(pts, extra):
    row = iota(pts.shape, 0)
    s = jnp.where(row < 3, pts - 0.5, 0.0)
    norm = jnp.sum(s * s, axis=0, keepdims=True) + SOFTENING
    return jnp.where(row < 3, -2.0 * s, jnp.where(row == 3, norm, jnp.where(row == 4, 1.0, extra)))


def target_rows(pts):
    row = iota(pts.shape, 0)
    t = jnp.where(row < 3, pts - 0.5, 0.0)
    norm = jnp.sum(t * t, axis=0, keepdims=True)
    return jnp.where(row < 3, t, jnp.where(row == 3, 1.0, jnp.where(row == 4, norm, 0.0)))


def column3(a, b, c, shape):
    row = iota(shape, 0)
    return jnp.where(row == 0, a, jnp.where(row == 1, b, jnp.where(row == 2, c, 0.0)))


def prologue_kernel(leaf_ref, count_ref, centers_ref, charges_ref, coords_ref, targets_ref, zsend_ref, tsend_ref, current_ref):
    leaf = leaf_ref[0]
    shape = (8, 128)
    lane = iota(shape, 1)
    live = (lane < count_ref[0]).astype(f32)
    current = charges_ref[...] * live
    current_ref[...] = current
    u = jnp.concatenate([coords_ref[...], jnp.zeros((5, 128), f32)], 0)
    center = column3(centers_ref[0, leaf], centers_ref[1, leaf], centers_ref[2, leaf], shape)
    pts = center + HALF_SIDE * u
    shifted = jnp.concatenate([jnp.zeros((5, 128), f32), coords_ref[...]], 0)
    rows = source_rows(pts, shifted)
    for k in range(NZ):
        zsend_ref[k, 0:8] = current
        zsend_ref[k, 8:16] = rows
    trows = target_rows(jnp.concatenate([targets_ref[...], jnp.zeros((5, 128), f32)], 0))
    for k in range(PLANE):
        tsend_ref[k] = trows


def a_block(rows):
    rows = jnp.where(iota(rows.shape, 0) < 5, rows, 0.0)
    h, m, low = split3(rows)
    return jnp.concatenate([h, h, m, m, h, low], 0).T.astype(bf16)


def interp_tables():
    p = iota((32, 128), 0)
    parts = (p >> 4, (p >> 2) & 3, p & 3)
    tables = []
    for index, number in zip(parts, (2, 4, 4)):
        nodes = cheby_nodes(number)
        others = [[nodes[i] for i in range(number) if i != k] for k in range(number)]
        roots = [pick(index, [others[k][j] for k in range(number)]) for j in range(number - 1)]
        scale = pick(index, [1.0 / np.prod([nodes[k] - o for o in others[k]]) for k in range(number)])
        tables.append((roots, scale))
    return tables


def setup_kernel(pos_ref, centers_ref, near_ref, recv_ref, tgt_ref, a_ref, b_ref, ih_ref, il_ref, list_ref, cnt_ref, mask_ref):
    y, z, member = pos_ref[0], pos_ref[1], pos_ref[2]
    tables = interp_tables()
    for k in range(NZ):
        rows = recv_ref[k, 8:16]
        a_ref[k * 128 : (k + 1) * 128, :DEPTH] = a_block(rows)
        value = None
        for axis, (roots, scale) in enumerate(tables):
            u = jnp.broadcast_to(rows[5 + axis : 6 + axis], (32, 128))
            line = scale
            for root in roots:
                line = line * (u - root)
            value = line if value is None else value * line
        hi, lo = split2(value)
        ih_ref[k * 32 : (k + 1) * 32] = hi
        il_ref[k * 32 : (k + 1) * 32] = lo
    a_ref[ZERO_BLOCK * 128 : (ZERO_BLOCK + 1) * 128, :DEPTH] = a_ref[0:128, :DEPTH]
    lane = iota((8, 128), 1)
    p = lane & 31
    row = iota((8, 128), 0)
    offset = jnp.where(
        row == 0,
        pick(p >> 4, cheby_nodes(2)),
        jnp.where(row == 1, pick((p >> 2) & 3, cheby_nodes(4)), jnp.where(row == 2, pick(p & 3, cheby_nodes(4)), 0.0)),
    )
    for block in range(4):
        center = jnp.zeros((8, 128), f32)
        for k in range(4):
            leaf = (y * NZ + block * 4 + k) * MEMBERS + member
            column = column3(centers_ref[0, leaf], centers_ref[1, leaf], centers_ref[2, leaf], (8, 128))
            center = jnp.where((lane >> 5) == k, column, center)
        rows = source_rows(center + HALF_SIDE * offset, 0.0)
        a_ref[(FAR_A + block) * 128 : (FAR_A + block + 1) * 128, :DEPTH] = a_block(rows)
    for other in range(NY):
        rows = jnp.concatenate([tgt_ref[other * MEMBERS + k] for k in range(MEMBERS)], 1)
        h, m, low = split3(rows)
        b_ref[other] = jnp.concatenate([h, m, h, m, low, h], 0).astype(bf16)
    group = iota((1, 512), 1) >> 5
    for other in range(NY):
        own = (y == other).astype(jnp.int32)
        list_ref[other, 0] = z

        def visit(j, state):
            count, mask = state
            cluster = near_ref[j, other * NZ + z]
            mine = (cluster >> 4) == y
            zz = cluster & 15
            list_ref[other, count] = zz
            mask = jnp.where((group == zz) & mine, 0.0, mask)
            return count + mine.astype(jnp.int32), mask

        first = jnp.where((group == z) & (own > 0), 0.0, jnp.ones((1, 512), f32))
        count, mask = lax.fori_loop(0, NEAR, visit, (own, first))
        mask_ref[other] = jnp.broadcast_to(mask, (16, 512))
        for k in range(4):
            list_ref[other, count + k] = FAR_A + k
        for k in range(4, 8):
            list_ref[other, count + k] = ZERO_BLOCK
        cnt_ref[other] = (count + 4 + 3) // 4


def field_kernel(list_ref, cnt_ref, recv_ref, a_ref, b_ref, ih_ref, il_ref, mask_ref, out_ref, q_ref):
    far = []
    for k in range(NZ):
        hi, lo = split2(recv_ref[k, 0:8])
        q = jnp.concatenate([hi.astype(f32), lo.astype(f32)], 0).astype(bf16)
        q_ref[k] = q
        nt = (((1,), (1,)), ((), ()))
        both = lax.dot_general(q, ih_ref[k * 32 : (k + 1) * 32], nt, preferred_element_type=f32)
        both = both + lax.dot_general(q, il_ref[k * 32 : (k + 1) * 32], nt, preferred_element_type=f32)
        far.append(both[0:8] + both[8:16])
    far = jnp.concatenate(far, 1)
    hi = far.astype(bf16).astype(f32)
    far = jnp.concatenate([hi, far - hi], 0)
    q_ref[ZERO_BLOCK] = jnp.zeros((16, 128), bf16)
    for other in range(NY):
        masked = (far * mask_ref[other]).astype(bf16)
        for k in range(4):
            q_ref[FAR_Q + other * 4 + k] = masked[:, k * 128 : (k + 1) * 128]

    def per_cluster(other, carry):
        b = b_ref[other]

        def chunk(i, acc):
            blocks = [list_ref[other, i * 4 + k] for k in range(4)]
            a = jnp.concatenate([a_ref[pl.ds(pl.multiple_of(n * 128, 128), 128), :DEPTH] for n in blocks], 0)
            q = jnp.concatenate([q_ref[jnp.where(n >= FAR_A, n + other * 4, n)] for n in blocks], 1)
            square = jnp.dot(a, b, preferred_element_type=f32)
            hi, lo = split2(lax.rsqrt(square))
            acc = acc + jnp.dot(q, hi, preferred_element_type=f32)
            return acc + jnp.dot(q, lo, preferred_element_type=f32)

        acc = lax.fori_loop(0, cnt_ref[other], chunk, jnp.zeros((16, MEMBERS * 128), f32))
        total = acc[0:8] + acc[8:16]
        for k in range(MEMBERS):
            out_ref[other * MEMBERS + k] = total[:, k * 128 : (k + 1) * 128]
        return carry

    lax.fori_loop(0, NY, per_cluster, 0)


def update_kernel(scale, count_ref, steps_ref, recv_ref, boundary_ref, current_ref, new_ref, residual_ref, *zsend):
    parts = [recv_ref[k] for k in range(PLANE)]
    while len(parts) > 1:
        parts = [parts[i] + parts[i + 1] for i in range(0, len(parts), 2)]
    shape = (8, 128)
    live = (iota(shape, 1) < count_ref[0]).astype(f32)
    row = iota(shape, 0)
    steps = jnp.zeros(shape, f32)
    for k in range(8):
        steps = jnp.where(row == k, steps_ref[k], steps)
    residual = live * (boundary_ref[...] - scale * parts[0])
    new = live * (current_ref[...] + steps * residual / (1.0 + jnp.abs(residual)))
    new_ref[...] = new
    residual_ref[...] = residual
    for ref in zsend:
        for k in range(NZ):
            ref[k] = new


VM = pl.BlockSpec(memory_space=pltpu.VMEM)
SM = pl.BlockSpec(memory_space=pltpu.SMEM)


def sds(shape, dtype=f32):
    return jax.ShapeDtypeStruct(shape, dtype)


def body(leaf_centers, source_coords, target_points, charges, boundary_data, step_sizes, valid_count, near_lists):
    y, z = lax.axis_index("y"), lax.axis_index("z")
    member = lax.axis_index("x") * NC + lax.axis_index("core")
    leaf = (y * NZ + z) * MEMBERS + member
    pos = jnp.stack([y, z, member, leaf]).astype(jnp.int32)
    plane = ("y", "x", "core")
    params = pltpu.CompilerParams(vmem_limit_bytes=56 * 2**20)
    zsend, tsend, current = pl.pallas_call(
        prologue_kernel,
        out_shape=(sds((NZ, 16, 128)), sds((PLANE, 8, 128)), sds((8, 128))),
        in_specs=[SM, SM, SM, VM, VM, VM],
        out_specs=(VM, VM, VM),
        name="prologue",
    )(pos[3:], valid_count, leaf_centers, charges, source_coords, target_points)
    targets = lax.all_to_all(tsend, plane, 0, 0, tiled=True)
    recv = lax.all_to_all(zsend, "z", 0, 0, tiled=True)
    a, b, ih, il, lists, counts, mask = pl.pallas_call(
        setup_kernel,
        out_shape=(
            sds((A_BLOCKS * 128, 128), bf16),
            sds((NY, DEPTH, MEMBERS * 128), bf16),
            sds((NZ * 32, 128), bf16),
            sds((NZ * 32, 128), bf16),
            sds((NY, SLOTS), jnp.int32),
            sds((NY,), jnp.int32),
            sds((NY, 16, 512)),
        ),
        in_specs=[SM, SM, SM, VM, VM],
        out_specs=(VM, VM, VM, VM, SM, SM, VM),
        compiler_params=params,
        name="setup",
    )(pos, leaf_centers, near_lists.T, recv, targets)
    scale = 1.0 / math.sqrt(NY * NZ * MEMBERS * 128)
    residual = None
    for turn in range(2):
        sums = pl.pallas_call(
            field_kernel,
            out_shape=sds((PLANE, 8, 128)),
            in_specs=[SM, SM, VM, VM, VM, VM, VM, VM],
            out_specs=VM,
            scratch_shapes=[pltpu.VMEM((Q_BLOCKS, 16, 128), bf16)],
            compiler_params=params,
            name="field",
        )(lists, counts, recv, a, b, ih, il, mask)
        sums = lax.all_to_all(sums, plane, 0, 0, tiled=True)
        more = (sds((NZ, 8, 128)),) if turn == 0 else ()
        current, residual, *zsend = pl.pallas_call(
            functools.partial(update_kernel, scale),
            out_shape=(sds((8, 128)), sds((8, 128))) + more,
            in_specs=[SM, SM, VM, VM, VM],
            out_specs=(VM, VM) + (VM,) * len(more),
            name="update",
        )(valid_count, step_sizes, sums, boundary_data, current)
        if turn == 0:
            recv = lax.all_to_all(zsend[0], "z", 0, 0, tiled=True)
    return (current, residual)


def solution(mesh):
    grid = Mesh(mesh.devices.reshape(NY, NZ, NX, NC), ("y", "z", "x", "core"))
    split = P(None, ("y", "z", "x", "core"))
    in_specs = (P(), split, split, split, split, P(), P(("y", "z", "x", "core")), P())
    return jax.shard_map(body, mesh=grid, in_specs=in_specs, out_specs=(split, split), check_vma=False)
```

time: 409 us -> 122 us (0.30)
  blocking collectives: 279 us -> 64.7 us
  matrix products: 60.2 us -> 0 us
  Pallas kernels: 0 us -> 31.3 us
  starting transfers between devices: 38.4 us -> 12.5 us
  local copies, waits for them, and re-layouts: 13.7 us -> 0.65 us
  other arithmetic: 7.24 us -> 0.6 us
  waiting for transfers between devices: 5.93 us -> 11.5 us
    all_gather x5 -> x0, blocking collectives: 279 us -> none  [the longest x2 237 us: body(): lax.all_gather(proxy_charges, ('cluster', 'member'), axis=1, tiled=True)]
    all_to_all x0 -> x4, blocking collectives: none -> 64.7 us  [the longest x2 29.3 us: body(): sums = lax.all_to_all(sums, plane, 0, 0, tiled=True)]
    dot_general x60 -> x0, matrix products: 60.2 us -> none  [the longest x58 60 us: advance(): jnp.dot(wts, kernel, precision=lax.Precision.HIGHEST, preferred_element_t...]
    pallas_call x0 -> x6, Pallas kernels: none -> 31.3 us  [the longest x2 22.3 us: body(): pl.pallas_call(field_kernel, out_shape=sds((PLANE, 8, 128)), in_specs=[SM...]
    all_to_all x3 -> x1, starting transfers between devices: 38.4 us -> 12.5 us  [body(): recv = lax.all_to_all(zsend, 'z', 0, 0, tiled=True)]
    slice x58 -> x0, local copies, waits for them, and re-layouts: 5.63 us -> none  [advance(): distance = (pts[0][:, None] - targets[0][None, :]) ** 2]
    all_to_all x3 -> x1, waiting for transfers between devices: 5.93 us -> 11.5 us  [body(): recv = lax.all_to_all(zsend, 'z', 0, 0, tiled=True)]
  transfers between devices with their start and end apart: 3 -> 1, of which waited for: 1 -> 1; matrix products, arithmetic and copies ran while one was open for 7% -> 0% of each run, Pallas kernels for 0% -> 0%
where the time goes in v1:
time: 122 us
  blocking collectives  64.7 us (53%)
  Pallas kernels  31.3 us (26%)
  starting transfers between devices  12.5 us (10%)
  waiting for transfers between devices  11.5 us (9%)
  between operations  1.31 us (1%)
    all_to_all x2, blocking collectives, body(): sums = lax.all_to_all(sums, plane, 0, 0, tiled=True)  29.3 us
    pallas_call x2, Pallas kernels, body(): pl.pallas_call(field_kernel, out_shape=sds((PLANE, 8, 128)), in_specs=[SM...  22.3 us
    all_to_all x1, blocking collectives, body(): targets = lax.all_to_all(tsend, plane, 0, 0, tiled=True)  18.7 us
    all_to_all x1, blocking collectives, body(): recv = lax.all_to_all(zsend[0], 'z', 0, 0, tiled=True)  16.7 us
    all_to_all x1, starting transfers between devices, body(): recv = lax.all_to_all(zsend, 'z', 0, 0, tiled=True)  12.5 us
    all_to_all x1, waiting for transfers between devices, body(): recv = lax.all_to_all(zsend, 'z', 0, 0, tiled=True)  11.5 us
    pallas_call x1, Pallas kernels, body(): pl.pallas_call(setup_kernel, out_shape=(sds((A_BLOCKS * 128, 128), bf16),...  4.21 us
    pallas_call x2, Pallas kernels, body(): pl.pallas_call(functools.partial(update_kernel, scale), out_shape=(sds((8...  3.13 us
  transfers between devices with their start and end apart: 1, of which 1 were waited for; matrix products, arithmetic and copies ran while one was open for 0% of the time, Pallas kernels for 0%

profile of v1, /device:TPU:1, one launch (start us, length us, event | category | flops | bytes accessed | tf_op | source)
XLA Modules:
  0.0 122.5 jit_solution(5997557987827118131)
XLA Ops:
  1.3 1.6 %prologue.1 = (f32[16,16,128]{2,1,0:T(8,128)}, f32[32,8,128]{2,1,0:T(8,128)}, f32[8,128]{1,0:T(8,128)}) custom-call(s32[1]{0:T(128)} %bitcast.3.leaf_ref, s32[1]{0:T(128)S(6)} %copy.10.count_ref, f32[3,512]{1,0:T(4,128)} %centers_ref.3, f32[8,128]{1,0:T(8,128)} %charges_ref.1, f32[3,128]{1,0:T(4,128)} %coords_ref.1, f32[3,128]{1,0:T(4,128)} %targets_ref.1), custom_call_target="tpu_custom_call" | custom-call | tf_op jit(solution)/shard_map/prologue/pallas_call | solution.py:250
  2.9 18.7 %all_to_all.25.tgt_ref = f32[32,8,128]{2,1,0:T(8,128)} all-to-all(f32[32,8,128]{2,1,0:T(8,128)} %get-tuple-element.15), channel_id=1, replica_groups=mesh['y'=4,'z'=16,'x'=4,'core'=2] {'y','x','core'}, dimensions={0} | all-to-all | bytes 262144 | tf_op jit(solution)/shard_map/all_to_all | solution.py:257
  21.7 12.5 %all-to-all-start = ((f32[16,16,128]{2,1,0:T(8,128)}), f32[16,16,128]{2,1,0:T(8,128)S(1)}, u32[]{:S(2)}, u32[]{:S(2)}) async-start(f32[16,16,128]{2,1,0:T(8,128)} %get-tuple-element.14), calls=%async_computation | async-start | bytes 262144 | tf_op jit(solution)/shard_map/all_to_all | solution.py:258
  34.1 0.6 pad_add_fusion.pos_ref
  34.7 11.5 %all-to-all-done.recv_ref = f32[16,16,128]{2,1,0:T(8,128)S(1)} async-done(((f32[16,16,128]{2,1,0:T(8,128)}), f32[16,16,128]{2,1,0:T(8,128)S(1)}, u32[]{:S(2)}, u32[]{:S(2)}) %all-to-all-start) | async-done | bytes 131104 | tf_op jit(solution)/shard_map/all_to_all | solution.py:258
  46.2 0.0 copy-start
  46.2 0.6 copy-done
  46.9 4.2 %setup.1 = (bf16[2688,128]{1,0:T(8,128)(2,1)}, bf16[4,48,1024]{2,1,0:T(8,128)(2,1)}, bf16[512,128]{1,0:T(8,128)(2,1)}, bf16[512,128]{1,0:T(8,128)(2,1)}, s32[4,3...) custom-call(s32[4]{0:T(128)} %pad_add_fusion.pos_ref, f32[3,512]{1,0:T(4,128)} %centers_ref.3, s32[26,64]{1,0:T(8,128)} %bitcast.5, ...), custom_call_target="tpu_custom_call" | custom-call | tf_op jit(solution)/shard_map/setup/pallas_call | solution.py:259
  51.1 11.2 %field.2 = f32[32,8,128]{2,1,0:T(8,128)} custom-call(s32[4,32]{1,0:T(4,128)} %get-tuple-element.16.list_ref, s32[4]{0:T(128)} %get-tuple-element.17.cnt_ref, f32[16,16,128]{2,1,0:T(8,128)} %copy-done, bf16[2688,128]{1,0:T(8,128)(2,1)} %get-tuple-element.18.a_ref, bf16[4,48,1024]{2,1,0:T(8,128)(2,1)} %get-tuple-element.19.b_ref, ...), custom_call_target="tpu_custom_call" | custom-call | tf_op jit(solution)/shard_map/field/pallas_call | solution.py:278
  62.3 15.2 %all_to_all.26.recv_ref = f32[32,8,128]{2,1,0:T(8,128)} all-to-all(f32[32,8,128]{2,1,0:T(8,128)} %field.2), channel_id=1, replica_groups=mesh['y'=4,'z'=16,'x'=4,'core'=2] {'y','x','core'}, dimensions={0} | all-to-all | bytes 262144 | tf_op jit(solution)/shard_map/all_to_all | solution.py:287
  77.4 1.6 %update.2 = (f32[8,128]{1,0:T(8,128)}, f32[8,128]{1,0:T(8,128)}, f32[16,8,128]{2,1,0:T(8,128)}) custom-call(s32[1]{0:T(128)S(6)} %copy.10.count_ref, f32[8]{0:T(128)} %steps_ref.3, f32[32,8,128]{2,1,0:T(8,128)} %all_to_all.26.recv_ref, f32[8,128]{1,0:T(8,128)} %boundary_ref.3, f32[8,128]{1,0:T(8,128)} %get-tuple-element.23.current_ref), custom_call_target="tpu_custom_call" | custom-call | tf_op jit(solution)/shard_map/update/pallas_call | solution.py:289
  79.0 16.7 %all_to_all.27.recv_ref = f32[16,8,128]{2,1,0:T(8,128)} all-to-all(f32[16,8,128]{2,1,0:T(8,128)} %get-tuple-element.24), channel_id=1, replica_groups=mesh['y'=4,'z'=16,'x'=4,'core'=2] {'z'}, dimensions={0} | all-to-all | bytes 131072 | tf_op jit(solution)/shard_map/all_to_all | solution.py:297
  95.7 11.2 %field.3 = f32[32,8,128]{2,1,0:T(8,128)} custom-call(s32[4,32]{1,0:T(4,128)} %get-tuple-element.16.list_ref, s32[4]{0:T(128)} %get-tuple-element.17.cnt_ref, f32[16,8,128]{2,1,0:T(8,128)} %all_to_all.27.recv_ref, bf16[2688,128]{1,0:T(8,128)(2,1)} %get-tuple-element.18.a_ref, bf16[4,48,1024]{2,1,0:T(8,128)(2,1)} %get-tuple-element.19.b_ref, ...), custom_call_target="tpu_custom_call" | custom-call | tf_op jit(solution)/shard_map/field/pallas_call | solution.py:278
  106.8 14.1 %all_to_all.28.recv_ref = f32[32,8,128]{2,1,0:T(8,128)} all-to-all(f32[32,8,128]{2,1,0:T(8,128)} %field.3), channel_id=1, replica_groups=mesh['y'=4,'z'=16,'x'=4,'core'=2] {'y','x','core'}, dimensions={0} | all-to-all | bytes 262144 | tf_op jit(solution)/shard_map/all_to_all | solution.py:287
  120.9 1.6 %update.3 = (f32[8,128]{1,0:T(8,128)}, f32[8,128]{1,0:T(8,128)}) custom-call(s32[1]{0:T(128)S(6)} %copy.10.count_ref, f32[8]{0:T(128)} %steps_ref.3, f32[32,8,128]{2,1,0:T(8,128)} %all_to_all.28.recv_ref, f32[8,128]{1,0:T(8,128)} %boundary_ref.3, f32[8,128]{1,0:T(8,128)} %get-tuple-element.25.current_ref), custom_call_target="tpu_custom_call" | custom-call | tf_op jit(solution)/shard_map/update/pallas_call | solution.py:289
Async XLA Ops:
  21.7 24.6 %all-to-all-start = ((f32[16,16,128]{2,1,0:T(8,128)}), f32[16,16,128]{2,1,0:T(8,128)S(1)}, u32[]{:S(2)}, u32[]{:S(2)}) async-start(f32[16,16,128]{2,1,0:T(8,128)} %get-tuple-element.14), calls=%async_computation | async-start | bytes 262144 | tf_op jit(solution)/shard_map/all_to_all | solution.py:258
  46.2 0.7 copy-start

commit v2 on v1

v2 whole, which is shorter than its diff:
```python
import functools
import math

import jax
import jax.numpy as jnp
import numpy as np
from jax import lax
from jax.experimental import pallas as pl
from jax.experimental.pallas import tpu as pltpu
from jax.sharding import Mesh
from jax.sharding import PartitionSpec as P

HALF_SIDE = 0.08
SOFTENING = 0.0025
NY, NZ, NX, NC = 4, 16, 4, 2
MEMBERS = NX * NC
PLANE = NY * MEMBERS
NEAR = 26
DEPTH = 48
FAR = NZ
ZERO_BLOCK = FAR + 4 * NY
FAR_SLOTS = 32
CHUNK_OWNER = 80
CHUNK_SLOTS = 128
PAIRS = 17
bf16, f32 = jnp.bfloat16, jnp.float32


def cheby_nodes(number):
    return np.cos(np.pi * (2 * np.arange(number) + 1) / (2 * number))


def pick(index, values):
    out = jnp.full(index.shape, float(values[0]), f32)
    for k in range(1, len(values)):
        out = jnp.where(index == k, float(values[k]), out)
    return out


def iota(shape, dim):
    return lax.broadcasted_iota(jnp.int32, shape, dim)


def split3(v):
    h = v.astype(bf16).astype(f32)
    r = v - h
    m = r.astype(bf16).astype(f32)
    low = (r - m).astype(bf16).astype(f32)
    return h, m, low


def split2(v):
    h = v.astype(bf16)
    return h, (v - h.astype(f32)).astype(bf16)


def source_rows(pts, extra):
    row = iota(pts.shape, 0)
    s = jnp.where(row < 3, pts - 0.5, 0.0)
    norm = jnp.sum(s * s, axis=0, keepdims=True) + SOFTENING
    return jnp.where(row < 3, -2.0 * s, jnp.where(row == 3, norm, jnp.where(row == 4, 1.0, extra)))


def target_rows(pts):
    row = iota(pts.shape, 0)
    t = jnp.where(row < 3, pts - 0.5, 0.0)
    norm = jnp.sum(t * t, axis=0, keepdims=True)
    return jnp.where(row < 3, t, jnp.where(row == 3, 1.0, jnp.where(row == 4, norm, 0.0)))


def column3(a, b, c, shape):
    row = iota(shape, 0)
    return jnp.where(row == 0, a, jnp.where(row == 1, b, jnp.where(row == 2, c, 0.0)))


def here():
    member = lax.axis_index("x") * NC + lax.axis_index("core")
    return lax.axis_index("y"), lax.axis_index("z"), member


def prologue_kernel(count_ref, centers_ref, charges_ref, coords_ref, targets_ref, zsend_ref, tsend_ref, current_ref):
    y, z, member = here()
    leaf = (y * NZ + z) * MEMBERS + member
    shape = (8, 128)
    lane = iota(shape, 1)
    live = (lane < count_ref[0]).astype(f32)
    current = charges_ref[...] * live
    current_ref[...] = current
    u = jnp.concatenate([coords_ref[...], jnp.zeros((5, 128), f32)], 0)
    center = column3(centers_ref[0, leaf], centers_ref[1, leaf], centers_ref[2, leaf], shape)
    pts = center + HALF_SIDE * u
    shifted = jnp.concatenate([jnp.zeros((5, 128), f32), coords_ref[...]], 0)
    rows = source_rows(pts, shifted)
    for k in range(NZ):
        zsend_ref[k, 0:8] = current
        zsend_ref[k, 8:16] = rows
    trows = target_rows(jnp.concatenate([targets_ref[...], jnp.zeros((5, 128), f32)], 0))
    for k in range(PLANE):
        tsend_ref[k] = trows


def a_block(rows):
    rows = jnp.where(iota(rows.shape, 0) < 5, rows, 0.0)
    h, m, low = split3(rows)
    return jnp.concatenate([h, h, m, m, h, low], 0).T.astype(bf16)


def interp_tables():
    p = iota((32, 128), 0)
    parts = (p >> 4, (p >> 2) & 3, p & 3)
    tables = []
    for index, number in zip(parts, (2, 4, 4)):
        nodes = cheby_nodes(number)
        others = [[nodes[i] for i in range(number) if i != k] for k in range(number)]
        roots = [pick(index, [others[k][j] for k in range(number)]) for j in range(number - 1)]
        scale = pick(index, [1.0 / np.prod([nodes[k] - o for o in others[k]]) for k in range(number)])
        tables.append((roots, scale))
    return tables


def lists_kernel(near_ref, far_ref, chunk_ref, count_ref, mine_ref):
    y, z, _ = here()
    total = jnp.int32(0)
    for other in range(NY):
        for k in range(NZ):
            mine_ref[k] = 0
        mine_ref[z] = (y == other).astype(jnp.int32)

        def visit(j, carry):
            cluster = near_ref[j, other * NZ + z]
            slot = jnp.where((cluster >> 4) == y, cluster & 15, NZ)
            mine_ref[slot] = 1
            return carry

        lax.fori_loop(0, NEAR, visit, 0, unroll=True)
        near_count = jnp.int32(0)
        far_count = jnp.int32(0)
        for k in range(NZ):
            mine = mine_ref[k]
            chunk_ref[total + near_count] = k
            far_ref[other, far_count] = k
            near_count = near_count + mine
            far_count = far_count + 1 - mine
        for k in range(3):
            far_ref[other, far_count + k] = NZ
        far_blocks = (far_count + 3) // 4
        start = total + near_count
        for k in range(4):
            chunk_ref[start + k] = FAR + other * 4 + k
        end = start + far_blocks
        chunk_ref[end] = ZERO_BLOCK
        far_ref[other, FAR_SLOTS - 1] = far_blocks
        rounded = ((end + 1) >> 1) << 1

        def owner(k, carry):
            chunk_ref[CHUNK_OWNER + k] = other
            return carry

        lax.fori_loop(total >> 1, rounded >> 1, owner, 0)
        total = rounded
    count_ref[0] = total >> 1


def charge_blocks(recv_ref, ih_ref, il_ref, far_ref, q_ref, wide_ref):
    far = []
    nt = (((1,), (1,)), ((), ()))
    for k in range(NZ):
        hi, lo = split2(recv_ref[k, 0:8])
        q = jnp.concatenate([hi.astype(f32), lo.astype(f32)], 0).astype(bf16)
        q_ref[k] = q
        both = lax.dot_general(q, ih_ref[k * 32 : (k + 1) * 32], nt, preferred_element_type=f32)
        both = both + lax.dot_general(q, il_ref[k * 32 : (k + 1) * 32], nt, preferred_element_type=f32)
        far.append(both[0:8] + both[8:16])
    for k in range(4):
        wide = jnp.concatenate(far[4 * k : 4 * k + 4], 1)
        hi = wide.astype(bf16).astype(f32)
        wide_ref[k] = jnp.concatenate([hi, wide - hi], 0)
    wide_ref[4] = jnp.zeros((16, 128), f32)
    q_ref[ZERO_BLOCK] = jnp.zeros((16, 128), bf16)
    group = iota((16, 128), 1) >> 5
    for other in range(NY):
        for block in range(4):

            @pl.when(block < far_ref[other, FAR_SLOTS - 1])
            def _(other=other, block=block):
                out = jnp.zeros((16, 128), f32)
                for k in range(4):
                    leaf = far_ref[other, block * 4 + k]
                    moved = pltpu.roll(wide_ref[leaf >> 2], ((4 + k - leaf) & 3) * 32, 1)
                    out = jnp.where(group == k, moved, out)
                q_ref[FAR + other * 4 + block] = out.astype(bf16)


def setup_kernel(centers_ref, far_ref, recv_ref, a_ref, ih_ref, il_ref, q_ref, proxy_ref, wide_ref):
    y, _, member = here()
    tables = interp_tables()
    for k in range(NZ):
        rows = recv_ref[k, 8:16]
        a_ref[k * 128 : (k + 1) * 128, :DEPTH] = a_block(rows)
        value = None
        for axis, (roots, scale) in enumerate(tables):
            u = jnp.broadcast_to(rows[5 + axis : 6 + axis], (32, 128))
            line = scale
            for root in roots:
                line = line * (u - root)
            value = line if value is None else value * line
        hi, lo = split2(value)
        ih_ref[k * 32 : (k + 1) * 32] = hi
        il_ref[k * 32 : (k + 1) * 32] = lo
    lane = iota((8, 128), 1)
    p = lane & 31
    row = iota((8, 128), 0)
    offset = jnp.where(
        row == 0,
        pick(p >> 4, cheby_nodes(2)),
        jnp.where(row == 1, pick((p >> 2) & 3, cheby_nodes(4)), jnp.where(row == 2, pick(p & 3, cheby_nodes(4)), 0.0)),
    )
    for block in range(4):
        center = jnp.zeros((8, 128), f32)
        for k in range(4):
            leaf = (y * NZ + block * 4 + k) * MEMBERS + member
            column = column3(centers_ref[0, leaf], centers_ref[1, leaf], centers_ref[2, leaf], (8, 128))
            center = jnp.where((lane >> 5) == k, column, center)
        rows = source_rows(center + HALF_SIDE * offset, 0.0)
        proxy_ref[block * 128 : (block + 1) * 128, :DEPTH] = a_block(rows)
    proxy_ref[512:544, :DEPTH] = proxy_ref[0:32, :DEPTH]
    for other in range(NY):
        for block in range(4):

            @pl.when(block < far_ref[other, FAR_SLOTS - 1])
            def _(other=other, block=block):
                for k in range(4):
                    leaf = far_ref[other, block * 4 + k]
                    base = (FAR + other * 4 + block) * 128 + k * 32
                    a_ref[base : base + 32] = proxy_ref[pl.ds(pl.multiple_of(leaf * 32, 32), 32)]

    charge_blocks(recv_ref, ih_ref, il_ref, far_ref, q_ref, wide_ref)


def charges_of(chunk_ref, q_ref, i):
    return jnp.concatenate([q_ref[chunk_ref[2 * i + k]] for k in range(2)], 1)


def multiply(chunk_ref, q_ref, acc_ref, i, hi_ref, lo_ref, j):
    q = charges_of(chunk_ref, q_ref, i)
    rows = pl.ds(pl.multiple_of(chunk_ref[CHUNK_OWNER + i] * 16, 16), 16)
    part = jnp.dot(q, hi_ref[j], preferred_element_type=f32) + jnp.dot(q, lo_ref[j], preferred_element_type=f32)
    acc_ref[rows] = acc_ref[rows] + part


def write_sums(acc_ref, out_ref):
    for other in range(NY):
        total = acc_ref[other * 16 : other * 16 + 8] + acc_ref[other * 16 + 8 : other * 16 + 16]
        for k in range(MEMBERS):
            out_ref[other * MEMBERS + k] = total[:, k * 128 : (k + 1) * 128]


def first_kernel(chunk_ref, count_ref, tgt_ref, a_ref, q_ref, out_ref, eh_ref, el_ref, oh_ref, ol_ref, b_ref, acc_ref):
    for other in range(NY):
        rows = jnp.concatenate([tgt_ref[other * MEMBERS + k] for k in range(MEMBERS)], 1)
        h, m, low = split3(rows)
        b_ref[other] = jnp.concatenate([h, m, h, m, low, h], 0).astype(bf16)
    acc_ref[...] = jnp.zeros_like(acc_ref)
    count = count_ref[0]

    def evaluate(i, hi_ref, lo_ref, j):
        blocks = [chunk_ref[2 * i + k] for k in range(2)]
        starts = [pl.multiple_of(jnp.where(n == ZERO_BLOCK, 0, n) * 128, 128) for n in blocks]
        a = jnp.concatenate([a_ref[pl.ds(n, 128), :DEPTH] for n in starts], 0)
        square = jnp.dot(a, b_ref[chunk_ref[CHUNK_OWNER + i]], preferred_element_type=f32)
        hi, lo = split2(lax.rsqrt(square))
        hi_ref[j] = hi
        lo_ref[j] = lo

    even, odd = (eh_ref, el_ref), (oh_ref, ol_ref)
    mul = functools.partial(multiply, chunk_ref, q_ref, acc_ref)
    evaluate(0, *even, 0)

    def pair(j, carry):
        evaluate(2 * j + 1, *odd, j)
        mul(2 * j, *even, j)
        evaluate(2 * j + 2, *even, j + 1)
        mul(2 * j + 1, *odd, j)
        return carry

    pairs = (count - 1) >> 1
    lax.fori_loop(0, pairs, pair, 0)

    @pl.when((count & 1) == 0)
    def _():
        evaluate(2 * pairs + 1, *odd, pairs)
        mul(2 * pairs, *even, pairs)
        mul(2 * pairs + 1, *odd, pairs)

    @pl.when((count & 1) == 1)
    def _():
        mul(2 * pairs, *even, pairs)

    write_sums(acc_ref, out_ref)


def second_kernel(chunk_ref, count_ref, far_ref, recv_ref, ih_ref, il_ref, eh_ref, el_ref, oh_ref, ol_ref, out_ref, q_ref, wide_ref, acc_ref):
    charge_blocks(recv_ref, ih_ref, il_ref, far_ref, q_ref, wide_ref)
    acc_ref[...] = jnp.zeros_like(acc_ref)
    count = count_ref[0]
    mul = functools.partial(multiply, chunk_ref, q_ref, acc_ref)

    def pair(j, carry):
        mul(2 * j, eh_ref, el_ref, j)
        mul(2 * j + 1, oh_ref, ol_ref, j)
        return carry

    lax.fori_loop(0, count >> 1, pair, 0)

    @pl.when((count & 1) == 1)
    def _():
        mul(count - 1, eh_ref, el_ref, count >> 1)

    write_sums(acc_ref, out_ref)


def update_kernel(scale, count_ref, steps_ref, recv_ref, boundary_ref, current_ref, new_ref, residual_ref, *zsend):
    parts = [recv_ref[k] for k in range(PLANE)]
    while len(parts) > 1:
        parts = [parts[i] + parts[i + 1] for i in range(0, len(parts), 2)]
    shape = (8, 128)
    live = (iota(shape, 1) < count_ref[0]).astype(f32)
    row = iota(shape, 0)
    steps = jnp.zeros(shape, f32)
    for k in range(8):
        steps = jnp.where(row == k, steps_ref[k], steps)
    residual = live * (boundary_ref[...] - scale * parts[0])
    new = live * (current_ref[...] + steps * residual / (1.0 + jnp.abs(residual)))
    new_ref[...] = new
    residual_ref[...] = residual
    for ref in zsend:
        for k in range(NZ):
            ref[k] = new


VM = pl.BlockSpec(memory_space=pltpu.VMEM)
SM = pl.BlockSpec(memory_space=pltpu.SMEM)


def sds(shape, dtype=f32):
    return jax.ShapeDtypeStruct(shape, dtype)


def body(leaf_centers, source_coords, target_points, charges, boundary_data, step_sizes, valid_count, near_lists):
    plane = ("y", "x", "core")
    params = pltpu.CompilerParams(vmem_limit_bytes=12 * 2**20)
    small = pltpu.CompilerParams(vmem_limit_bytes=4 * 2**20)
    zsend, tsend, current = pl.pallas_call(
        prologue_kernel,
        out_shape=(sds((NZ, 16, 128)), sds((PLANE, 8, 128)), sds((8, 128))),
        in_specs=[SM, SM, VM, VM, VM],
        out_specs=(VM, VM, VM),
        compiler_params=small,
        name="prologue",
    )(valid_count, leaf_centers, charges, source_coords, target_points)
    recv = lax.all_to_all(zsend, "z", 0, 0, tiled=True)
    recv, tsend, near_lists = lax.optimization_barrier((recv, tsend, near_lists))
    targets = lax.all_to_all(tsend, plane, 0, 0, tiled=True)
    far, chunks, count = pl.pallas_call(
        lists_kernel,
        out_shape=(sds((NY, FAR_SLOTS), jnp.int32), sds((CHUNK_SLOTS,), jnp.int32), sds((1,), jnp.int32)),
        in_specs=[SM],
        out_specs=(SM, SM, SM),
        scratch_shapes=[pltpu.SMEM((NZ + 1,), jnp.int32)],
        compiler_params=small,
        cost_estimate=pl.CostEstimate(flops=10**9, bytes_accessed=4 * 10**6, transcendentals=0),
        name="lists",
    )(near_lists.T)
    a, ih, il, q = pl.pallas_call(
        setup_kernel,
        out_shape=(
            sds((ZERO_BLOCK * 128, 128), bf16),
            sds((NZ * 32, 128), bf16),
            sds((NZ * 32, 128), bf16),
            sds((ZERO_BLOCK + 1, 16, 128), bf16),
        ),
        in_specs=[SM, SM, VM],
        out_specs=(VM, VM, VM, VM),
        scratch_shapes=[pltpu.VMEM((544, 128), bf16), pltpu.VMEM((5, 16, 128), f32)],
        compiler_params=params,
        cost_estimate=pl.CostEstimate(flops=10**9, bytes_accessed=8 * 10**6, transcendentals=0),
        name="setup",
    )(leaf_centers, far, recv)
    scale = 1.0 / math.sqrt(NY * NZ * MEMBERS * 128)
    half = pltpu.VMEM((PAIRS, 256, MEMBERS * 128), bf16)
    sums, *kernels = pl.pallas_call(
        first_kernel,
        out_shape=(sds((PLANE, 8, 128)), half, half, half, half),
        in_specs=[SM, SM, VM, VM, VM],
        out_specs=(VM,) * 5,
        scratch_shapes=[pltpu.VMEM((NY, DEPTH, MEMBERS * 128), bf16), pltpu.VMEM((NY * 16, MEMBERS * 128), f32)],
        compiler_params=params,
        name="first",
    )(chunks, count, targets, a, q)

    def update(sums, more):
        return pl.pallas_call(
            functools.partial(update_kernel, scale),
            out_shape=(sds((8, 128)), sds((8, 128))) + more,
            in_specs=[SM, SM, VM, VM, VM],
            out_specs=(VM, VM) + (VM,) * len(more),
            compiler_params=small,
            name="update",
        )(valid_count, step_sizes, lax.all_to_all(sums, plane, 0, 0, tiled=True), boundary_data, current)

    current, residual, zsend = update(sums, (sds((NZ, 8, 128)),))
    recv = lax.all_to_all(zsend, "z", 0, 0, tiled=True)
    sums = pl.pallas_call(
        second_kernel,
        out_shape=sds((PLANE, 8, 128)),
        in_specs=[SM, SM, SM] + [VM] * 7,
        out_specs=VM,
        scratch_shapes=[
            pltpu.VMEM((ZERO_BLOCK + 1, 16, 128), bf16),
            pltpu.VMEM((5, 16, 128), f32),
            pltpu.VMEM((NY * 16, MEMBERS * 128), f32),
        ],
        compiler_params=params,
        name="second",
    )(chunks, count, far, recv, ih, il, *kernels)
    current, residual = update(sums, ())
    return (current, residual)


def solution(mesh):
    grid = Mesh(mesh.devices.reshape(NY, NZ, NX, NC), ("y", "z", "x", "core"))
    split = P(None, ("y", "z", "x", "core"))
    in_specs = (P(), split, split, split, split, P(), P(("y", "z", "x", "core")), P())
    return jax.shard_map(body, mesh=grid, in_specs=in_specs, out_specs=(split, split), check_vma=False)
```

time: 122 us -> 111 us (0.910); the launches traced: 122 us -> 110 us
  waiting for transfers between devices: 11.5 us -> 1.51 us
  Pallas kernels: 31.3 us -> 23.2 us
  blocking collectives: 64.7 us -> 68.6 us
  local copies, waits for them, and re-layouts: 0.65 us -> 4.15 us
  starting transfers between devices: 12.5 us -> 10.8 us
    all_to_all x1, waiting for transfers between devices: 11.5 us -> 1.51 us  [body(): targets = lax.all_to_all(tsend, plane, 0, 0, tiled=True)]
    pallas_call x5 -> x6, Pallas kernels: 29.6 us -> 21.9 us  [the longest x1 8.51 us: body(): pl.pallas_call(first_kernel, out_shape=(sds((PLANE, 8, 128)), half, half,...]
    all_to_all x4, blocking collectives: 64.7 us -> 68.6 us  [the longest x2 42.7 us: body(): recv = lax.all_to_all(zsend, 'z', 0, 0, tiled=True)]
    unnamed x2 -> x16, local copies, waits for them, and re-layouts: 0.65 us -> 4.15 us
    all_to_all x1, starting transfers between devices: 12.5 us -> 10.8 us  [body(): targets = lax.all_to_all(tsend, plane, 0, 0, tiled=True)]
  transfers between devices with their start and end apart: 1 -> 1, of which waited for: 1 -> 1; matrix products, arithmetic and copies ran while one was open for 0% -> 0% of each run, Pallas kernels for 0% -> 4%
where the time goes in v2:
time: 111 us; the launch traced here: 110 us
  blocking collectives  68.6 us (62%)
  Pallas kernels  23.2 us (21%)
  starting transfers between devices  10.8 us (10%)
  local copies, waits for them, and re-layouts  4.15 us (4%)
  waiting for transfers between devices  1.51 us (1%)
  between operations  1.36 us (1%)
    all_to_all x2, blocking collectives, body(): recv = lax.all_to_all(zsend, 'z', 0, 0, tiled=True)  42.7 us
    all_to_all x2, blocking collectives, update(): lax.all_to_all(sums, plane, 0, 0, tiled=True)  25.9 us
    all_to_all x1, starting transfers between devices, body(): targets = lax.all_to_all(tsend, plane, 0, 0, tiled=True)  10.8 us
    pallas_call x1, Pallas kernels, body(): pl.pallas_call(first_kernel, out_shape=(sds((PLANE, 8, 128)), half, half,...  8.51 us
    pallas_call x1, Pallas kernels, body(): pl.pallas_call(second_kernel, out_shape=sds((PLANE, 8, 128)), in_specs=[S...  6.4 us
    unnamed x16, local copies, waits for them, and re-layouts  4.15 us
    pallas_call x1, Pallas kernels, body(): pl.pallas_call(setup_kernel, out_shape=(sds((ZERO_BLOCK * 128, 128), bf16...  2.52 us
    pallas_call x2, Pallas kernels, update(): pl.pallas_call(functools.partial(update_kernel, scale), out_shape=(sds((8...  2.31 us
  transfers between devices with their start and end apart: 1, of which 1 were waited for; matrix products, arithmetic and copies ran while one was open for 0% of the time, Pallas kernels for 4%

profile of v2, /device:TPU:1, one launch (start us, length us, event | category | flops | bytes accessed | tf_op | source)
XLA Modules:
  0.0 109.7 jit_solution(11808195883167536571)
XLA Ops:
  0.6 0.0 copy-start
  1.3 0.0 copy-start.1
  1.3 0.7 copy-done.1
  2.0 0.0 copy-start.3
  2.0 0.7 copy-done.3
  2.7 0.0 copy-start.5
  2.7 0.7 copy-done.5
  3.4 0.0 copy-start.6
  3.4 0.7 copy-done.6
  4.1 0.0 copy-start.4
  4.1 1.3 %prologue.1 = (f32[16,16,128]{2,1,0:T(8,128)S(1)}, f32[32,8,128]{2,1,0:T(8,128)}, f32[8,128]{1,0:T(8,128)S(1)}) custom-call(s32[1]{0:T(128)S(6)} %copy.10.count_ref, f32[3,512]{1,0:T(4,128)S(1)} %copy-done.1, f32[8,128]{1,0:T(8,128)S(1)} %copy-done.3, f32[3,128]{1,0:T(4,128)S(1)} %copy-done.5, f32[3,128]{1,0:T(4,128)S(1)} %copy-done.6), custom_call_target="tpu_custom_call" | custom-call | tf_op jit(solution)/shard_map/prologue/pallas_call | solution.py:353
  5.4 27.5 %all_to_all.25.recv_ref = f32[16,16,128]{2,1,0:T(8,128)S(1)} all-to-all(f32[16,16,128]{2,1,0:T(8,128)S(1)} %get-tuple-element.22), channel_id=1, replica_groups=mesh['y'=4,'z'=16,'x'=4,'core'=2] {'z'}, dimensions={0} | all-to-all | bytes 262144 | tf_op jit(solution)/shard_map/all_to_all | solution.py:361
  32.9 10.8 %all-to-all-start.1 = ((f32[32,8,128]{2,1,0:T(8,128)}), f32[32,8,128]{2,1,0:T(8,128)S(1)}, u32[]{:S(2)}, u32[]{:S(2)}) async-start(f32[32,8,128]{2,1,0:T(8,128)} %get-tuple-element.28), calls=%async_computation.1 | async-start | bytes 262144 | tf_op jit(solution)/shard_map/all_to_all | solution.py:363
  43.7 0.0 copy-start.7
  43.8 0.7 copy-done.7
  44.5 2.1 %lists.1 = (s32[4,32]{1,0:T(4,128)S(1)}, s32[128]{0:T(128)S(1)}, s32[1]{0:T(128)}) custom-call(s32[26,64]{1,0:T(8,128)S(1)} %bitcast.1), custom_call_target="tpu_custom_call" | custom-call | flops 1000000000 | bytes 4000000 | tf_op jit(solution)/shard_map/lists/pallas_call | solution.py:364
  46.6 0.0 copy-start.2
  46.6 0.7 copy-done.2
  47.3 2.5 %setup.1 = (bf16[4096,128]{1,0:T(8,128)(2,1)S(1)}, bf16[512,128]{1,0:T(8,128)(2,1)S(1)}, bf16[512,128]{1,0:T(8,128)(2,1)S(1)}, bf16[33,16,128]{2,1,0:T(8,128)(2,1)S(1)}) custom-call(f32[3,512]{1,0:T(4,128)S(1)} %copy-done.2, s32[4,32]{1,0:T(4,128)S(1)} %get-tuple-element.27.far_ref, f32[16,16,128]{2,1,0:T(8,128)S(1)} %all_to_all.25.recv_ref), custom_call_target="tpu_custom_call" | custom-call | flops 1000000000 | bytes 8000000 | tf_op jit(solution)/shard_map/setup/pallas_call | solution.py:374
  49.8 1.5 %all-to-all-done.1.tgt_ref = f32[32,8,128]{2,1,0:T(8,128)S(1)} async-done(((f32[32,8,128]{2,1,0:T(8,128)}), f32[32,8,128]{2,1,0:T(8,128)S(1)}, u32[]{:S(2)}, u32[]{:S(2)}) %all-to-all-start.1) | async-done | bytes 131104 | tf_op jit(solution)/shard_map/all_to_all | solution.py:363
  51.3 8.5 %first.1 = (f32[32,8,128]{2,1,0:T(8,128)S(1)}, bf16[17,256,1024]{2,1,0:T(8,128)(2,1)S(1)}, bf16[17,256,1024]{2,1,0:T(8,128)(2,1)S(1)}, bf16[17,256,1024]{2,1,0:T(8,128)(2,1)S(1)}, bf16[17,256,1024]{2,1,0:T(8,128)(2,1)S(1)}) custom-call(s32[128]{0:T(128)S(1)} %get-tuple-element.25.chunk_ref, s32[1]{0:T(128)} %get-tuple-element.26.count_ref, ...), custom_call_target="tpu_custom_call" | custom-call | tf_op jit(solution)/shard_map/first/pallas_call | solution.py:391
  59.9 13.2 %all_to_all.26.recv_ref = f32[32,8,128]{2,1,0:T(8,128)S(1)} all-to-all(f32[32,8,128]{2,1,0:T(8,128)S(1)} %get-tuple-element.32), channel_id=1, replica_groups=mesh['y'=4,'z'=16,'x'=4,'core'=2] {'y','x','core'}, dimensions={0} | all-to-all | bytes 262144 | tf_op jit(solution)/shard_map/all_to_all | solution.py:409
  73.1 0.0 copy-done
  73.1 0.0 copy-done.4
  73.1 1.1 %update.2 = (f32[8,128]{1,0:T(8,128)S(1)}, f32[8,128]{1,0:T(8,128)}, f32[16,8,128]{2,1,0:T(8,128)S(1)}) custom-call(s32[1]{0:T(128)S(6)} %copy.10.count_ref, f32[8]{0:T(128)S(1)} %copy-done.4, f32[32,8,128]{2,1,0:T(8,128)S(1)} %all_to_all.26.recv_ref, f32[8,128]{1,0:T(8,128)S(1)} %copy-done, f32[8,128]{1,0:T(8,128)S(1)} %get-tuple-element.33.current_ref), custom_call_target="tpu_custom_call" | custom-call | tf_op jit(solution)/shard_map/update/pallas_call | solution.py:402
  74.2 15.2 %all_to_all.27.recv_ref = f32[16,8,128]{2,1,0:T(8,128)S(1)} all-to-all(f32[16,8,128]{2,1,0:T(8,128)S(1)} %get-tuple-element.34), channel_id=1, replica_groups=mesh['y'=4,'z'=16,'x'=4,'core'=2] {'z'}, dimensions={0} | all-to-all | bytes 131072 | tf_op jit(solution)/shard_map/all_to_all | solution.py:412
  89.5 6.4 %second.1 = f32[32,8,128]{2,1,0:T(8,128)S(1)} custom-call(s32[128]{0:T(128)S(1)} %get-tuple-element.25.chunk_ref, s32[1]{0:T(128)} %get-tuple-element.26.count_ref, s32[4,32]{1,0:T(4,128)S(1)} %get-tuple-element.27.far_ref, f32[16,8,128]{2,1,0:T(8,128)S(1)} %all_to_all.27.recv_ref, bf16[512,128]{1,0:T(8,128)(2,1)S(1)} %get-tuple-element.35.ih_ref, ...), custom_call_target="tpu_custom_call" | custom-call | tf_op jit(solution)/shard_map/second/pallas_call | solution.py:413
  95.9 12.7 %all_to_all.28.recv_ref = f32[32,8,128]{2,1,0:T(8,128)S(1)} all-to-all(f32[32,8,128]{2,1,0:T(8,128)S(1)} %second.1), channel_id=1, replica_groups=mesh['y'=4,'z'=16,'x'=4,'core'=2] {'y','x','core'}, dimensions={0} | all-to-all | bytes 262144 | tf_op jit(solution)/shard_map/all_to_all | solution.py:409
  108.6 1.2 %update.3 = (f32[8,128]{1,0:T(8,128)}, f32[8,128]{1,0:T(8,128)}) custom-call(s32[1]{0:T(128)S(6)} %copy.10.count_ref, f32[8]{0:T(128)S(1)} %copy-done.4, f32[32,8,128]{2,1,0:T(8,128)S(1)} %all_to_all.28.recv_ref, f32[8,128]{1,0:T(8,128)S(1)} %copy-done, f32[8,128]{1,0:T(8,128)S(1)} %get-tuple-element.41.current_ref), custom_call_target="tpu_custom_call" | custom-call | tf_op jit(solution)/shard_map/update/pallas_call | solution.py:402
Async XLA Ops:
  0.6 72.4 %copy-start = (f32[8,128]{1,0:T(8,128)S(1)}, f32[8,128]{1,0:T(8,128)}, u32[]{:S(2)}) copy-start(f32[8,128]{1,0:T(8,128)} %boundary_ref.3) | copy-start | bytes 12292
  1.3 0.7 copy-start.1
  2.0 0.7 copy-start.3
  2.7 0.7 copy-start.5
  3.4 0.7 copy-start.6
  4.1 69.0 %copy-start.4 = (f32[8]{0:T(128)S(1)}, f32[8]{0:T(128)}, u32[]{:S(2)}) copy-start(f32[8]{0:T(128)} %steps_ref.3) | copy-start | bytes 100
  32.9 18.5 %all-to-all-start.1 = ((f32[32,8,128]{2,1,0:T(8,128)}), f32[32,8,128]{2,1,0:T(8,128)S(1)}, u32[]{:S(2)}, u32[]{:S(2)}) async-start(f32[32,8,128]{2,1,0:T(8,128)} %get-tuple-element.28), calls=%async_computation.1 | async-start | bytes 262144 | tf_op jit(solution)/shard_map/all_to_all | solution.py:363
  43.7 0.7 copy-start.7
  46.6 0.7 copy-start.2

commit v3 on v2

--- a/solution.py
+++ b/solution.py
@@ -78,27 +78,6 @@
     return lax.axis_index("y"), lax.axis_index("z"), member
 
 
-def prologue_kernel(count_ref, centers_ref, charges_ref, coords_ref, targets_ref, zsend_ref, tsend_ref, current_ref):
-    y, z, member = here()
-    leaf = (y * NZ + z) * MEMBERS + member
-    shape = (8, 128)
-    lane = iota(shape, 1)
-    live = (lane < count_ref[0]).astype(f32)
-    current = charges_ref[...] * live
-    current_ref[...] = current
-    u = jnp.concatenate([coords_ref[...], jnp.zeros((5, 128), f32)], 0)
-    center = column3(centers_ref[0, leaf], centers_ref[1, leaf], centers_ref[2, leaf], shape)
-    pts = center + HALF_SIDE * u
-    shifted = jnp.concatenate([jnp.zeros((5, 128), f32), coords_ref[...]], 0)
-    rows = source_rows(pts, shifted)
-    for k in range(NZ):
-        zsend_ref[k, 0:8] = current
-        zsend_ref[k, 8:16] = rows
-    trows = target_rows(jnp.concatenate([targets_ref[...], jnp.zeros((5, 128), f32)], 0))
-    for k in range(PLANE):
-        tsend_ref[k] = trows
-
-
 def a_block(rows):
     rows = jnp.where(iota(rows.shape, 0) < 5, rows, 0.0)
     h, m, low = split3(rows)
@@ -118,21 +97,15 @@
     return tables
 
 
-def lists_kernel(near_ref, far_ref, chunk_ref, count_ref, mine_ref):
-    y, z, _ = here()
+def make_lists(y, z, near_ref, far_ref, chunk_ref, count_ref, mine_ref):
     total = jnp.int32(0)
     for other in range(NY):
         for k in range(NZ):
             mine_ref[k] = 0
         mine_ref[z] = (y == other).astype(jnp.int32)
-
-        def visit(j, carry):
+        for j in range(NEAR):
             cluster = near_ref[j, other * NZ + z]
-            slot = jnp.where((cluster >> 4) == y, cluster & 15, NZ)
-            mine_ref[slot] = 1
-            return carry
-
-        lax.fori_loop(0, NEAR, visit, 0, unroll=True)
+            mine_ref[jnp.where((cluster >> 4) == y, cluster & 15, NZ)] = 1
         near_count = jnp.int32(0)
         far_count = jnp.int32(0)
         for k in range(NZ):
@@ -159,6 +132,65 @@
         lax.fori_loop(total >> 1, rounded >> 1, owner, 0)
         total = rounded
     count_ref[0] = total >> 1
+
+
+def prep_kernel(
+    centers_ref, near_ref, count_ref, steps_ref, charges_hbm, coords_hbm, boundary_hbm,
+    zsend_ref, held_ref, far_ref, chunk_ref, chunks_ref, proxy_ref,
+    mine_ref, wide_ref, coords_ref, sem,
+):
+    y, z, member = here()
+    leaf = (y * NZ + z) * MEMBERS + member
+    copies = [
+        pltpu.make_async_copy(source, target, sem.at[k])
+        for k, (source, target) in enumerate(((charges_hbm, held_ref.at[0]), (coords_hbm, coords_ref), (boundary_hbm, held_ref.at[1])))
+    ]
+    for copy in copies:
+        copy.start()
+    make_lists(y, z, near_ref, far_ref, chunk_ref, chunks_ref, mine_ref)
+    for copy in copies:
+        copy.wait()
+    lane = iota((8, 128), 1)
+    row = iota((8, 128), 0)
+    live = (lane < count_ref[0]).astype(f32)
+    current = held_ref[0] * live
+    held_ref[0] = current
+    steps = jnp.zeros((8, 128), f32)
+    for k in range(8):
+        steps = jnp.where(row == k, steps_ref[k], steps)
+    held_ref[2] = steps
+    held_ref[3] = live
+    u = jnp.concatenate([coords_ref[...], jnp.zeros((5, 128), f32)], 0)
+    center = column3(centers_ref[0, leaf], centers_ref[1, leaf], centers_ref[2, leaf], (8, 128))
+    shifted = jnp.concatenate([jnp.zeros((5, 128), f32), coords_ref[...]], 0)
+    rows = source_rows(center + HALF_SIDE * u, shifted)
+    for k in range(NZ):
+        zsend_ref[k, 0:8] = current
+        zsend_ref[k, 8:16] = rows
+    p = lane & 31
+    offset = jnp.where(
+        row == 0,
+        pick(p >> 4, cheby_nodes(2)),
+        jnp.where(row == 1, pick((p >> 2) & 3, cheby_nodes(4)), jnp.where(row == 2, pick(p & 3, cheby_nodes(4)), 0.0)),
+    )
+    for block in range(4):
+        center = jnp.zeros((8, 128), f32)
+        for k in range(4):
+            leaf = (y * NZ + block * 4 + k) * MEMBERS + member
+            column = column3(centers_ref[0, leaf], centers_ref[1, leaf], centers_ref[2, leaf], (8, 128))
+            center = jnp.where((lane >> 5) == k, column, center)
+        rows = source_rows(center + HALF_SIDE * offset, 0.0)
+        wide_ref[block * 128 : (block + 1) * 128, :DEPTH] = a_block(rows)
+    wide_ref[512:544, :DEPTH] = wide_ref[0:32, :DEPTH]
+    for other in range(NY):
+        for block in range(4):
+
+            @pl.when(block < far_ref[other, FAR_SLOTS - 1])
+            def _(other=other, block=block):
+                for k in range(4):
+                    leaf = far_ref[other, block * 4 + k]
+                    base = (other * 4 + block) * 128 + k * 32
+                    proxy_ref[base : base + 32] = wide_ref[pl.ds(pl.multiple_of(leaf * 32, 32), 32)]
 
 
 def charge_blocks(recv_ref, ih_ref, il_ref, far_ref, q_ref, wide_ref):
@@ -191,8 +223,7 @@
                 q_ref[FAR + other * 4 + block] = out.astype(bf16)
 
 
-def setup_kernel(centers_ref, far_ref, recv_ref, a_ref, ih_ref, il_ref, q_ref, proxy_ref, wide_ref):
-    y, _, member = here()
+def setup_kernel(far_ref, recv_ref, a_ref, ih_ref, il_ref, q_ref, wide_ref):
     tables = interp_tables()
     for k in range(NZ):
         rows = recv_ref[k, 8:16]
@@ -207,33 +238,6 @@
         hi, lo = split2(value)
         ih_ref[k * 32 : (k + 1) * 32] = hi
         il_ref[k * 32 : (k + 1) * 32] = lo
-    lane = iota((8, 128), 1)
-    p = lane & 31
-    row = iota((8, 128), 0)
-    offset = jnp.where(
-        row == 0,
-        pick(p >> 4, cheby_nodes(2)),
-        jnp.where(row == 1, pick((p >> 2) & 3, cheby_nodes(4)), jnp.where(row == 2, pick(p & 3, cheby_nodes(4)), 0.0)),
-    )
-    for block in range(4):
-        center = jnp.zeros((8, 128), f32)
-        for k in range(4):
-            leaf = (y * NZ + block * 4 + k) * MEMBERS + member
-            column = column3(centers_ref[0, leaf], centers_ref[1, leaf], centers_ref[2, leaf], (8, 128))
-            center = jnp.where((lane >> 5) == k, column, center)
-        rows = source_rows(center + HALF_SIDE * offset, 0.0)
-        proxy_ref[block * 128 : (block + 1) * 128, :DEPTH] = a_block(rows)
-    proxy_ref[512:544, :DEPTH] = proxy_ref[0:32, :DEPTH]
-    for other in range(NY):
-        for block in range(4):
-
-            @pl.when(block < far_ref[other, FAR_SLOTS - 1])
-            def _(other=other, block=block):
-                for k in range(4):
-                    leaf = far_ref[other, block * 4 + k]
-                    base = (FAR + other * 4 + block) * 128 + k * 32
-                    a_ref[base : base + 32] = proxy_ref[pl.ds(pl.multiple_of(leaf * 32, 32), 32)]
-
     charge_blocks(recv_ref, ih_ref, il_ref, far_ref, q_ref, wide_ref)
 
 
@@ -255,10 +259,14 @@
             out_ref[other * MEMBERS + k] = total[:, k * 128 : (k + 1) * 128]
 
 
-def first_kernel(chunk_ref, count_ref, tgt_ref, a_ref, q_ref, out_ref, eh_ref, el_ref, oh_ref, ol_ref, b_ref, acc_ref):
+def first_kernel(
+    chunk_ref, count_ref, far_ref, tgt_ref, recv_ref, proxy_ref, out_ref, ih_ref, il_ref, eh_ref, el_ref, oh_ref, ol_ref, a_ref, q_ref, wide_ref, b_ref, acc_ref
+):
+    setup_kernel(far_ref, recv_ref, a_ref, ih_ref, il_ref, q_ref, wide_ref)
+    a_ref[FAR * 128 :] = proxy_ref[...]
     for other in range(NY):
-        rows = jnp.concatenate([tgt_ref[other * MEMBERS + k] for k in range(MEMBERS)], 1)
-        h, m, low = split3(rows)
+        points = jnp.concatenate([tgt_ref[other * MEMBERS + k] for k in range(MEMBERS)], 1)
+        h, m, low = split3(target_rows(jnp.concatenate([points, jnp.zeros((5, MEMBERS * 128), f32)], 0)))
         b_ref[other] = jnp.concatenate([h, m, h, m, low, h], 0).astype(bf16)
     acc_ref[...] = jnp.zeros_like(acc_ref)
     count = count_ref[0]
@@ -319,27 +327,29 @@
     write_sums(acc_ref, out_ref)
 
 
-def update_kernel(scale, count_ref, steps_ref, recv_ref, boundary_ref, current_ref, new_ref, residual_ref, *zsend):
+def update_kernel(scale, last, recv_ref, held_ref, *refs):
     parts = [recv_ref[k] for k in range(PLANE)]
     while len(parts) > 1:
         parts = [parts[i] + parts[i + 1] for i in range(0, len(parts), 2)]
-    shape = (8, 128)
-    live = (iota(shape, 1) < count_ref[0]).astype(f32)
-    row = iota(shape, 0)
-    steps = jnp.zeros(shape, f32)
-    for k in range(8):
-        steps = jnp.where(row == k, steps_ref[k], steps)
-    residual = live * (boundary_ref[...] - scale * parts[0])
-    new = live * (current_ref[...] + steps * residual / (1.0 + jnp.abs(residual)))
+    live = held_ref[3]
+    residual = live * (held_ref[1] - scale * parts[0])
+    if last:
+        current_ref, new_ref, residual_ref = refs
+        residual_ref[...] = residual
+        current = current_ref[...]
+    else:
+        new_ref, zsend_ref = refs
+        current = held_ref[0]
+    new = live * (current + held_ref[2] * residual / (1.0 + jnp.abs(residual)))
     new_ref[...] = new
-    residual_ref[...] = residual
-    for ref in zsend:
+    if not last:
         for k in range(NZ):
-            ref[k] = new
+            zsend_ref[k] = new
 
 
 VM = pl.BlockSpec(memory_space=pltpu.VMEM)
 SM = pl.BlockSpec(memory_space=pltpu.SMEM)
+HB = pl.BlockSpec(memory_space=pltpu.HBM)
 
 
 def sds(shape, dtype=f32):
@@ -350,65 +360,62 @@
     plane = ("y", "x", "core")
     params = pltpu.CompilerParams(vmem_limit_bytes=12 * 2**20)
     small = pltpu.CompilerParams(vmem_limit_bytes=4 * 2**20)
-    zsend, tsend, current = pl.pallas_call(
-        prologue_kernel,
-        out_shape=(sds((NZ, 16, 128)), sds((PLANE, 8, 128)), sds((8, 128))),
-        in_specs=[SM, SM, VM, VM, VM],
-        out_specs=(VM, VM, VM),
+    targets = lax.all_to_all(jnp.broadcast_to(target_points[None], (PLANE, 3, 128)), plane, 0, 0, tiled=True)
+    zsend, held, far, chunks, count, proxies = pl.pallas_call(
+        prep_kernel,
+        out_shape=(
+            sds((NZ, 16, 128)),
+            sds((4, 8, 128)),
+            sds((NY, FAR_SLOTS), jnp.int32),
+            sds((CHUNK_SLOTS,), jnp.int32),
+            sds((1,), jnp.int32),
+            sds((4 * NY * 128, 128), bf16),
+        ),
+        in_specs=[SM, SM, SM, SM, HB, HB, HB],
+        out_specs=(VM, VM, SM, SM, SM, VM),
+        scratch_shapes=[
+            pltpu.SMEM((NZ + 1,), jnp.int32),
+            pltpu.VMEM((544, 128), bf16),
+            pltpu.VMEM((3, 128), f32),
+            pltpu.SemaphoreType.DMA((3,)),
+        ],
         compiler_params=small,
-        name="prologue",
-    )(valid_count, leaf_centers, charges, source_coords, target_points)
+        cost_estimate=pl.CostEstimate(flops=10**9, bytes_accessed=12 * 10**6, transcendentals=0),
+        name="prep",
+    )(leaf_centers, near_lists.T, valid_count, step_sizes, charges, source_coords, boundary_data)
+    zsend, targets = lax.optimization_barrier((zsend, targets))
     recv = lax.all_to_all(zsend, "z", 0, 0, tiled=True)
-    recv, tsend, near_lists = lax.optimization_barrier((recv, tsend, near_lists))
-    targets = lax.all_to_all(tsend, plane, 0, 0, tiled=True)
-    far, chunks, count = pl.pallas_call(
-        lists_kernel,
-        out_shape=(sds((NY, FAR_SLOTS), jnp.int32), sds((CHUNK_SLOTS,), jnp.int32), sds((1,), jnp.int32)),
-        in_specs=[SM],
-        out_specs=(SM, SM, SM),
-        scratch_shapes=[pltpu.SMEM((NZ + 1,), jnp.int32)],
-        compiler_params=small,
-        cost_estimate=pl.CostEstimate(flops=10**9, bytes_accessed=4 * 10**6, transcendentals=0),
-        name="lists",
-    )(near_lists.T)
-    a, ih, il, q = pl.pallas_call(
-        setup_kernel,
-        out_shape=(
-            sds((ZERO_BLOCK * 128, 128), bf16),
-            sds((NZ * 32, 128), bf16),
-            sds((NZ * 32, 128), bf16),
-            sds((ZERO_BLOCK + 1, 16, 128), bf16),
-        ),
-        in_specs=[SM, SM, VM],
-        out_specs=(VM, VM, VM, VM),
-        scratch_shapes=[pltpu.VMEM((544, 128), bf16), pltpu.VMEM((5, 16, 128), f32)],
-        compiler_params=params,
-        cost_estimate=pl.CostEstimate(flops=10**9, bytes_accessed=8 * 10**6, transcendentals=0),
-        name="setup",
-    )(leaf_centers, far, recv)
     scale = 1.0 / math.sqrt(NY * NZ * MEMBERS * 128)
     half = pltpu.VMEM((PAIRS, 256, MEMBERS * 128), bf16)
-    sums, *kernels = pl.pallas_call(
+    interp = sds((NZ * 32, 128), bf16)
+    sums, ih, il, *kernels = pl.pallas_call(
         first_kernel,
-        out_shape=(sds((PLANE, 8, 128)), half, half, half, half),
-        in_specs=[SM, SM, VM, VM, VM],
-        out_specs=(VM,) * 5,
-        scratch_shapes=[pltpu.VMEM((NY, DEPTH, MEMBERS * 128), bf16), pltpu.VMEM((NY * 16, MEMBERS * 128), f32)],
+        out_shape=(sds((PLANE, 8, 128)), interp, interp, half, half, half, half),
+        in_specs=[SM, SM, SM, VM, VM, VM],
+        out_specs=(VM,) * 7,
+        scratch_shapes=[
+            pltpu.VMEM((ZERO_BLOCK * 128, 128), bf16),
+            pltpu.VMEM((ZERO_BLOCK + 1, 16, 128), bf16),
+            pltpu.VMEM((5, 16, 128), f32),
+            pltpu.VMEM((NY, DEPTH, MEMBERS * 128), bf16),
+            pltpu.VMEM((NY * 16, MEMBERS * 128), f32),
+        ],
         compiler_params=params,
         name="first",
-    )(chunks, count, targets, a, q)
-
-    def update(sums, more):
+    )(chunks, count, far, targets, recv, proxies)
+
+    def update(sums, *current):
+        last = len(current) > 0
         return pl.pallas_call(
-            functools.partial(update_kernel, scale),
-            out_shape=(sds((8, 128)), sds((8, 128))) + more,
-            in_specs=[SM, SM, VM, VM, VM],
-            out_specs=(VM, VM) + (VM,) * len(more),
+            functools.partial(update_kernel, scale, last),
+            out_shape=(sds((8, 128)), sds((8, 128) if last else (NZ, 8, 128))),
+            in_specs=[VM, VM] + [VM] * last,
+            out_specs=(VM, VM),
             compiler_params=small,
             name="update",
-        )(valid_count, step_sizes, lax.all_to_all(sums, plane, 0, 0, tiled=True), boundary_data, current)
-
-    current, residual, zsend = update(sums, (sds((NZ, 8, 128)),))
+        )(lax.all_to_all(sums, plane, 0, 0, tiled=True), held, *current)
+
+    current, zsend = update(sums)
     recv = lax.all_to_all(zsend, "z", 0, 0, tiled=True)
     sums = pl.pallas_call(
         second_kernel,
@@ -423,7 +430,7 @@
         compiler_params=params,
         name="second",
     )(chunks, count, far, recv, ih, il, *kernels)
-    current, residual = update(sums, ())
+    current, residual = update(sums, current)
     return (current, residual)
 
 

time: 111 us -> 109 us (0.982)
  Pallas kernels: 23.2 us -> 18.3 us
  blocking collectives: 68.6 us -> 72.4 us
  waiting for transfers between devices: 1.51 us -> 0.01 us
  local copies, waits for them, and re-layouts: 4.15 us -> 5.43 us
    all_to_all x2, blocking collectives: 25.9 us -> 32 us  [update(): lax.all_to_all(sums, plane, 0, 0, tiled=True)]
    pallas_call x6 -> x4, Pallas kernels: 16.8 us -> 12.4 us  [the longest x1 9.11 us: body(): pl.pallas_call(first_kernel, out_shape=(sds((PLANE, 8, 128)), interp, int...]
    all_to_all x2, blocking collectives: 42.7 us -> 40.4 us  [body(): recv = lax.all_to_all(zsend, 'z', 0, 0, tiled=True)]
    all_to_all x1, waiting for transfers between devices: 1.51 us -> 0.01 us  [body(): lax.all_to_all(jnp.broadcast_to(target_points[None], (PLANE, 3, 128)), pl...]
    broadcast_in_dim x0 -> x1, local copies, waits for them, and re-layouts: none -> 1.32 us  [body(): jnp.broadcast_to(target_points[None], (PLANE, 3, 128))]
    unnamed x16 -> x12, local copies, waits for them, and re-layouts: 4.15 us -> 4.12 us
  transfers between devices with their start and end apart: 1 -> 1, of which waited for: 1 -> 0; matrix products, arithmetic and copies ran while one was open for 0% -> 0% of each run, Pallas kernels for 4% -> 2%
where the time goes in v3:
time: 109 us; the launch traced here: 108 us
  blocking collectives  72.4 us (66%)
  Pallas kernels  18.3 us (17%)
  starting transfers between devices  10.3 us (9%)
  local copies, waits for them, and re-layouts  5.43 us (5%)
  between operations  1.33 us (1%)
    all_to_all x2, blocking collectives, body(): recv = lax.all_to_all(zsend, 'z', 0, 0, tiled=True)  40.4 us
    all_to_all x2, blocking collectives, update(): lax.all_to_all(sums, plane, 0, 0, tiled=True)  32 us
    all_to_all x1, starting transfers between devices, body(): lax.all_to_all(jnp.broadcast_to(target_points[None], (PLANE, 3, 128)), pl...  10.3 us
    pallas_call x1, Pallas kernels, body(): pl.pallas_call(first_kernel, out_shape=(sds((PLANE, 8, 128)), interp, int...  9.11 us
    pallas_call x1, Pallas kernels, body(): pl.pallas_call(second_kernel, out_shape=sds((PLANE, 8, 128)), in_specs=[S...  5.86 us
    unnamed x12, local copies, waits for them, and re-layouts  4.12 us
    pallas_call x1, Pallas kernels, body(): pl.pallas_call(prep_kernel, out_shape=(sds((NZ, 16, 128)), sds((4, 8, 128...  2.68 us
  transfers between devices with their start and end apart: 1, of which 0 were waited for; matrix products, arithmetic and copies ran while one was open for 0% of the time, Pallas kernels for 2%

profile of v3, /device:TPU:1, one launch (start us, length us, event | category | flops | bytes accessed | tf_op | source)
XLA Modules:
  0.0 107.8 jit_solution(9928171060897522292)
XLA Ops:
  0.6 1.3 %broadcast_in_dim.2 = f32[32,3,128]{2,1,0:T(4,128)} broadcast(f32[3,128]{1,0:T(4,128)} %param.10), dimensions={1,2} | broadcast | bytes 50688 | tf_op jit(solution)/shard_map/broadcast_in_dim | solution.py:363
  1.9 10.3 %all-to-all-start = ((f32[32,3,128]{2,1,0:T(4,128)}), f32[32,3,128]{2,1,0:T(4,128)S(1)}, u32[]{:S(2)}, u32[]{:S(2)}) async-start(f32[32,3,128]{2,1,0:T(4,128)} %broadcast_in_dim.2), calls=%async_computation | async-start | bytes 131072 | tf_op jit(solution)/shard_map/all_to_all | solution.py:363
  12.9 0.0 copy-start
  12.9 0.7 copy-done
  13.6 0.0 copy-start.1
  13.6 0.7 copy-done.1
  14.3 0.0 copy-start.2
  14.3 0.7 copy-done.2
  15.0 0.0 copy-start.3
  15.0 0.7 copy-done.3
  15.7 0.0 copy-start.4
  15.7 0.7 copy-done.4
  16.4 0.0 copy-start.5
  16.4 0.7 copy-done.5
  17.1 2.7 %prep.1 = (f32[16,16,128]{2,1,0:T(8,128)S(1)}, f32[4,8,128]{2,1,0:T(8,128)S(1)}, s32[4,32]{1,0:T(4,128)S(1)}, s32[128]{0:T(128)S(1)}, s32[1]{0:T(128)}, /*index=5*/bf16[2048,128]{1,0:T(8,128)(2,1)S(1)}) custom-call(f32[3,512]{1,0:T(4,128)S(1)} %copy-done.1, s32[26,64]{1,0:T(8,128)S(1)} %bitcast.1, s32[1]{0:T(128)S(6)} %copy.10.count_ref, f32[8]{0:T(128)S(1)} %copy-done.5, ...), custom_call_target="tpu_custom_call" | custom-call | flops 1000000000 | bytes 12000000 | tf_op jit(solution)/shard_map/prep/pallas_call | solution.py:364
  19.7 0.0 all-to-all-done.tgt_ref
  19.8 25.1 %all_to_all.25.recv_ref = f32[16,16,128]{2,1,0:T(8,128)S(1)} all-to-all(f32[16,16,128]{2,1,0:T(8,128)S(1)} %get-tuple-element.24), channel_id=1, replica_groups=mesh['y'=4,'z'=16,'x'=4,'core'=2] {'z'}, dimensions={0} | all-to-all | bytes 262144 | tf_op jit(solution)/shard_map/all_to_all | solution.py:387
  44.9 9.1 %first.1 = (f32[32,8,128]{2,1,0:T(8,128)S(1)}, bf16[512,128]{1,0:T(8,128)(2,1)S(1)}, bf16[512,128]{1,0:T(8,128)(2,1)S(1)}, bf16[17,256,1024]{2,1,0:T(8,128)(2,1)...) custom-call(s32[128]{0:T(128)S(1)} %get-tuple-element.19.chunk_ref, ...), custom_call_target="tpu_custom_call" | custom-call | tf_op jit(solution)/shard_map/first/pallas_call | solution.py:391
  54.0 18.5 %all_to_all.26.recv_ref = f32[32,8,128]{2,1,0:T(8,128)S(1)} all-to-all(f32[32,8,128]{2,1,0:T(8,128)S(1)} %get-tuple-element.26), channel_id=1, replica_groups=mesh['y'=4,'z'=16,'x'=4,'core'=2] {'y','x','core'}, dimensions={0} | all-to-all | bytes 262144 | tf_op jit(solution)/shard_map/all_to_all | solution.py:416
  72.5 15.3 %all_to_all.27.recv_ref = f32[16,8,128]{2,1,0:T(8,128)S(1)} all-to-all(f32[16,8,128]{2,1,0:T(8,128)S(1)} %get-tuple-element.28), channel_id=1, replica_groups=mesh['y'=4,'z'=16,'x'=4,'core'=2] {'z'}, dimensions={0} | all-to-all | bytes 131072 | tf_op jit(solution)/shard_map/all_to_all | solution.py:419
  87.8 5.9 %second.1 = f32[32,8,128]{2,1,0:T(8,128)S(1)} custom-call(s32[128]{0:T(128)S(1)} %get-tuple-element.19.chunk_ref, s32[1]{0:T(128)} %get-tuple-element.20.count_ref, s32[4,32]{1,0:T(4,128)S(1)} %get-tuple-element.21.far_ref, f32[16,8,128]{2,1,0:T(8,128)S(1)} %all_to_all.27.recv_ref, bf16[512,128]{1,0:T(8,128)(2,1)S(1)} %get-tuple-element.29.ih_ref, ...), custom_call_target="tpu_custom_call" | custom-call | tf_op jit(solution)/shard_map/second/pallas_call | solution.py:420
  93.6 13.5 %all_to_all.28.recv_ref = f32[32,8,128]{2,1,0:T(8,128)S(1)} all-to-all(f32[32,8,128]{2,1,0:T(8,128)S(1)} %second.1), channel_id=1, replica_groups=mesh['y'=4,'z'=16,'x'=4,'core'=2] {'y','x','core'}, dimensions={0} | all-to-all | bytes 262144 | tf_op jit(solution)/shard_map/all_to_all | solution.py:416
  107.1 0.6 update.3
  (1 shorter events, 0.0 us)
Async XLA Ops:
  1.9 17.8 %all-to-all-start = ((f32[32,3,128]{2,1,0:T(4,128)}), f32[32,3,128]{2,1,0:T(4,128)S(1)}, u32[]{:S(2)}, u32[]{:S(2)}) async-start(f32[32,3,128]{2,1,0:T(4,128)} %broadcast_in_dim.2), calls=%async_computation | async-start | bytes 131072 | tf_op jit(solution)/shard_map/all_to_all | solution.py:363
  12.9 0.7 copy-start
  13.6 0.7 copy-start.1
  14.3 0.7 copy-start.2
  15.0 0.7 copy-start.3
  15.7 0.7 copy-start.4
  16.4 0.7 copy-start.5

commit v4 on v3

--- a/solution.py
+++ b/solution.py
@@ -134,32 +134,20 @@
     count_ref[0] = total >> 1
 
 
-def prep_kernel(
-    centers_ref, near_ref, count_ref, steps_ref, charges_hbm, coords_hbm, boundary_hbm,
-    zsend_ref, held_ref, far_ref, chunk_ref, chunks_ref, proxy_ref,
-    mine_ref, wide_ref, coords_ref, sem,
-):
+def prologue_kernel(count_ref, centers_hbm, charges_hbm, coords_hbm, zsend_ref, current_ref, coords_ref, centers_ref, sem):
     y, z, member = here()
     leaf = (y * NZ + z) * MEMBERS + member
     copies = [
-        pltpu.make_async_copy(source, target, sem.at[k])
-        for k, (source, target) in enumerate(((charges_hbm, held_ref.at[0]), (coords_hbm, coords_ref), (boundary_hbm, held_ref.at[1])))
+        pltpu.make_async_copy(charges_hbm, current_ref, sem.at[0]),
+        pltpu.make_async_copy(coords_hbm, coords_ref, sem.at[1]),
+        pltpu.make_async_copy(centers_hbm, centers_ref, sem.at[2]),
     ]
     for copy in copies:
         copy.start()
-    make_lists(y, z, near_ref, far_ref, chunk_ref, chunks_ref, mine_ref)
     for copy in copies:
         copy.wait()
-    lane = iota((8, 128), 1)
-    row = iota((8, 128), 0)
-    live = (lane < count_ref[0]).astype(f32)
-    current = held_ref[0] * live
-    held_ref[0] = current
-    steps = jnp.zeros((8, 128), f32)
-    for k in range(8):
-        steps = jnp.where(row == k, steps_ref[k], steps)
-    held_ref[2] = steps
-    held_ref[3] = live
+    current = current_ref[...] * (iota((8, 128), 1) < count_ref[0]).astype(f32)
+    current_ref[...] = current
     u = jnp.concatenate([coords_ref[...], jnp.zeros((5, 128), f32)], 0)
     center = column3(centers_ref[0, leaf], centers_ref[1, leaf], centers_ref[2, leaf], (8, 128))
     shifted = jnp.concatenate([jnp.zeros((5, 128), f32), coords_ref[...]], 0)
@@ -167,6 +155,33 @@
     for k in range(NZ):
         zsend_ref[k, 0:8] = current
         zsend_ref[k, 8:16] = rows
+
+
+def prep_kernel(
+    centers_ref, near_ref, count_ref, steps_ref, boundary_hbm, targets_hbm,
+    tsend_ref, held_ref, far_ref, chunk_ref, chunks_ref, proxy_ref,
+    mine_ref, wide_ref, targets_ref, sem,
+):
+    y, z, member = here()
+    copies = [
+        pltpu.make_async_copy(boundary_hbm, held_ref.at[0], sem.at[0]),
+        pltpu.make_async_copy(targets_hbm, targets_ref, sem.at[1]),
+    ]
+    for copy in copies:
+        copy.start()
+    make_lists(y, z, near_ref, far_ref, chunk_ref, chunks_ref, mine_ref)
+    for copy in copies:
+        copy.wait()
+    rows = target_rows(jnp.concatenate([targets_ref[...], jnp.zeros((5, 128), f32)], 0))
+    for k in range(PLANE):
+        tsend_ref[k] = rows
+    lane = iota((8, 128), 1)
+    row = iota((8, 128), 0)
+    steps = jnp.zeros((8, 128), f32)
+    for k in range(8):
+        steps = jnp.where(row == k, steps_ref[k], steps)
+    held_ref[1] = steps
+    held_ref[2] = (lane < count_ref[0]).astype(f32)
     p = lane & 31
     offset = jnp.where(
         row == 0,
@@ -223,7 +238,7 @@
                 q_ref[FAR + other * 4 + block] = out.astype(bf16)
 
 
-def setup_kernel(far_ref, recv_ref, a_ref, ih_ref, il_ref, q_ref, wide_ref):
+def setup_kernel(far_ref, recv_ref, proxy_ref, a_ref, ih_ref, il_ref, q_ref, wide_ref):
     tables = interp_tables()
     for k in range(NZ):
         rows = recv_ref[k, 8:16]
@@ -238,6 +253,7 @@
         hi, lo = split2(value)
         ih_ref[k * 32 : (k + 1) * 32] = hi
         il_ref[k * 32 : (k + 1) * 32] = lo
+    a_ref[FAR * 128 :] = proxy_ref[...]
     charge_blocks(recv_ref, ih_ref, il_ref, far_ref, q_ref, wide_ref)
 
 
@@ -259,14 +275,9 @@
             out_ref[other * MEMBERS + k] = total[:, k * 128 : (k + 1) * 128]
 
 
-def first_kernel(
-    chunk_ref, count_ref, far_ref, tgt_ref, recv_ref, proxy_ref, out_ref, ih_ref, il_ref, eh_ref, el_ref, oh_ref, ol_ref, a_ref, q_ref, wide_ref, b_ref, acc_ref
-):
-    setup_kernel(far_ref, recv_ref, a_ref, ih_ref, il_ref, q_ref, wide_ref)
-    a_ref[FAR * 128 :] = proxy_ref[...]
+def first_kernel(chunk_ref, count_ref, tgt_ref, a_ref, q_ref, out_ref, eh_ref, el_ref, oh_ref, ol_ref, b_ref, acc_ref):
     for other in range(NY):
-        points = jnp.concatenate([tgt_ref[other * MEMBERS + k] for k in range(MEMBERS)], 1)
-        h, m, low = split3(target_rows(jnp.concatenate([points, jnp.zeros((5, MEMBERS * 128), f32)], 0)))
+        h, m, low = split3(jnp.concatenate([tgt_ref[other * MEMBERS + k] for k in range(MEMBERS)], 1))
         b_ref[other] = jnp.concatenate([h, m, h, m, low, h], 0).astype(bf16)
     acc_ref[...] = jnp.zeros_like(acc_ref)
     count = count_ref[0]
@@ -327,24 +338,19 @@
     write_sums(acc_ref, out_ref)
 
 
-def update_kernel(scale, last, recv_ref, held_ref, *refs):
+def update_kernel(scale, last, recv_ref, held_ref, current_ref, new_ref, other_ref):
     parts = [recv_ref[k] for k in range(PLANE)]
     while len(parts) > 1:
         parts = [parts[i] + parts[i + 1] for i in range(0, len(parts), 2)]
-    live = held_ref[3]
-    residual = live * (held_ref[1] - scale * parts[0])
+    live = held_ref[2]
+    residual = live * (held_ref[0] - scale * parts[0])
+    new = live * (current_ref[...] + held_ref[1] * residual / (1.0 + jnp.abs(residual)))
+    new_ref[...] = new
     if last:
-        current_ref, new_ref, residual_ref = refs
-        residual_ref[...] = residual
-        current = current_ref[...]
+        other_ref[...] = residual
     else:
-        new_ref, zsend_ref = refs
-        current = held_ref[0]
-    new = live * (current + held_ref[2] * residual / (1.0 + jnp.abs(residual)))
-    new_ref[...] = new
-    if not last:
         for k in range(NZ):
-            zsend_ref[k] = new
+            other_ref[k] = new
 
 
 VM = pl.BlockSpec(memory_space=pltpu.VMEM)
@@ -360,62 +366,76 @@
     plane = ("y", "x", "core")
     params = pltpu.CompilerParams(vmem_limit_bytes=12 * 2**20)
     small = pltpu.CompilerParams(vmem_limit_bytes=4 * 2**20)
-    targets = lax.all_to_all(jnp.broadcast_to(target_points[None], (PLANE, 3, 128)), plane, 0, 0, tiled=True)
-    zsend, held, far, chunks, count, proxies = pl.pallas_call(
+    hbm = functools.partial(pltpu.with_memory_space_constraint, memory_space=pltpu.HBM)
+    charges, source_coords, boundary_data, target_points = map(hbm, (charges, source_coords, boundary_data, target_points))
+    zsend, current = pl.pallas_call(
+        prologue_kernel,
+        out_shape=(sds((NZ, 16, 128)), sds((8, 128))),
+        in_specs=[SM, HB, HB, HB],
+        out_specs=(VM, VM),
+        scratch_shapes=[pltpu.VMEM((3, 128), f32), pltpu.SMEM((3, NZ * NY * MEMBERS), f32), pltpu.SemaphoreType.DMA((3,))],
+        compiler_params=small,
+        name="prologue",
+    )(valid_count, hbm(leaf_centers), charges, source_coords)
+    recv = lax.all_to_all(zsend, "z", 0, 0, tiled=True)
+    tsend, held, far, chunks, count, proxies = pl.pallas_call(
         prep_kernel,
         out_shape=(
-            sds((NZ, 16, 128)),
-            sds((4, 8, 128)),
+            sds((PLANE, 8, 128)),
+            sds((3, 8, 128)),
             sds((NY, FAR_SLOTS), jnp.int32),
             sds((CHUNK_SLOTS,), jnp.int32),
             sds((1,), jnp.int32),
             sds((4 * NY * 128, 128), bf16),
         ),
-        in_specs=[SM, SM, SM, SM, HB, HB, HB],
+        in_specs=[SM, SM, SM, SM, HB, HB],
         out_specs=(VM, VM, SM, SM, SM, VM),
         scratch_shapes=[
             pltpu.SMEM((NZ + 1,), jnp.int32),
             pltpu.VMEM((544, 128), bf16),
             pltpu.VMEM((3, 128), f32),
-            pltpu.SemaphoreType.DMA((3,)),
+            pltpu.SemaphoreType.DMA((2,)),
         ],
         compiler_params=small,
         cost_estimate=pl.CostEstimate(flops=10**9, bytes_accessed=12 * 10**6, transcendentals=0),
         name="prep",
-    )(leaf_centers, near_lists.T, valid_count, step_sizes, charges, source_coords, boundary_data)
-    zsend, targets = lax.optimization_barrier((zsend, targets))
-    recv = lax.all_to_all(zsend, "z", 0, 0, tiled=True)
+    )(leaf_centers, near_lists.T, valid_count, step_sizes, boundary_data, target_points)
+    recv, tsend = lax.optimization_barrier((recv, tsend))
+    targets = lax.all_to_all(tsend, plane, 0, 0, tiled=True)
+    interp = sds((NZ * 32, 128), bf16)
+    a, ih, il, q = pl.pallas_call(
+        setup_kernel,
+        out_shape=(sds((ZERO_BLOCK * 128, 128), bf16), interp, interp, sds((ZERO_BLOCK + 1, 16, 128), bf16)),
+        in_specs=[SM, VM, VM],
+        out_specs=(VM,) * 4,
+        scratch_shapes=[pltpu.VMEM((5, 16, 128), f32)],
+        compiler_params=params,
+        cost_estimate=pl.CostEstimate(flops=10**9, bytes_accessed=8 * 10**6, transcendentals=0),
+        name="setup",
+    )(far, recv, proxies)
     scale = 1.0 / math.sqrt(NY * NZ * MEMBERS * 128)
     half = pltpu.VMEM((PAIRS, 256, MEMBERS * 128), bf16)
-    interp = sds((NZ * 32, 128), bf16)
-    sums, ih, il, *kernels = pl.pallas_call(
+    sums, *kernels = pl.pallas_call(
         first_kernel,
-        out_shape=(sds((PLANE, 8, 128)), interp, interp, half, half, half, half),
-        in_specs=[SM, SM, SM, VM, VM, VM],
-        out_specs=(VM,) * 7,
-        scratch_shapes=[
-            pltpu.VMEM((ZERO_BLOCK * 128, 128), bf16),
-            pltpu.VMEM((ZERO_BLOCK + 1, 16, 128), bf16),
-            pltpu.VMEM((5, 16, 128), f32),
-            pltpu.VMEM((NY, DEPTH, MEMBERS * 128), bf16),
-            pltpu.VMEM((NY * 16, MEMBERS * 128), f32),
-        ],
+        out_shape=(sds((PLANE, 8, 128)), half, half, half, half),
+        in_specs=[SM, SM, VM, VM, VM],
+        out_specs=(VM,) * 5,
+        scratch_shapes=[pltpu.VMEM((NY, DEPTH, MEMBERS * 128), bf16), pltpu.VMEM((NY * 16, MEMBERS * 128), f32)],
         compiler_params=params,
         name="first",
-    )(chunks, count, far, targets, recv, proxies)
-
-    def update(sums, *current):
-        last = len(current) > 0
+    )(chunks, count, targets, a, q)
+
+    def update(sums, current, last):
         return pl.pallas_call(
             functools.partial(update_kernel, scale, last),
             out_shape=(sds((8, 128)), sds((8, 128) if last else (NZ, 8, 128))),
-            in_specs=[VM, VM] + [VM] * last,
+            in_specs=[VM, VM, VM],
             out_specs=(VM, VM),
             compiler_params=small,
             name="update",
-        )(lax.all_to_all(sums, plane, 0, 0, tiled=True), held, *current)
-
-    current, zsend = update(sums)
+        )(lax.all_to_all(sums, plane, 0, 0, tiled=True), held, current)
+
+    current, zsend = update(sums, current, False)
     recv = lax.all_to_all(zsend, "z", 0, 0, tiled=True)
     sums = pl.pallas_call(
         second_kernel,
@@ -430,7 +450,7 @@
         compiler_params=params,
         name="second",
     )(chunks, count, far, recv, ih, il, *kernels)
-    current, residual = update(sums, current)
+    current, residual = update(sums, current, True)
     return (current, residual)
 
 

time: 109 us -> 105 us (0.963)
  blocking collectives: 72.4 us -> 40.2 us
  starting transfers between devices: 10.3 us -> 26.6 us
  waiting for transfers between devices: 0.01 us -> 12.9 us
  local copies, waits for them, and re-layouts: 5.43 us -> 2.06 us
  Pallas kernels: 18.3 us -> 21.3 us
    all_to_all x2 -> x1, blocking collectives: 40.4 us -> 14.8 us  [body(): recv = lax.all_to_all(zsend, 'z', 0, 0, tiled=True)]
    all_to_all x1 -> x2, starting transfers between devices: 10.3 us -> 26.6 us  [the longest x1 15.7 us: body(): recv = lax.all_to_all(zsend, 'z', 0, 0, tiled=True)]
    all_to_all x1 -> x2, waiting for transfers between devices: 0.01 us -> 12.9 us  [the longest x1 7.21 us: body(): recv = lax.all_to_all(zsend, 'z', 0, 0, tiled=True)]
    all_to_all x2, blocking collectives: 32 us -> 25.4 us  [update(): lax.all_to_all(sums, plane, 0, 0, tiled=True)]
    pallas_call x2 -> x4, Pallas kernels: 11.8 us -> 14.5 us  [the longest x1 8.19 us: body(): pl.pallas_call(first_kernel, out_shape=(sds((PLANE, 8, 128)), half, half,...]
    unnamed x12 -> x6, local copies, waits for them, and re-layouts: 4.12 us -> 2.06 us
    broadcast_in_dim x1 -> x0, local copies, waits for them, and re-layouts: 1.32 us -> none  [body(): jnp.broadcast_to(target_points[None], (PLANE, 3, 128))]
  transfers between devices with their start and end apart: 1 -> 2, of which waited for: 0 -> 2; matrix products, arithmetic and copies ran while one was open for 0% -> 0% of each run, Pallas kernels for 2% -> 4%
where the time goes in v4:
time: 105 us; the launch traced here: 104 us
  blocking collectives  40.2 us (38%)
  starting transfers between devices  26.6 us (25%)
  Pallas kernels  21.3 us (20%)
  waiting for transfers between devices  12.9 us (12%)
  local copies, waits for them, and re-layouts  2.06 us (2%)
  between operations  1.34 us (1%)
    all_to_all x2, blocking collectives, update(): lax.all_to_all(sums, plane, 0, 0, tiled=True)  25.4 us
    all_to_all x1, starting transfers between devices, body(): recv = lax.all_to_all(zsend, 'z', 0, 0, tiled=True)  15.7 us
    all_to_all x1, blocking collectives, body(): recv = lax.all_to_all(zsend, 'z', 0, 0, tiled=True)  14.8 us
    all_to_all x1, starting transfers between devices, body(): targets = lax.all_to_all(tsend, plane, 0, 0, tiled=True)  10.8 us
    pallas_call x1, Pallas kernels, body(): pl.pallas_call(first_kernel, out_shape=(sds((PLANE, 8, 128)), half, half,...  8.19 us
    all_to_all x1, waiting for transfers between devices, body(): recv = lax.all_to_all(zsend, 'z', 0, 0, tiled=True)  7.21 us
    pallas_call x1, Pallas kernels, body(): pl.pallas_call(second_kernel, out_shape=sds((PLANE, 8, 128)), in_specs=[S...  6.19 us
    all_to_all x1, waiting for transfers between devices, body(): targets = lax.all_to_all(tsend, plane, 0, 0, tiled=True)  5.65 us
  transfers between devices with their start and end apart: 2, of which 2 were waited for; matrix products, arithmetic and copies ran while one was open for 0% of the time, Pallas kernels for 4%

profile of v4, /device:TPU:1, one launch (start us, length us, event | category | flops | bytes accessed | tf_op | source)
XLA Modules:
  0.0 104.4 jit_solution(1113769710624123433)
XLA Ops:
  1.3 1.6 %prologue.1 = (f32[16,16,128]{2,1,0:T(8,128)}, f32[8,128]{1,0:T(8,128)S(1)}) custom-call(s32[1]{0:T(128)S(6)} %copy.10.count_ref, f32[3,512]{1,0:T(4,128)} %centers_hbm.1, f32[8,128]{1,0:T(8,128)} %charges_hbm.1, f32[3,128]{1,0:T(4,128)} %coords_hbm.1), custom_call_target="tpu_custom_call" | custom-call | tf_op jit(solution)/shard_map/prologue/pallas_call | solution.py:371
  2.9 15.7 %all-to-all-start = ((f32[16,16,128]{2,1,0:T(8,128)}), f32[16,16,128]{2,1,0:T(8,128)S(1)}, u32[]{:S(2)}, u32[]{:S(2)}) async-start(f32[16,16,128]{2,1,0:T(8,128)} %get-tuple-element.26), calls=%async_computation | async-start | bytes 262144 | tf_op jit(solution)/shard_map/all_to_all | solution.py:380
  18.7 0.0 copy-start
  18.7 0.7 copy-done
  19.4 0.0 copy-start.1
  19.4 0.7 copy-done.1
  20.1 0.0 copy-start.2
  20.1 0.7 copy-done.2
  20.7 2.7 %prep.1 = (f32[32,8,128]{2,1,0:T(8,128)}, f32[3,8,128]{2,1,0:T(8,128)S(1)}, s32[4,32]{1,0:T(4,128)S(1)}, s32[128]{0:T(128)S(1)}, s32[1]{0:T(128)}, /*index=5*/bf16[2048,128]{1,0:T(8,128)(2,1)S(1)}) custom-call(f32[3,512]{1,0:T(4,128)S(1)} %copy-done, s32[26,64]{1,0:T(8,128)S(1)} %bitcast.1, s32[1]{0:T(128)S(6)} %copy.10.count_ref, f32[8]{0:T(128)S(1)} %copy-done.2, ...), custom_call_target="tpu_custom_call" | custom-call | flops 1000000000 | bytes 12000000 | tf_op jit(solution)/shard_map/prep/pallas_call | solution.py:381
  23.4 7.2 %all-to-all-done.recv_ref = f32[16,16,128]{2,1,0:T(8,128)S(1)} async-done(((f32[16,16,128]{2,1,0:T(8,128)}), f32[16,16,128]{2,1,0:T(8,128)S(1)}, u32[]{:S(2)}, u32[]{:S(2)}) %all-to-all-start) | async-done | bytes 131104 | tf_op jit(solution)/shard_map/all_to_all | solution.py:380
  30.7 10.8 %all-to-all-start.1 = ((f32[32,8,128]{2,1,0:T(8,128)}), f32[32,8,128]{2,1,0:T(8,128)S(1)}, u32[]{:S(2)}, u32[]{:S(2)}) async-start(f32[32,8,128]{2,1,0:T(8,128)} %get-tuple-element.28), calls=%async_computation.1 | async-start | bytes 262144 | tf_op jit(solution)/shard_map/all_to_all | solution.py:404
  41.5 1.9 %setup.1 = (bf16[4096,128]{1,0:T(8,128)(2,1)S(1)}, bf16[512,128]{1,0:T(8,128)(2,1)S(1)}, bf16[512,128]{1,0:T(8,128)(2,1)S(1)}, bf16[33,16,128]{2,1,0:T(8,128)(2,1)S(1)}) custom-call(s32[4,32]{1,0:T(4,128)S(1)} %get-tuple-element.25.far_ref, f32[16,16,128]{2,1,0:T(8,128)S(1)} %all-to-all-done.recv_ref, bf16[2048,128]{1,0:T(8,128)(2,1)S(1)} %get-tuple-element.30.proxy_ref), custom_call_target="tpu_custom_call" | custom-call | flops 1000000000 | bytes 8000000 | tf_op jit(solution)/shard_map/setup/pallas_call | solution.py:406
  43.5 5.7 %all-to-all-done.1.tgt_ref = f32[32,8,128]{2,1,0:T(8,128)S(1)} async-done(((f32[32,8,128]{2,1,0:T(8,128)}), f32[32,8,128]{2,1,0:T(8,128)S(1)}, u32[]{:S(2)}, u32[]{:S(2)}) %all-to-all-start.1) | async-done | bytes 131104 | tf_op jit(solution)/shard_map/all_to_all | solution.py:404
  49.1 8.2 %first.1 = (f32[32,8,128]{2,1,0:T(8,128)S(1)}, bf16[17,256,1024]{2,1,0:T(8,128)(2,1)S(1)}, bf16[17,256,1024]{2,1,0:T(8,128)(2,1)S(1)}, bf16[17,256,1024]{2,1,0:T(8,128)(2,1)S(1)}, bf16[17,256,1024]{2,1,0:T(8,128)(2,1)S(1)}) custom-call(s32[128]{0:T(128)S(1)} %get-tuple-element.23.chunk_ref, s32[1]{0:T(128)} %get-tuple-element.24.count_ref, ...), custom_call_target="tpu_custom_call" | custom-call | tf_op jit(solution)/shard_map/first/pallas_call | solution.py:418
  57.3 12.3 %all_to_all.25.recv_ref = f32[32,8,128]{2,1,0:T(8,128)S(1)} all-to-all(f32[32,8,128]{2,1,0:T(8,128)S(1)} %get-tuple-element.33), channel_id=1, replica_groups=mesh['y'=4,'z'=16,'x'=4,'core'=2] {'y','x','core'}, dimensions={0} | all-to-all | bytes 262144 | tf_op jit(solution)/shard_map/all_to_all | solution.py:436
  69.6 14.8 %all_to_all.26.recv_ref = f32[16,8,128]{2,1,0:T(8,128)S(1)} all-to-all(f32[16,8,128]{2,1,0:T(8,128)S(1)} %get-tuple-element.36), channel_id=1, replica_groups=mesh['y'=4,'z'=16,'x'=4,'core'=2] {'z'}, dimensions={0} | all-to-all | bytes 131072 | tf_op jit(solution)/shard_map/all_to_all | solution.py:439
  84.4 6.2 %second.1 = f32[32,8,128]{2,1,0:T(8,128)S(1)} custom-call(s32[128]{0:T(128)S(1)} %get-tuple-element.23.chunk_ref, s32[1]{0:T(128)} %get-tuple-element.24.count_ref, s32[4,32]{1,0:T(4,128)S(1)} %get-tuple-element.25.far_ref, f32[16,8,128]{2,1,0:T(8,128)S(1)} %all_to_all.26.recv_ref, bf16[512,128]{1,0:T(8,128)(2,1)S(1)} %get-tuple-element.37.ih_ref, ...), custom_call_target="tpu_custom_call" | custom-call | tf_op jit(solution)/shard_map/second/pallas_call | solution.py:440
  90.6 13.2 %all_to_all.27.recv_ref = f32[32,8,128]{2,1,0:T(8,128)S(1)} all-to-all(f32[32,8,128]{2,1,0:T(8,128)S(1)} %second.1), channel_id=1, replica_groups=mesh['y'=4,'z'=16,'x'=4,'core'=2] {'y','x','core'}, dimensions={0} | all-to-all | bytes 262144 | tf_op jit(solution)/shard_map/all_to_all | solution.py:436
  103.8 0.6 update.3
  (1 shorter events, 0.0 us)
Async XLA Ops:
  2.9 27.7 %all-to-all-start = ((f32[16,16,128]{2,1,0:T(8,128)}), f32[16,16,128]{2,1,0:T(8,128)S(1)}, u32[]{:S(2)}, u32[]{:S(2)}) async-start(f32[16,16,128]{2,1,0:T(8,128)} %get-tuple-element.26), calls=%async_computation | async-start | bytes 262144 | tf_op jit(solution)/shard_map/all_to_all | solution.py:380
  18.7 0.7 copy-start
  19.4 0.7 copy-start.1
  20.1 0.7 copy-start.2
  30.7 18.5 %all-to-all-start.1 = ((f32[32,8,128]{2,1,0:T(8,128)}), f32[32,8,128]{2,1,0:T(8,128)S(1)}, u32[]{:S(2)}, u32[]{:S(2)}) async-start(f32[32,8,128]{2,1,0:T(8,128)} %get-tuple-element.28), calls=%async_computation.1 | async-start | bytes 262144 | tf_op jit(solution)/shard_map/all_to_all | solution.py:404

commit v5 on v4

--- a/solution.py
+++ b/solution.py
@@ -23,6 +23,8 @@
 CHUNK_OWNER = 80
 CHUNK_SLOTS = 128
 PAIRS = 17
+TILE = 256
+TILES = MEMBERS * 128 // TILE
 bf16, f32 = jnp.bfloat16, jnp.float32
 
 
@@ -54,11 +56,11 @@
     return h, (v - h.astype(f32)).astype(bf16)
 
 
-def source_rows(pts, extra):
+def source_rows(pts):
     row = iota(pts.shape, 0)
     s = jnp.where(row < 3, pts - 0.5, 0.0)
     norm = jnp.sum(s * s, axis=0, keepdims=True) + SOFTENING
-    return jnp.where(row < 3, -2.0 * s, jnp.where(row == 3, norm, jnp.where(row == 4, 1.0, extra)))
+    return jnp.where(row < 3, -2.0 * s, jnp.where(row == 3, norm, jnp.where(row == 4, 1.0, 0.0)))
 
 
 def target_rows(pts):
@@ -79,7 +81,6 @@
 
 
 def a_block(rows):
-    rows = jnp.where(iota(rows.shape, 0) < 5, rows, 0.0)
     h, m, low = split3(rows)
     return jnp.concatenate([h, h, m, m, h, low], 0).T.astype(bf16)
 
@@ -102,6 +103,7 @@
     for other in range(NY):
         for k in range(NZ):
             mine_ref[k] = 0
+            far_ref[other, k] = NZ
         mine_ref[z] = (y == other).astype(jnp.int32)
         for j in range(NEAR):
             cluster = near_ref[j, other * NZ + z]
@@ -111,11 +113,9 @@
         for k in range(NZ):
             mine = mine_ref[k]
             chunk_ref[total + near_count] = k
-            far_ref[other, far_count] = k
+            far_ref[other, far_count] = jnp.where(mine > 0, NZ, k)
             near_count = near_count + mine
             far_count = far_count + 1 - mine
-        for k in range(3):
-            far_ref[other, far_count + k] = NZ
         far_blocks = (far_count + 3) // 4
         start = total + near_count
         for k in range(4):
@@ -134,27 +134,19 @@
     count_ref[0] = total >> 1
 
 
-def prologue_kernel(count_ref, centers_hbm, charges_hbm, coords_hbm, zsend_ref, current_ref, coords_ref, centers_ref, sem):
-    y, z, member = here()
-    leaf = (y * NZ + z) * MEMBERS + member
-    copies = [
-        pltpu.make_async_copy(charges_hbm, current_ref, sem.at[0]),
-        pltpu.make_async_copy(coords_hbm, coords_ref, sem.at[1]),
-        pltpu.make_async_copy(centers_hbm, centers_ref, sem.at[2]),
-    ]
+def prologue_kernel(count_ref, charges_hbm, coords_hbm, zsend_ref, current_ref, coords_ref, sem):
+    copies = [pltpu.make_async_copy(charges_hbm, current_ref, sem.at[0]), pltpu.make_async_copy(coords_hbm, coords_ref, sem.at[1])]
     for copy in copies:
         copy.start()
     for copy in copies:
         copy.wait()
     current = current_ref[...] * (iota((8, 128), 1) < count_ref[0]).astype(f32)
     current_ref[...] = current
-    u = jnp.concatenate([coords_ref[...], jnp.zeros((5, 128), f32)], 0)
-    center = column3(centers_ref[0, leaf], centers_ref[1, leaf], centers_ref[2, leaf], (8, 128))
-    shifted = jnp.concatenate([jnp.zeros((5, 128), f32), coords_ref[...]], 0)
-    rows = source_rows(center + HALF_SIDE * u, shifted)
+    coords = jnp.concatenate([coords_ref[...], jnp.zeros((1, 128), f32)], 0)
     for k in range(NZ):
-        zsend_ref[k, 0:8] = current
-        zsend_ref[k, 8:16] = rows
+        zsend_ref[3 * k] = current[0:4]
+        zsend_ref[3 * k + 1] = current[4:8]
+        zsend_ref[3 * k + 2] = coords
 
 
 def prep_kernel(
@@ -194,7 +186,7 @@
             leaf = (y * NZ + block * 4 + k) * MEMBERS + member
             column = column3(centers_ref[0, leaf], centers_ref[1, leaf], centers_ref[2, leaf], (8, 128))
             center = jnp.where((lane >> 5) == k, column, center)
-        rows = source_rows(center + HALF_SIDE * offset, 0.0)
+        rows = source_rows(center + HALF_SIDE * offset)
         wide_ref[block * 128 : (block + 1) * 128, :DEPTH] = a_block(rows)
     wide_ref[512:544, :DEPTH] = wide_ref[0:32, :DEPTH]
     for other in range(NY):
@@ -208,11 +200,11 @@
                     proxy_ref[base : base + 32] = wide_ref[pl.ds(pl.multiple_of(leaf * 32, 32), 32)]
 
 
-def charge_blocks(recv_ref, ih_ref, il_ref, far_ref, q_ref, wide_ref):
+def charge_blocks(charges, ih_ref, il_ref, far_ref, q_ref, wide_ref):
     far = []
     nt = (((1,), (1,)), ((), ()))
     for k in range(NZ):
-        hi, lo = split2(recv_ref[k, 0:8])
+        hi, lo = split2(charges(k))
         q = jnp.concatenate([hi.astype(f32), lo.astype(f32)], 0).astype(bf16)
         q_ref[k] = q
         both = lax.dot_general(q, ih_ref[k * 32 : (k + 1) * 32], nt, preferred_element_type=f32)
@@ -227,25 +219,26 @@
     group = iota((16, 128), 1) >> 5
     for other in range(NY):
         for block in range(4):
-
-            @pl.when(block < far_ref[other, FAR_SLOTS - 1])
-            def _(other=other, block=block):
-                out = jnp.zeros((16, 128), f32)
-                for k in range(4):
-                    leaf = far_ref[other, block * 4 + k]
-                    moved = pltpu.roll(wide_ref[leaf >> 2], ((4 + k - leaf) & 3) * 32, 1)
-                    out = jnp.where(group == k, moved, out)
-                q_ref[FAR + other * 4 + block] = out.astype(bf16)
-
-
-def setup_kernel(far_ref, recv_ref, proxy_ref, a_ref, ih_ref, il_ref, q_ref, wide_ref):
+            out = None
+            for k in range(4):
+                leaf = far_ref[other, block * 4 + k]
+                moved = pltpu.roll(wide_ref[leaf >> 2], ((4 + k - leaf) & 3) * 32, 1)
+                out = moved if out is None else jnp.where(group == k, moved, out)
+            q_ref[FAR + other * 4 + block] = out.astype(bf16)
+
+
+def setup_kernel(far_ref, centers_ref, recv_ref, proxy_ref, a_ref, ih_ref, il_ref, q_ref, wide_ref):
     tables = interp_tables()
+    y, _, member = here()
     for k in range(NZ):
-        rows = recv_ref[k, 8:16]
-        a_ref[k * 128 : (k + 1) * 128, :DEPTH] = a_block(rows)
+        rows = recv_ref[3 * k + 2]
+        leaf = (y * NZ + k) * MEMBERS + member
+        center = column3(centers_ref[0, leaf], centers_ref[1, leaf], centers_ref[2, leaf], (8, 128))
+        points = center + HALF_SIDE * jnp.concatenate([rows, jnp.zeros((4, 128), f32)], 0)
+        a_ref[k * 128 : (k + 1) * 128, :DEPTH] = a_block(source_rows(points))
         value = None
         for axis, (roots, scale) in enumerate(tables):
-            u = jnp.broadcast_to(rows[5 + axis : 6 + axis], (32, 128))
+            u = jnp.broadcast_to(rows[axis : axis + 1], (32, 128))
             line = scale
             for root in roots:
                 line = line * (u - root)
@@ -254,18 +247,15 @@
         ih_ref[k * 32 : (k + 1) * 32] = hi
         il_ref[k * 32 : (k + 1) * 32] = lo
     a_ref[FAR * 128 :] = proxy_ref[...]
-    charge_blocks(recv_ref, ih_ref, il_ref, far_ref, q_ref, wide_ref)
-
-
-def charges_of(chunk_ref, q_ref, i):
-    return jnp.concatenate([q_ref[chunk_ref[2 * i + k]] for k in range(2)], 1)
-
-
-def multiply(chunk_ref, q_ref, acc_ref, i, hi_ref, lo_ref, j):
-    q = charges_of(chunk_ref, q_ref, i)
+    charge_blocks(lambda k: jnp.concatenate([recv_ref[3 * k], recv_ref[3 * k + 1]], 0), ih_ref, il_ref, far_ref, q_ref, wide_ref)
+
+
+def multiply_tile(chunk_ref, q_ref, acc_ref, i, hi_ref, lo_ref, j, t):
+    q = jnp.concatenate([q_ref[chunk_ref[2 * i + k]] for k in range(2)], 1)
     rows = pl.ds(pl.multiple_of(chunk_ref[CHUNK_OWNER + i] * 16, 16), 16)
-    part = jnp.dot(q, hi_ref[j], preferred_element_type=f32) + jnp.dot(q, lo_ref[j], preferred_element_type=f32)
-    acc_ref[rows] = acc_ref[rows] + part
+    cols = slice(t * TILE, (t + 1) * TILE)
+    both = jnp.concatenate([hi_ref[j, t], lo_ref[j, t]], 0)
+    acc_ref[rows, cols] = acc_ref[rows, cols] + jnp.dot(jnp.concatenate([q, q], 1), both, preferred_element_type=f32)
 
 
 def write_sums(acc_ref, out_ref):
@@ -282,24 +272,33 @@
     acc_ref[...] = jnp.zeros_like(acc_ref)
     count = count_ref[0]
 
-    def evaluate(i, hi_ref, lo_ref, j):
+    def rows_of(i):
         blocks = [chunk_ref[2 * i + k] for k in range(2)]
         starts = [pl.multiple_of(jnp.where(n == ZERO_BLOCK, 0, n) * 128, 128) for n in blocks]
-        a = jnp.concatenate([a_ref[pl.ds(n, 128), :DEPTH] for n in starts], 0)
-        square = jnp.dot(a, b_ref[chunk_ref[CHUNK_OWNER + i]], preferred_element_type=f32)
+        return jnp.concatenate([a_ref[pl.ds(n, 128), :DEPTH] for n in starts], 0), chunk_ref[CHUNK_OWNER + i]
+
+    def evaluate_tile(rows, hi_ref, lo_ref, j, t):
+        square = jnp.dot(rows[0], b_ref[rows[1], :, t * TILE : (t + 1) * TILE], preferred_element_type=f32)
         hi, lo = split2(lax.rsqrt(square))
-        hi_ref[j] = hi
-        lo_ref[j] = lo
+        hi_ref[j, t] = hi
+        lo_ref[j, t] = lo
 
     even, odd = (eh_ref, el_ref), (oh_ref, ol_ref)
-    mul = functools.partial(multiply, chunk_ref, q_ref, acc_ref)
-    evaluate(0, *even, 0)
+    mul = functools.partial(multiply_tile, chunk_ref, q_ref, acc_ref)
+
+    def both(done, source, js, new, target, jt):
+        rows = rows_of(new)
+        for t in range(TILES):
+            mul(done, *source, js, t)
+            evaluate_tile(rows, *target, jt, t)
+
+    rows = rows_of(0)
+    for t in range(TILES):
+        evaluate_tile(rows, *even, 0, t)
 
     def pair(j, carry):
-        evaluate(2 * j + 1, *odd, j)
-        mul(2 * j, *even, j)
-        evaluate(2 * j + 2, *even, j + 1)
-        mul(2 * j + 1, *odd, j)
+        both(2 * j, even, j, 2 * j + 1, odd, j)
+        both(2 * j + 1, odd, j, 2 * j + 2, even, j + 1)
         return carry
 
     pairs = (count - 1) >> 1
@@ -307,33 +306,44 @@
 
     @pl.when((count & 1) == 0)
     def _():
-        evaluate(2 * pairs + 1, *odd, pairs)
-        mul(2 * pairs, *even, pairs)
-        mul(2 * pairs + 1, *odd, pairs)
+        both(2 * pairs, even, pairs, 2 * pairs + 1, odd, pairs)
+        for t in range(TILES):
+            mul(2 * pairs + 1, *odd, pairs, t)
 
     @pl.when((count & 1) == 1)
     def _():
-        mul(2 * pairs, *even, pairs)
+        for t in range(TILES):
+            mul(2 * pairs, *even, pairs, t)
 
     write_sums(acc_ref, out_ref)
 
 
 def second_kernel(chunk_ref, count_ref, far_ref, recv_ref, ih_ref, il_ref, eh_ref, el_ref, oh_ref, ol_ref, out_ref, q_ref, wide_ref, acc_ref):
-    charge_blocks(recv_ref, ih_ref, il_ref, far_ref, q_ref, wide_ref)
+    charge_blocks(lambda k: recv_ref[k], ih_ref, il_ref, far_ref, q_ref, wide_ref)
     acc_ref[...] = jnp.zeros_like(acc_ref)
     count = count_ref[0]
-    mul = functools.partial(multiply, chunk_ref, q_ref, acc_ref)
-
-    def pair(j, carry):
-        mul(2 * j, eh_ref, el_ref, j)
-        mul(2 * j + 1, oh_ref, ol_ref, j)
+    mul = functools.partial(multiply_tile, chunk_ref, q_ref, acc_ref)
+
+    def pair(j):
+        for t in range(TILES):
+            mul(2 * j, eh_ref, el_ref, j, t)
+            mul(2 * j + 1, oh_ref, ol_ref, j, t)
+
+    def four(j, carry):
+        pair(2 * j)
+        pair(2 * j + 1)
         return carry
 
-    lax.fori_loop(0, count >> 1, pair, 0)
+    lax.fori_loop(0, count >> 2, four, 0)
+
+    @pl.when((count & 2) == 2)
+    def _():
+        pair((count >> 2) * 2)
 
     @pl.when((count & 1) == 1)
     def _():
-        mul(count - 1, eh_ref, el_ref, count >> 1)
+        for t in range(TILES):
+            mul(count - 1, eh_ref, el_ref, count >> 1, t)
 
     write_sums(acc_ref, out_ref)
 
@@ -370,13 +380,13 @@
     charges, source_coords, boundary_data, target_points = map(hbm, (charges, source_coords, boundary_data, target_points))
     zsend, current = pl.pallas_call(
         prologue_kernel,
-        out_shape=(sds((NZ, 16, 128)), sds((8, 128))),
-        in_specs=[SM, HB, HB, HB],
+        out_shape=(sds((3 * NZ, 4, 128)), sds((8, 128))),
+        in_specs=[SM, HB, HB],
         out_specs=(VM, VM),
-        scratch_shapes=[pltpu.VMEM((3, 128), f32), pltpu.SMEM((3, NZ * NY * MEMBERS), f32), pltpu.SemaphoreType.DMA((3,))],
+        scratch_shapes=[pltpu.VMEM((3, 128), f32), pltpu.SemaphoreType.DMA((2,))],
         compiler_params=small,
         name="prologue",
-    )(valid_count, hbm(leaf_centers), charges, source_coords)
+    )(valid_count, charges, source_coords)
     recv = lax.all_to_all(zsend, "z", 0, 0, tiled=True)
     tsend, held, far, chunks, count, proxies = pl.pallas_call(
         prep_kernel,
@@ -406,15 +416,15 @@
     a, ih, il, q = pl.pallas_call(
         setup_kernel,
         out_shape=(sds((ZERO_BLOCK * 128, 128), bf16), interp, interp, sds((ZERO_BLOCK + 1, 16, 128), bf16)),
-        in_specs=[SM, VM, VM],
+        in_specs=[SM, SM, VM, VM],
         out_specs=(VM,) * 4,
         scratch_shapes=[pltpu.VMEM((5, 16, 128), f32)],
         compiler_params=params,
         cost_estimate=pl.CostEstimate(flops=10**9, bytes_accessed=8 * 10**6, transcendentals=0),
         name="setup",
-    )(far, recv, proxies)
+    )(far, leaf_centers, recv, proxies)
     scale = 1.0 / math.sqrt(NY * NZ * MEMBERS * 128)
-    half = pltpu.VMEM((PAIRS, 256, MEMBERS * 128), bf16)
+    half = pltpu.VMEM((PAIRS, TILES, 256, TILE), bf16)
     sums, *kernels = pl.pallas_call(
         first_kernel,
         out_shape=(sds((PLANE, 8, 128)), half, half, half, half),

time: 105 us -> 101 us (0.962)
  Pallas kernels: 21.3 us -> 17.9 us
    pallas_call x1, Pallas kernels: 6.19 us -> 4.81 us  [body(): pl.pallas_call(second_kernel, out_shape=sds((PLANE, 8, 128)), in_specs=[S...]
    pallas_call x1, Pallas kernels: 8.19 us -> 6.88 us  [body(): pl.pallas_call(first_kernel, out_shape=(sds((PLANE, 8, 128)), half, half,...]
    unnamed x6 -> x8, local copies, waits for them, and re-layouts: 2.06 us -> 2.76 us
where the time goes in v5:
time: 101 us; the launch traced here: 100 us
  blocking collectives  40.4 us (40%)
  starting transfers between devices  25.6 us (25%)
  Pallas kernels  17.9 us (18%)
  waiting for transfers between devices  12.5 us (12%)
  local copies, waits for them, and re-layouts  2.76 us (3%)
  between operations  1.35 us (1%)
    all_to_all x2, blocking collectives, update(): lax.all_to_all(sums, plane, 0, 0, tiled=True)  24.9 us
    all_to_all x1, starting transfers between devices, body(): recv = lax.all_to_all(zsend, 'z', 0, 0, tiled=True)  15.7 us
    all_to_all x1, blocking collectives, body(): recv = lax.all_to_all(zsend, 'z', 0, 0, tiled=True)  15.5 us
    all_to_all x1, starting transfers between devices, body(): targets = lax.all_to_all(tsend, plane, 0, 0, tiled=True)  9.84 us
    all_to_all x1, waiting for transfers between devices, body(): recv = lax.all_to_all(zsend, 'z', 0, 0, tiled=True)  7.04 us
    pallas_call x1, Pallas kernels, body(): pl.pallas_call(first_kernel, out_shape=(sds((PLANE, 8, 128)), half, half,...  6.88 us
    all_to_all x1, waiting for transfers between devices, body(): targets = lax.all_to_all(tsend, plane, 0, 0, tiled=True)  5.45 us
    pallas_call x1, Pallas kernels, body(): pl.pallas_call(second_kernel, out_shape=sds((PLANE, 8, 128)), in_specs=[S...  4.81 us
  transfers between devices with their start and end apart: 2, of which 2 were waited for; matrix products, arithmetic and copies ran while one was open for 0% of the time, Pallas kernels for 4%

profile of v5, /device:TPU:1, one launch (start us, length us, event | category | flops | bytes accessed | tf_op | source)
XLA Modules:
  0.0 100.4 jit_solution(1422338173719864095)
XLA Ops:
  1.3 1.4 %prologue.1 = (f32[48,4,128]{2,1,0:T(4,128)}, f32[8,128]{1,0:T(8,128)S(1)}) custom-call(s32[1]{0:T(128)S(6)} %copy.10.count_ref, f32[8,128]{1,0:T(8,128)} %charges_hbm.1, f32[3,128]{1,0:T(4,128)} %coords_hbm.1), custom_call_target="tpu_custom_call" | custom-call | tf_op jit(solution)/shard_map/prologue/pallas_call | solution.py:381
  2.7 15.7 %all-to-all-start = ((f32[48,4,128]{2,1,0:T(4,128)}), f32[48,4,128]{2,1,0:T(4,128)S(1)}, u32[]{:S(2)}, u32[]{:S(2)}) async-start(f32[48,4,128]{2,1,0:T(4,128)} %get-tuple-element.26), calls=%async_computation | async-start | bytes 196608 | tf_op jit(solution)/shard_map/all_to_all | solution.py:390
  18.4 0.0 copy-start
  18.4 0.7 copy-done
  19.1 0.0 copy-start.1
  19.1 0.7 copy-done.1
  19.8 0.0 copy-start.3
  19.8 0.7 copy-done.3
  20.5 2.7 %prep.1 = (f32[32,8,128]{2,1,0:T(8,128)}, f32[3,8,128]{2,1,0:T(8,128)S(1)}, s32[4,32]{1,0:T(4,128)S(1)}, s32[128]{0:T(128)S(1)}, s32[1]{0:T(128)}, /*index=5*/bf16[2048,128]{1,0:T(8,128)(2,1)S(1)}) custom-call(f32[3,512]{1,0:T(4,128)S(1)} %copy-done.1, s32[26,64]{1,0:T(8,128)S(1)} %bitcast.1, s32[1]{0:T(128)S(6)} %copy.10.count_ref, f32[8]{0:T(128)S(1)} %copy-done.3, ...), custom_call_target="tpu_custom_call" | custom-call | flops 1000000000 | bytes 12000000 | tf_op jit(solution)/shard_map/prep/pallas_call | solution.py:391
  23.2 7.0 %all-to-all-done.recv_ref = f32[48,4,128]{2,1,0:T(4,128)S(1)} async-done(((f32[48,4,128]{2,1,0:T(4,128)}), f32[48,4,128]{2,1,0:T(4,128)S(1)}, u32[]{:S(2)}, u32[]{:S(2)}) %all-to-all-start) | async-done | bytes 98336 | tf_op jit(solution)/shard_map/all_to_all | solution.py:390
  30.3 9.8 %all-to-all-start.1 = ((f32[32,8,128]{2,1,0:T(8,128)}), f32[32,8,128]{2,1,0:T(8,128)S(1)}, u32[]{:S(2)}, u32[]{:S(2)}) async-start(f32[32,8,128]{2,1,0:T(8,128)} %get-tuple-element.28), calls=%async_computation.1 | async-start | bytes 262144 | tf_op jit(solution)/shard_map/all_to_all | solution.py:414
  40.1 0.0 copy-start.2
  40.1 0.7 copy-done.2
  40.8 1.4 %setup.1 = (bf16[4096,128]{1,0:T(8,128)(2,1)S(1)}, bf16[512,128]{1,0:T(8,128)(2,1)S(1)}, bf16[512,128]{1,0:T(8,128)(2,1)S(1)}, bf16[33,16,128]{2,1,0:T(8,128)(2,1)S(1)}) custom-call(s32[4,32]{1,0:T(4,128)S(1)} %get-tuple-element.25.far_ref, f32[3,512]{1,0:T(4,128)S(1)} %copy-done.2, f32[48,4,128]{2,1,0:T(4,128)S(1)} %all-to-all-done.recv_ref, ...), custom_call_target="tpu_custom_call" | custom-call | flops 1000000000 | bytes 8000000 | tf_op jit(solution)/shard_map/setup/pallas_call | solution.py:416
  42.3 5.5 %all-to-all-done.1.tgt_ref = f32[32,8,128]{2,1,0:T(8,128)S(1)} async-done(((f32[32,8,128]{2,1,0:T(8,128)}), f32[32,8,128]{2,1,0:T(8,128)S(1)}, u32[]{:S(2)}, u32[]{:S(2)}) %all-to-all-start.1) | async-done | bytes 131104 | tf_op jit(solution)/shard_map/all_to_all | solution.py:414
  47.7 6.9 %first.1 = (f32[32,8,128]{2,1,0:T(8,128)S(1)}, bf16[17,4,256,256]{3,2,1,0:T(8,128)(2,1)S(1)}, bf16[17,4,256,256]{3,2,1,0:T(8,128)(2,1)S(1)}, bf16[17,4,256,256]{...) custom-call(s32[128]{0:T(128)S(1)} %get-tuple-element.23.chunk_ref, s32[1]{0:T(128)} %get-tuple-element.24.count_ref, ...), custom_call_target="tpu_custom_call" | custom-call | tf_op jit(solution)/shard_map/first/pallas_call | solution.py:428
  54.6 11.7 %all_to_all.25.recv_ref = f32[32,8,128]{2,1,0:T(8,128)S(1)} all-to-all(f32[32,8,128]{2,1,0:T(8,128)S(1)} %get-tuple-element.33), channel_id=1, replica_groups=mesh['y'=4,'z'=16,'x'=4,'core'=2] {'y','x','core'}, dimensions={0} | all-to-all | bytes 262144 | tf_op jit(solution)/shard_map/all_to_all | solution.py:446
  66.3 15.5 %all_to_all.26.recv_ref = f32[16,8,128]{2,1,0:T(8,128)S(1)} all-to-all(f32[16,8,128]{2,1,0:T(8,128)S(1)} %get-tuple-element.36), channel_id=1, replica_groups=mesh['y'=4,'z'=16,'x'=4,'core'=2] {'z'}, dimensions={0} | all-to-all | bytes 131072 | tf_op jit(solution)/shard_map/all_to_all | solution.py:449
  81.8 4.8 %second.1 = f32[32,8,128]{2,1,0:T(8,128)S(1)} custom-call(s32[128]{0:T(128)S(1)} %get-tuple-element.23.chunk_ref, s32[1]{0:T(128)} %get-tuple-element.24.count_ref, s32[4,32]{1,0:T(4,128)S(1)} %get-tuple-element.25.far_ref, f32[16,8,128]{2,1,0:T(8,128)S(1)} %all_to_all.26.recv_ref, bf16[512,128]{1,0:T(8,128)(2,1)S(1)} %get-tuple-element.37.ih_ref, ...), custom_call_target="tpu_custom_call" | custom-call | tf_op jit(solution)/shard_map/second/pallas_call | solution.py:450
  86.6 13.2 %all_to_all.27.recv_ref = f32[32,8,128]{2,1,0:T(8,128)S(1)} all-to-all(f32[32,8,128]{2,1,0:T(8,128)S(1)} %second.1), channel_id=1, replica_groups=mesh['y'=4,'z'=16,'x'=4,'core'=2] {'y','x','core'}, dimensions={0} | all-to-all | bytes 262144 | tf_op jit(solution)/shard_map/all_to_all | solution.py:446
  99.8 0.6 update.3
  (1 shorter events, 0.0 us)
Async XLA Ops:
  2.7 27.6 %all-to-all-start = ((f32[48,4,128]{2,1,0:T(4,128)}), f32[48,4,128]{2,1,0:T(4,128)S(1)}, u32[]{:S(2)}, u32[]{:S(2)}) async-start(f32[48,4,128]{2,1,0:T(4,128)} %get-tuple-element.26), calls=%async_computation | async-start | bytes 196608 | tf_op jit(solution)/shard_map/all_to_all | solution.py:390
  18.4 0.7 copy-start
  19.1 0.7 copy-start.1
  19.8 0.7 copy-start.3
  30.3 17.4 %all-to-all-start.1 = ((f32[32,8,128]{2,1,0:T(8,128)}), f32[32,8,128]{2,1,0:T(8,128)S(1)}, u32[]{:S(2)}, u32[]{:S(2)}) async-start(f32[32,8,128]{2,1,0:T(8,128)} %get-tuple-element.28), calls=%async_computation.1 | async-start | bytes 262144 | tf_op jit(solution)/shard_map/all_to_all | solution.py:414
  40.1 0.7 copy-start.2

commit v6 on v5

--- a/solution.py
+++ b/solution.py
@@ -19,7 +19,7 @@
 DEPTH = 48
 FAR = NZ
 ZERO_BLOCK = FAR + 4 * NY
-FAR_SLOTS = 32
+FAR_SLOTS = 16
 CHUNK_OWNER = 80
 CHUNK_SLOTS = 128
 PAIRS = 17
@@ -98,39 +98,30 @@
     return tables
 
 
-def make_lists(y, z, near_ref, far_ref, chunk_ref, count_ref, mine_ref):
+def make_lists(y, z, near_ref, far_ref, chunk_ref, count_ref):
     total = jnp.int32(0)
     for other in range(NY):
-        for k in range(NZ):
-            mine_ref[k] = 0
-            far_ref[other, k] = NZ
-        mine_ref[z] = (y == other).astype(jnp.int32)
+        bits = jnp.where(y == other, 1 << z, 0)
         for j in range(NEAR):
             cluster = near_ref[j, other * NZ + z]
-            mine_ref[jnp.where((cluster >> 4) == y, cluster & 15, NZ)] = 1
+            bits = bits | jnp.where((cluster >> 4) == y, 1 << (cluster & 15), 0)
         near_count = jnp.int32(0)
-        far_count = jnp.int32(0)
         for k in range(NZ):
-            mine = mine_ref[k]
+            far_ref[other, k] = NZ
+        for k in range(NZ):
+            mine = (bits >> k) & 1
             chunk_ref[total + near_count] = k
-            far_ref[other, far_count] = jnp.where(mine > 0, NZ, k)
+            far_ref[other, k - near_count] = jnp.where(mine > 0, NZ, k)
             near_count = near_count + mine
-            far_count = far_count + 1 - mine
-        far_blocks = (far_count + 3) // 4
+        far_blocks = (NZ + 3 - near_count) >> 2
         start = total + near_count
         for k in range(4):
             chunk_ref[start + k] = FAR + other * 4 + k
         end = start + far_blocks
         chunk_ref[end] = ZERO_BLOCK
-        far_ref[other, FAR_SLOTS - 1] = far_blocks
-        rounded = ((end + 1) >> 1) << 1
-
-        def owner(k, carry):
-            chunk_ref[CHUNK_OWNER + k] = other
-            return carry
-
-        lax.fori_loop(total >> 1, rounded >> 1, owner, 0)
-        total = rounded
+        for k in range(8):
+            chunk_ref[CHUNK_OWNER + (total >> 1) + k] = other
+        total = ((end + 1) >> 1) << 1
     count_ref[0] = total >> 1
 
 
@@ -150,54 +141,43 @@
 
 
 def prep_kernel(
-    centers_ref, near_ref, count_ref, steps_ref, boundary_hbm, targets_hbm,
-    tsend_ref, held_ref, far_ref, chunk_ref, chunks_ref, proxy_ref,
-    mine_ref, wide_ref, targets_ref, sem,
+    count_ref, steps_ref, centers_hbm, near_hbm, boundary_hbm, targets_hbm,
+    tsend_ref, held_ref, near_ref, center_ref, proxy_ref,
+    centers_ref, targets_ref, sem,
 ):
-    y, z, member = here()
-    copies = [
-        pltpu.make_async_copy(boundary_hbm, held_ref.at[0], sem.at[0]),
-        pltpu.make_async_copy(targets_hbm, targets_ref, sem.at[1]),
-    ]
+    y, _, member = here()
+    moves = ((targets_hbm, targets_ref), (centers_hbm, centers_ref), (boundary_hbm, held_ref.at[0]), (near_hbm, near_ref))
+    copies = [pltpu.make_async_copy(source, target, sem.at[k]) for k, (source, target) in enumerate(moves)]
     for copy in copies:
         copy.start()
-    make_lists(y, z, near_ref, far_ref, chunk_ref, chunks_ref, mine_ref)
-    for copy in copies:
-        copy.wait()
-    rows = target_rows(jnp.concatenate([targets_ref[...], jnp.zeros((5, 128), f32)], 0))
-    for k in range(PLANE):
-        tsend_ref[k] = rows
     lane = iota((8, 128), 1)
     row = iota((8, 128), 0)
-    steps = jnp.zeros((8, 128), f32)
-    for k in range(8):
-        steps = jnp.where(row == k, steps_ref[k], steps)
-    held_ref[1] = steps
-    held_ref[2] = (lane < count_ref[0]).astype(f32)
     p = lane & 31
     offset = jnp.where(
         row == 0,
         pick(p >> 4, cheby_nodes(2)),
         jnp.where(row == 1, pick((p >> 2) & 3, cheby_nodes(4)), jnp.where(row == 2, pick(p & 3, cheby_nodes(4)), 0.0)),
     )
+    steps = jnp.zeros((8, 128), f32)
+    for k in range(8):
+        steps = jnp.where(row == k, steps_ref[k], steps)
+    held_ref[1] = steps
+    held_ref[2] = (lane < count_ref[0]).astype(f32)
+    for copy in copies:
+        copy.wait()
+    rows = target_rows(jnp.concatenate([targets_ref[...], jnp.zeros((5, 128), f32)], 0))
+    for k in range(PLANE):
+        tsend_ref[k] = rows
     for block in range(4):
         center = jnp.zeros((8, 128), f32)
         for k in range(4):
             leaf = (y * NZ + block * 4 + k) * MEMBERS + member
             column = column3(centers_ref[0, leaf], centers_ref[1, leaf], centers_ref[2, leaf], (8, 128))
+            center_ref[block * 4 + k] = column
             center = jnp.where((lane >> 5) == k, column, center)
         rows = source_rows(center + HALF_SIDE * offset)
-        wide_ref[block * 128 : (block + 1) * 128, :DEPTH] = a_block(rows)
-    wide_ref[512:544, :DEPTH] = wide_ref[0:32, :DEPTH]
-    for other in range(NY):
-        for block in range(4):
-
-            @pl.when(block < far_ref[other, FAR_SLOTS - 1])
-            def _(other=other, block=block):
-                for k in range(4):
-                    leaf = far_ref[other, block * 4 + k]
-                    base = (other * 4 + block) * 128 + k * 32
-                    proxy_ref[base : base + 32] = wide_ref[pl.ds(pl.multiple_of(leaf * 32, 32), 32)]
+        proxy_ref[block * 128 : (block + 1) * 128, :DEPTH] = a_block(rows)
+    proxy_ref[512:544, :DEPTH] = proxy_ref[0:32, :DEPTH]
 
 
 def charge_blocks(charges, ih_ref, il_ref, far_ref, q_ref, wide_ref):
@@ -227,14 +207,15 @@
             q_ref[FAR + other * 4 + block] = out.astype(bf16)
 
 
-def setup_kernel(far_ref, centers_ref, recv_ref, proxy_ref, a_ref, ih_ref, il_ref, q_ref, wide_ref):
+def setup_kernel(
+    near_ref, center_ref, recv_ref, proxy_ref, a_ref, ih_ref, il_ref, q_ref, far_ref, chunk_ref, count_ref, wide_ref
+):
+    y, z, _ = here()
+    make_lists(y, z, near_ref, far_ref, chunk_ref, count_ref)
     tables = interp_tables()
-    y, _, member = here()
     for k in range(NZ):
         rows = recv_ref[3 * k + 2]
-        leaf = (y * NZ + k) * MEMBERS + member
-        center = column3(centers_ref[0, leaf], centers_ref[1, leaf], centers_ref[2, leaf], (8, 128))
-        points = center + HALF_SIDE * jnp.concatenate([rows, jnp.zeros((4, 128), f32)], 0)
+        points = center_ref[k] + HALF_SIDE * jnp.concatenate([rows, jnp.zeros((4, 128), f32)], 0)
         a_ref[k * 128 : (k + 1) * 128, :DEPTH] = a_block(source_rows(points))
         value = None
         for axis, (roots, scale) in enumerate(tables):
@@ -246,7 +227,10 @@
         hi, lo = split2(value)
         ih_ref[k * 32 : (k + 1) * 32] = hi
         il_ref[k * 32 : (k + 1) * 32] = lo
-    a_ref[FAR * 128 :] = proxy_ref[...]
+    for other in range(NY):
+        for k in range(NZ):
+            base = (FAR + other * 4) * 128 + k * 32
+            a_ref[base : base + 32] = proxy_ref[pl.ds(pl.multiple_of(far_ref[other, k] * 32, 32), 32)]
     charge_blocks(lambda k: jnp.concatenate([recv_ref[3 * k], recv_ref[3 * k + 1]], 0), ih_ref, il_ref, far_ref, q_ref, wide_ref)
 
 
@@ -388,41 +372,43 @@
         name="prologue",
     )(valid_count, charges, source_coords)
     recv = lax.all_to_all(zsend, "z", 0, 0, tiled=True)
-    tsend, held, far, chunks, count, proxies = pl.pallas_call(
+    tsend, held, near, centers, proxies = pl.pallas_call(
         prep_kernel,
         out_shape=(
             sds((PLANE, 8, 128)),
             sds((3, 8, 128)),
+            sds((NEAR, NY * NZ), jnp.int32),
+            sds((NZ, 8, 128)),
+            sds((544, 128), bf16),
+        ),
+        in_specs=[SM, SM, HB, HB, HB, HB],
+        out_specs=(VM,) * 5,
+        scratch_shapes=[pltpu.SMEM((3, NZ * NY * MEMBERS), f32), pltpu.VMEM((3, 128), f32), pltpu.SemaphoreType.DMA((4,))],
+        compiler_params=small,
+        cost_estimate=pl.CostEstimate(flops=10**9, bytes_accessed=12 * 10**6, transcendentals=0),
+        name="prep",
+    )(valid_count, step_sizes, hbm(leaf_centers), hbm(near_lists.T), boundary_data, target_points)
+    recv, tsend = lax.optimization_barrier((recv, tsend))
+    targets = lax.all_to_all(tsend, plane, 0, 0, tiled=True)
+    interp = sds((NZ * 32, 128), bf16)
+    a, ih, il, q, far, chunks, count = pl.pallas_call(
+        setup_kernel,
+        out_shape=(
+            sds((ZERO_BLOCK * 128, 128), bf16),
+            interp,
+            interp,
+            sds((ZERO_BLOCK + 1, 16, 128), bf16),
             sds((NY, FAR_SLOTS), jnp.int32),
             sds((CHUNK_SLOTS,), jnp.int32),
             sds((1,), jnp.int32),
-            sds((4 * NY * 128, 128), bf16),
         ),
-        in_specs=[SM, SM, SM, SM, HB, HB],
-        out_specs=(VM, VM, SM, SM, SM, VM),
-        scratch_shapes=[
-            pltpu.SMEM((NZ + 1,), jnp.int32),
-            pltpu.VMEM((544, 128), bf16),
-            pltpu.VMEM((3, 128), f32),
-            pltpu.SemaphoreType.DMA((2,)),
-        ],
-        compiler_params=small,
-        cost_estimate=pl.CostEstimate(flops=10**9, bytes_accessed=12 * 10**6, transcendentals=0),
-        name="prep",
-    )(leaf_centers, near_lists.T, valid_count, step_sizes, boundary_data, target_points)
-    recv, tsend = lax.optimization_barrier((recv, tsend))
-    targets = lax.all_to_all(tsend, plane, 0, 0, tiled=True)
-    interp = sds((NZ * 32, 128), bf16)
-    a, ih, il, q = pl.pallas_call(
-        setup_kernel,
-        out_shape=(sds((ZERO_BLOCK * 128, 128), bf16), interp, interp, sds((ZERO_BLOCK + 1, 16, 128), bf16)),
-        in_specs=[SM, SM, VM, VM],
-        out_specs=(VM,) * 4,
+        in_specs=[SM, VM, VM, VM],
+        out_specs=(VM,) * 4 + (SM,) * 3,
         scratch_shapes=[pltpu.VMEM((5, 16, 128), f32)],
         compiler_params=params,
         cost_estimate=pl.CostEstimate(flops=10**9, bytes_accessed=8 * 10**6, transcendentals=0),
         name="setup",
-    )(far, leaf_centers, recv, proxies)
+    )(near, centers, recv, proxies)
     scale = 1.0 / math.sqrt(NY * NZ * MEMBERS * 128)
     half = pltpu.VMEM((PAIRS, TILES, 256, TILE), bf16)
     sums, *kernels = pl.pallas_call(

time: 101 us -> 101 us (level)
  local copies, waits for them, and re-layouts: 2.76 us -> 0.65 us
  waiting for transfers between devices: 12.5 us -> 14 us
  Pallas kernels: 17.9 us -> 19.1 us
    unnamed x8 -> x2, local copies, waits for them, and re-layouts: 2.76 us -> 0.65 us
    all_to_all x1, waiting for transfers between devices: 7.04 us -> 8.98 us  [body(): recv = lax.all_to_all(zsend, 'z', 0, 0, tiled=True)]
    pallas_call x1, Pallas kernels: 1.44 us -> 2.59 us  [body(): pl.pallas_call(setup_kernel, out_shape=(sds((ZERO_BLOCK * 128, 128), bf16...]
  transfers between devices with their start and end apart: 2 -> 2, of which waited for: 2 -> 2; matrix products, arithmetic and copies ran while one was open for 0% -> 0% of each run, Pallas kernels for 4% -> 5%
where the time goes in v6:
time: 101 us
  blocking collectives  40 us (40%)
  starting transfers between devices  25.6 us (25%)
  Pallas kernels  19.1 us (19%)
  waiting for transfers between devices  14 us (14%)
  between operations  1.34 us (1%)
    all_to_all x2, blocking collectives, update(): lax.all_to_all(sums, plane, 0, 0, tiled=True)  25.3 us
    all_to_all x1, starting transfers between devices, body(): recv = lax.all_to_all(zsend, 'z', 0, 0, tiled=True)  15.7 us
    all_to_all x1, blocking collectives, body(): recv = lax.all_to_all(zsend, 'z', 0, 0, tiled=True)  14.7 us
    all_to_all x1, starting transfers between devices, body(): targets = lax.all_to_all(tsend, plane, 0, 0, tiled=True)  9.84 us
    all_to_all x1, waiting for transfers between devices, body(): recv = lax.all_to_all(zsend, 'z', 0, 0, tiled=True)  8.98 us
    pallas_call x1, Pallas kernels, body(): pl.pallas_call(first_kernel, out_shape=(sds((PLANE, 8, 128)), half, half,...  7.21 us
    pallas_call x1, Pallas kernels, body(): pl.pallas_call(second_kernel, out_shape=sds((PLANE, 8, 128)), in_specs=[S...  5.07 us
    all_to_all x1, waiting for transfers between devices, body(): targets = lax.all_to_all(tsend, plane, 0, 0, tiled=True)  5.01 us
  transfers between devices with their start and end apart: 2, of which 2 were waited for; matrix products, arithmetic and copies ran while one was open for 0% of the time, Pallas kernels for 5%

profile of v6, /device:TPU:1, one launch (start us, length us, event | category | flops | bytes accessed | tf_op | source)
XLA Modules:
  0.0 100.7 jit_solution(13037904178011107593)
XLA Ops:
  1.3 1.4 %prologue.1 = (f32[48,4,128]{2,1,0:T(4,128)}, f32[8,128]{1,0:T(8,128)S(1)}) custom-call(s32[1]{0:T(128)S(6)} %copy.10.count_ref, f32[8,128]{1,0:T(8,128)} %charges_hbm.1, f32[3,128]{1,0:T(4,128)} %coords_hbm.1), custom_call_target="tpu_custom_call" | custom-call | tf_op jit(solution)/shard_map/prologue/pallas_call | solution.py:365
  2.7 15.7 %all-to-all-start = ((f32[48,4,128]{2,1,0:T(4,128)}), f32[48,4,128]{2,1,0:T(4,128)S(1)}, u32[]{:S(2)}, u32[]{:S(2)}) async-start(f32[48,4,128]{2,1,0:T(4,128)} %get-tuple-element.27), calls=%async_computation | async-start | bytes 196608 | tf_op jit(solution)/shard_map/all_to_all | solution.py:374
  18.4 0.0 copy-start
  18.4 0.6 copy-done
  19.1 2.2 %prep.1 = (f32[32,8,128]{2,1,0:T(8,128)}, f32[3,8,128]{2,1,0:T(8,128)S(1)}, s32[26,64]{1,0:T(8,128)S(1)}, f32[16,8,128]{2,1,0:T(8,128)S(1)}, bf16[544,128]{1,0:T(8,128)(2,1)S(1)}) custom-call(s32[1]{0:T(128)S(6)} %copy.10.count_ref, f32[8]{0:T(128)S(1)} %copy-done, f32[3,512]{1,0:T(4,128)} %centers_hbm.1, s32[26,64]{1,0:T(8,128)} %bitcast.1, ...), custom_call_target="tpu_custom_call" | custom-call | flops 1000000000 | bytes 12000000 | tf_op jit(solution)/shard_map/prep/pallas_call | solution.py:375
  21.3 9.0 %all-to-all-done.recv_ref = f32[48,4,128]{2,1,0:T(4,128)S(1)} async-done(((f32[48,4,128]{2,1,0:T(4,128)}), f32[48,4,128]{2,1,0:T(4,128)S(1)}, u32[]{:S(2)}, u32[]{:S(2)}) %all-to-all-start) | async-done | bytes 98336 | tf_op jit(solution)/shard_map/all_to_all | solution.py:374
  30.3 9.8 %all-to-all-start.1 = ((f32[32,8,128]{2,1,0:T(8,128)}), f32[32,8,128]{2,1,0:T(8,128)S(1)}, u32[]{:S(2)}, u32[]{:S(2)}) async-start(f32[32,8,128]{2,1,0:T(8,128)} %get-tuple-element.34), calls=%async_computation.1 | async-start | bytes 262144 | tf_op jit(solution)/shard_map/all_to_all | solution.py:392
  40.1 2.6 %setup.1 = (bf16[4096,128]{1,0:T(8,128)(2,1)S(1)}, bf16[512,128]{1,0:T(8,128)(2,1)S(1)}, bf16[512,128]{1,0:T(8,128)(2,1)S(1)}, bf16[33,16,128]{2,1,0:T(8,128)(2,...) custom-call(s32[26,64]{1,0:T(8,128)S(1)} %get-tuple-element.25.near_ref, ...), custom_call_target="tpu_custom_call" | custom-call | flops 1000000000 | bytes 8000000 | tf_op jit(solution)/shard_map/setup/pallas_call | solution.py:394
  42.7 5.0 %all-to-all-done.1.tgt_ref = f32[32,8,128]{2,1,0:T(8,128)S(1)} async-done(((f32[32,8,128]{2,1,0:T(8,128)}), f32[32,8,128]{2,1,0:T(8,128)S(1)}, u32[]{:S(2)}, u32[]{:S(2)}) %all-to-all-start.1) | async-done | bytes 131104 | tf_op jit(solution)/shard_map/all_to_all | solution.py:392
  47.7 7.2 %first.1 = (f32[32,8,128]{2,1,0:T(8,128)S(1)}, bf16[17,4,256,256]{3,2,1,0:T(8,128)(2,1)S(1)}, bf16[17,4,256,256]{3,2,1,0:T(8,128)(2,1)S(1)}, bf16[17,4,256,256]{...) custom-call(s32[128]{0:T(128)S(1)} %get-tuple-element.31.chunk_ref, s32[1]{0:T(128)} %get-tuple-element.32.count_ref, ...), custom_call_target="tpu_custom_call" | custom-call | tf_op jit(solution)/shard_map/first/pallas_call | solution.py:414
  54.9 12.1 %all_to_all.25.recv_ref = f32[32,8,128]{2,1,0:T(8,128)S(1)} all-to-all(f32[32,8,128]{2,1,0:T(8,128)S(1)} %get-tuple-element.37), channel_id=1, replica_groups=mesh['y'=4,'z'=16,'x'=4,'core'=2] {'y','x','core'}, dimensions={0} | all-to-all | bytes 262144 | tf_op jit(solution)/shard_map/all_to_all | solution.py:432
  67.1 14.7 %all_to_all.26.recv_ref = f32[16,8,128]{2,1,0:T(8,128)S(1)} all-to-all(f32[16,8,128]{2,1,0:T(8,128)S(1)} %get-tuple-element.40), channel_id=1, replica_groups=mesh['y'=4,'z'=16,'x'=4,'core'=2] {'z'}, dimensions={0} | all-to-all | bytes 131072 | tf_op jit(solution)/shard_map/all_to_all | solution.py:435
  81.8 5.1 %second.1 = f32[32,8,128]{2,1,0:T(8,128)S(1)} custom-call(s32[128]{0:T(128)S(1)} %get-tuple-element.31.chunk_ref, s32[1]{0:T(128)} %get-tuple-element.32.count_ref, s32[4,16]{1,0:T(4,128)S(1)} %get-tuple-element.33.far_ref, f32[16,8,128]{2,1,0:T(8,128)S(1)} %all_to_all.26.recv_ref, bf16[512,128]{1,0:T(8,128)(2,1)S(1)} %get-tuple-element.41.ih_ref, ...), custom_call_target="tpu_custom_call" | custom-call | tf_op jit(solution)/shard_map/second/pallas_call | solution.py:436
  86.8 13.2 %all_to_all.27.recv_ref = f32[32,8,128]{2,1,0:T(8,128)S(1)} all-to-all(f32[32,8,128]{2,1,0:T(8,128)S(1)} %second.1), channel_id=1, replica_groups=mesh['y'=4,'z'=16,'x'=4,'core'=2] {'y','x','core'}, dimensions={0} | all-to-all | bytes 262144 | tf_op jit(solution)/shard_map/all_to_all | solution.py:432
  100.0 0.6 update.3
  (1 shorter events, 0.0 us)
Async XLA Ops:
  2.7 27.6 %all-to-all-start = ((f32[48,4,128]{2,1,0:T(4,128)}), f32[48,4,128]{2,1,0:T(4,128)S(1)}, u32[]{:S(2)}, u32[]{:S(2)}) async-start(f32[48,4,128]{2,1,0:T(4,128)} %get-tuple-element.27), calls=%async_computation | async-start | bytes 196608 | tf_op jit(solution)/shard_map/all_to_all | solution.py:374
  18.4 0.7 copy-start
  30.3 17.4 %all-to-all-start.1 = ((f32[32,8,128]{2,1,0:T(8,128)}), f32[32,8,128]{2,1,0:T(8,128)S(1)}, u32[]{:S(2)}, u32[]{:S(2)}) async-start(f32[32,8,128]{2,1,0:T(8,128)} %get-tuple-element.34), calls=%async_computation.1 | async-start | bytes 262144 | tf_op jit(solution)/shard_map/all_to_all | solution.py:392

commit v7 on v6

--- a/solution.py
+++ b/solution.py
@@ -242,6 +242,24 @@
     acc_ref[rows, cols] = acc_ref[rows, cols] + jnp.dot(jnp.concatenate([q, q], 1), both, preferred_element_type=f32)
 
 
+def in_steps(number, work):
+    def four(j, carry):
+        for k in range(4):
+            work(4 * j + k)
+        return carry
+
+    lax.fori_loop(0, number >> 2, four, 0)
+
+    @pl.when((number & 2) == 2)
+    def _():
+        work((number >> 2) * 4)
+        work((number >> 2) * 4 + 1)
+
+    @pl.when((number & 1) == 1)
+    def _():
+        work(number - 1)
+
+
 def write_sums(acc_ref, out_ref):
     for other in range(NY):
         total = acc_ref[other * 16 : other * 16 + 8] + acc_ref[other * 16 + 8 : other * 16 + 16]
@@ -280,13 +298,12 @@
     for t in range(TILES):
         evaluate_tile(rows, *even, 0, t)
 
-    def pair(j, carry):
+    def pair(j):
         both(2 * j, even, j, 2 * j + 1, odd, j)
         both(2 * j + 1, odd, j, 2 * j + 2, even, j + 1)
-        return carry
 
     pairs = (count - 1) >> 1
-    lax.fori_loop(0, pairs, pair, 0)
+    in_steps(pairs, pair)
 
     @pl.when((count & 1) == 0)
     def _():
@@ -313,16 +330,7 @@
             mul(2 * j, eh_ref, el_ref, j, t)
             mul(2 * j + 1, oh_ref, ol_ref, j, t)
 
-    def four(j, carry):
-        pair(2 * j)
-        pair(2 * j + 1)
-        return carry
-
-    lax.fori_loop(0, count >> 2, four, 0)
-
-    @pl.when((count & 2) == 2)
-    def _():
-        pair((count >> 2) * 2)
+    in_steps(count >> 1, pair)
 
     @pl.when((count & 1) == 1)
     def _():

time: 101 us -> 99.4 us (0.984)
  no operation moved by 1% of the time
where the time goes in v7:
time: 99.4 us; the launch traced here: 99.2 us
  blocking collectives  39.3 us (40%)
  starting transfers between devices  25.6 us (26%)
  Pallas kernels  18.3 us (18%)
  waiting for transfers between devices  14 us (14%)
  between operations  1.34 us (1%)
    all_to_all x2, blocking collectives, update(): lax.all_to_all(sums, plane, 0, 0, tiled=True)  24.4 us
    all_to_all x1, starting transfers between devices, body(): recv = lax.all_to_all(zsend, 'z', 0, 0, tiled=True)  15.7 us
    all_to_all x1, blocking collectives, body(): recv = lax.all_to_all(zsend, 'z', 0, 0, tiled=True)  14.8 us
    all_to_all x1, starting transfers between devices, body(): targets = lax.all_to_all(tsend, plane, 0, 0, tiled=True)  9.84 us
    all_to_all x1, waiting for transfers between devices, body(): recv = lax.all_to_all(zsend, 'z', 0, 0, tiled=True)  8.98 us
    pallas_call x1, Pallas kernels, body(): pl.pallas_call(first_kernel, out_shape=(sds((PLANE, 8, 128)), half, half,...  6.66 us
    all_to_all x1, waiting for transfers between devices, body(): targets = lax.all_to_all(tsend, plane, 0, 0, tiled=True)  5.01 us
    pallas_call x1, Pallas kernels, body(): pl.pallas_call(second_kernel, out_shape=sds((PLANE, 8, 128)), in_specs=[S...  4.85 us
  transfers between devices with their start and end apart: 2, of which 2 were waited for; matrix products, arithmetic and copies ran while one was open for 0% of the time, Pallas kernels for 5%

profile of v7, /device:TPU:1, one launch (start us, length us, event | category | flops | bytes accessed | tf_op | source)
XLA Modules:
  0.0 99.2 jit_solution(740427134753812811)
XLA Ops:
  1.3 1.4 %prologue.1 = (f32[48,4,128]{2,1,0:T(4,128)}, f32[8,128]{1,0:T(8,128)S(1)}) custom-call(s32[1]{0:T(128)S(6)} %copy.10.count_ref, f32[8,128]{1,0:T(8,128)} %charges_hbm.1, f32[3,128]{1,0:T(4,128)} %coords_hbm.1), custom_call_target="tpu_custom_call" | custom-call | tf_op jit(solution)/shard_map/prologue/pallas_call | solution.py:373
  2.7 15.7 %all-to-all-start = ((f32[48,4,128]{2,1,0:T(4,128)}), f32[48,4,128]{2,1,0:T(4,128)S(1)}, u32[]{:S(2)}, u32[]{:S(2)}) async-start(f32[48,4,128]{2,1,0:T(4,128)} %get-tuple-element.27), calls=%async_computation | async-start | bytes 196608 | tf_op jit(solution)/shard_map/all_to_all | solution.py:382
  18.4 0.0 copy-start
  18.4 0.6 copy-done
  19.1 2.2 %prep.1 = (f32[32,8,128]{2,1,0:T(8,128)}, f32[3,8,128]{2,1,0:T(8,128)S(1)}, s32[26,64]{1,0:T(8,128)S(1)}, f32[16,8,128]{2,1,0:T(8,128)S(1)}, bf16[544,128]{1,0:T(8,128)(2,1)S(1)}) custom-call(s32[1]{0:T(128)S(6)} %copy.10.count_ref, f32[8]{0:T(128)S(1)} %copy-done, f32[3,512]{1,0:T(4,128)} %centers_hbm.1, s32[26,64]{1,0:T(8,128)} %bitcast.1, ...), custom_call_target="tpu_custom_call" | custom-call | flops 1000000000 | bytes 12000000 | tf_op jit(solution)/shard_map/prep/pallas_call | solution.py:383
  21.3 9.0 %all-to-all-done.recv_ref = f32[48,4,128]{2,1,0:T(4,128)S(1)} async-done(((f32[48,4,128]{2,1,0:T(4,128)}), f32[48,4,128]{2,1,0:T(4,128)S(1)}, u32[]{:S(2)}, u32[]{:S(2)}) %all-to-all-start) | async-done | bytes 98336 | tf_op jit(solution)/shard_map/all_to_all | solution.py:382
  30.3 9.8 %all-to-all-start.1 = ((f32[32,8,128]{2,1,0:T(8,128)}), f32[32,8,128]{2,1,0:T(8,128)S(1)}, u32[]{:S(2)}, u32[]{:S(2)}) async-start(f32[32,8,128]{2,1,0:T(8,128)} %get-tuple-element.34), calls=%async_computation.1 | async-start | bytes 262144 | tf_op jit(solution)/shard_map/all_to_all | solution.py:400
  40.1 2.6 %setup.1 = (bf16[4096,128]{1,0:T(8,128)(2,1)S(1)}, bf16[512,128]{1,0:T(8,128)(2,1)S(1)}, bf16[512,128]{1,0:T(8,128)(2,1)S(1)}, bf16[33,16,128]{2,1,0:T(8,128)(2,...) custom-call(s32[26,64]{1,0:T(8,128)S(1)} %get-tuple-element.25.near_ref, ...), custom_call_target="tpu_custom_call" | custom-call | flops 1000000000 | bytes 8000000 | tf_op jit(solution)/shard_map/setup/pallas_call | solution.py:402
  42.7 5.0 %all-to-all-done.1.tgt_ref = f32[32,8,128]{2,1,0:T(8,128)S(1)} async-done(((f32[32,8,128]{2,1,0:T(8,128)}), f32[32,8,128]{2,1,0:T(8,128)S(1)}, u32[]{:S(2)}, u32[]{:S(2)}) %all-to-all-start.1) | async-done | bytes 131104 | tf_op jit(solution)/shard_map/all_to_all | solution.py:400
  47.7 6.7 %first.1 = (f32[32,8,128]{2,1,0:T(8,128)S(1)}, bf16[17,4,256,256]{3,2,1,0:T(8,128)(2,1)S(1)}, bf16[17,4,256,256]{3,2,1,0:T(8,128)(2,1)S(1)}, bf16[17,4,256,256]{...) custom-call(s32[128]{0:T(128)S(1)} %get-tuple-element.31.chunk_ref, s32[1]{0:T(128)} %get-tuple-element.32.count_ref, ...), custom_call_target="tpu_custom_call" | custom-call | tf_op jit(solution)/shard_map/first/pallas_call | solution.py:422
  54.4 11.4 %all_to_all.25.recv_ref = f32[32,8,128]{2,1,0:T(8,128)S(1)} all-to-all(f32[32,8,128]{2,1,0:T(8,128)S(1)} %get-tuple-element.37), channel_id=1, replica_groups=mesh['y'=4,'z'=16,'x'=4,'core'=2] {'y','x','core'}, dimensions={0} | all-to-all | bytes 262144 | tf_op jit(solution)/shard_map/all_to_all | solution.py:440
  65.8 14.8 %all_to_all.26.recv_ref = f32[16,8,128]{2,1,0:T(8,128)S(1)} all-to-all(f32[16,8,128]{2,1,0:T(8,128)S(1)} %get-tuple-element.40), channel_id=1, replica_groups=mesh['y'=4,'z'=16,'x'=4,'core'=2] {'z'}, dimensions={0} | all-to-all | bytes 131072 | tf_op jit(solution)/shard_map/all_to_all | solution.py:443
  80.7 4.8 %second.1 = f32[32,8,128]{2,1,0:T(8,128)S(1)} custom-call(s32[128]{0:T(128)S(1)} %get-tuple-element.31.chunk_ref, s32[1]{0:T(128)} %get-tuple-element.32.count_ref, s32[4,16]{1,0:T(4,128)S(1)} %get-tuple-element.33.far_ref, f32[16,8,128]{2,1,0:T(8,128)S(1)} %all_to_all.26.recv_ref, bf16[512,128]{1,0:T(8,128)(2,1)S(1)} %get-tuple-element.41.ih_ref, ...), custom_call_target="tpu_custom_call" | custom-call | tf_op jit(solution)/shard_map/second/pallas_call | solution.py:444
  85.5 13.0 %all_to_all.27.recv_ref = f32[32,8,128]{2,1,0:T(8,128)S(1)} all-to-all(f32[32,8,128]{2,1,0:T(8,128)S(1)} %second.1), channel_id=1, replica_groups=mesh['y'=4,'z'=16,'x'=4,'core'=2] {'y','x','core'}, dimensions={0} | all-to-all | bytes 262144 | tf_op jit(solution)/shard_map/all_to_all | solution.py:440
  98.5 0.6 update.3
  (1 shorter events, 0.0 us)
Async XLA Ops:
  2.7 27.6 %all-to-all-start = ((f32[48,4,128]{2,1,0:T(4,128)}), f32[48,4,128]{2,1,0:T(4,128)S(1)}, u32[]{:S(2)}, u32[]{:S(2)}) async-start(f32[48,4,128]{2,1,0:T(4,128)} %get-tuple-element.27), calls=%async_computation | async-start | bytes 196608 | tf_op jit(solution)/shard_map/all_to_all | solution.py:382
  18.4 0.7 copy-start
  30.3 17.4 %all-to-all-start.1 = ((f32[32,8,128]{2,1,0:T(8,128)}), f32[32,8,128]{2,1,0:T(8,128)S(1)}, u32[]{:S(2)}, u32[]{:S(2)}) async-start(f32[32,8,128]{2,1,0:T(8,128)} %get-tuple-element.34), calls=%async_computation.1 | async-start | bytes 262144 | tf_op jit(solution)/shard_map/all_to_all | solution.py:400

commit v8 on v7

--- a/solution.py
+++ b/solution.py
@@ -125,8 +125,9 @@
     count_ref[0] = total >> 1
 
 
-def prologue_kernel(count_ref, charges_hbm, coords_hbm, zsend_ref, current_ref, coords_ref, sem):
-    copies = [pltpu.make_async_copy(charges_hbm, current_ref, sem.at[0]), pltpu.make_async_copy(coords_hbm, coords_ref, sem.at[1])]
+def prologue_kernel(count_ref, charges_hbm, coords_hbm, targets_hbm, zsend_ref, tsend_ref, current_ref, coords_ref, targets_ref, sem):
+    moves = ((charges_hbm, current_ref), (coords_hbm, coords_ref), (targets_hbm, targets_ref))
+    copies = [pltpu.make_async_copy(source, target, sem.at[k]) for k, (source, target) in enumerate(moves)]
     for copy in copies:
         copy.start()
     for copy in copies:
@@ -138,46 +139,9 @@
         zsend_ref[3 * k] = current[0:4]
         zsend_ref[3 * k + 1] = current[4:8]
         zsend_ref[3 * k + 2] = coords
-
-
-def prep_kernel(
-    count_ref, steps_ref, centers_hbm, near_hbm, boundary_hbm, targets_hbm,
-    tsend_ref, held_ref, near_ref, center_ref, proxy_ref,
-    centers_ref, targets_ref, sem,
-):
-    y, _, member = here()
-    moves = ((targets_hbm, targets_ref), (centers_hbm, centers_ref), (boundary_hbm, held_ref.at[0]), (near_hbm, near_ref))
-    copies = [pltpu.make_async_copy(source, target, sem.at[k]) for k, (source, target) in enumerate(moves)]
-    for copy in copies:
-        copy.start()
-    lane = iota((8, 128), 1)
-    row = iota((8, 128), 0)
-    p = lane & 31
-    offset = jnp.where(
-        row == 0,
-        pick(p >> 4, cheby_nodes(2)),
-        jnp.where(row == 1, pick((p >> 2) & 3, cheby_nodes(4)), jnp.where(row == 2, pick(p & 3, cheby_nodes(4)), 0.0)),
-    )
-    steps = jnp.zeros((8, 128), f32)
-    for k in range(8):
-        steps = jnp.where(row == k, steps_ref[k], steps)
-    held_ref[1] = steps
-    held_ref[2] = (lane < count_ref[0]).astype(f32)
-    for copy in copies:
-        copy.wait()
     rows = target_rows(jnp.concatenate([targets_ref[...], jnp.zeros((5, 128), f32)], 0))
     for k in range(PLANE):
         tsend_ref[k] = rows
-    for block in range(4):
-        center = jnp.zeros((8, 128), f32)
-        for k in range(4):
-            leaf = (y * NZ + block * 4 + k) * MEMBERS + member
-            column = column3(centers_ref[0, leaf], centers_ref[1, leaf], centers_ref[2, leaf], (8, 128))
-            center_ref[block * 4 + k] = column
-            center = jnp.where((lane >> 5) == k, column, center)
-        rows = source_rows(center + HALF_SIDE * offset)
-        proxy_ref[block * 128 : (block + 1) * 128, :DEPTH] = a_block(rows)
-    proxy_ref[512:544, :DEPTH] = proxy_ref[0:32, :DEPTH]
 
 
 def charge_blocks(charges, ih_ref, il_ref, far_ref, q_ref, wide_ref):
@@ -208,15 +172,18 @@
 
 
 def setup_kernel(
-    near_ref, center_ref, recv_ref, proxy_ref, a_ref, ih_ref, il_ref, q_ref, far_ref, chunk_ref, count_ref, wide_ref
+    count_ref, steps_ref, centers_hbm, near_hbm, boundary_hbm, recv_ref,
+    a_ref, ih_ref, il_ref, q_ref, held_ref, far_ref, chunk_ref, chunks_ref,
+    wide_ref, proxy_ref, centers_ref, near_ref, sem,
 ):
-    y, z, _ = here()
-    make_lists(y, z, near_ref, far_ref, chunk_ref, count_ref)
+    y, z, member = here()
+    moves = ((near_hbm, near_ref), (centers_hbm, centers_ref), (boundary_hbm, held_ref.at[0]))
+    copies = [pltpu.make_async_copy(source, target, sem.at[k]) for k, (source, target) in enumerate(moves)]
+    for copy in copies:
+        copy.start()
     tables = interp_tables()
     for k in range(NZ):
         rows = recv_ref[3 * k + 2]
-        points = center_ref[k] + HALF_SIDE * jnp.concatenate([rows, jnp.zeros((4, 128), f32)], 0)
-        a_ref[k * 128 : (k + 1) * 128, :DEPTH] = a_block(source_rows(points))
         value = None
         for axis, (roots, scale) in enumerate(tables):
             u = jnp.broadcast_to(rows[axis : axis + 1], (32, 128))
@@ -227,6 +194,33 @@
         hi, lo = split2(value)
         ih_ref[k * 32 : (k + 1) * 32] = hi
         il_ref[k * 32 : (k + 1) * 32] = lo
+    lane = iota((8, 128), 1)
+    row = iota((8, 128), 0)
+    p = lane & 31
+    offset = jnp.where(
+        row == 0,
+        pick(p >> 4, cheby_nodes(2)),
+        jnp.where(row == 1, pick((p >> 2) & 3, cheby_nodes(4)), jnp.where(row == 2, pick(p & 3, cheby_nodes(4)), 0.0)),
+    )
+    steps = jnp.zeros((8, 128), f32)
+    for k in range(8):
+        steps = jnp.where(row == k, steps_ref[k], steps)
+    held_ref[1] = steps
+    held_ref[2] = (lane < count_ref[0]).astype(f32)
+    for copy in copies:
+        copy.wait()
+    make_lists(y, z, near_ref, far_ref, chunk_ref, chunks_ref)
+    for block in range(4):
+        center = jnp.zeros((8, 128), f32)
+        for k in range(4):
+            place = block * 4 + k
+            leaf = (y * NZ + place) * MEMBERS + member
+            column = column3(centers_ref[0, leaf], centers_ref[1, leaf], centers_ref[2, leaf], (8, 128))
+            points = column + HALF_SIDE * jnp.concatenate([recv_ref[3 * place + 2], jnp.zeros((4, 128), f32)], 0)
+            a_ref[place * 128 : (place + 1) * 128, :DEPTH] = a_block(source_rows(points))
+            center = jnp.where((lane >> 5) == k, column, center)
+        proxy_ref[block * 128 : (block + 1) * 128, :DEPTH] = a_block(source_rows(center + HALF_SIDE * offset))
+    proxy_ref[512:544, :DEPTH] = proxy_ref[0:32, :DEPTH]
     for other in range(NY):
         for k in range(NZ):
             base = (FAR + other * 4) * 128 + k * 32
@@ -369,54 +363,44 @@
     params = pltpu.CompilerParams(vmem_limit_bytes=12 * 2**20)
     small = pltpu.CompilerParams(vmem_limit_bytes=4 * 2**20)
     hbm = functools.partial(pltpu.with_memory_space_constraint, memory_space=pltpu.HBM)
-    charges, source_coords, boundary_data, target_points = map(hbm, (charges, source_coords, boundary_data, target_points))
-    zsend, current = pl.pallas_call(
+    zsend, tsend, current = pl.pallas_call(
         prologue_kernel,
-        out_shape=(sds((3 * NZ, 4, 128)), sds((8, 128))),
-        in_specs=[SM, HB, HB],
-        out_specs=(VM, VM),
-        scratch_shapes=[pltpu.VMEM((3, 128), f32), pltpu.SemaphoreType.DMA((2,))],
+        out_shape=(sds((3 * NZ, 4, 128)), sds((PLANE, 8, 128)), sds((8, 128))),
+        in_specs=[SM, HB, HB, HB],
+        out_specs=(VM,) * 3,
+        scratch_shapes=[pltpu.VMEM((3, 128), f32), pltpu.VMEM((3, 128), f32), pltpu.SemaphoreType.DMA((3,))],
         compiler_params=small,
         name="prologue",
-    )(valid_count, charges, source_coords)
+    )(valid_count, hbm(charges), hbm(source_coords), hbm(target_points))
     recv = lax.all_to_all(zsend, "z", 0, 0, tiled=True)
-    tsend, held, near, centers, proxies = pl.pallas_call(
-        prep_kernel,
-        out_shape=(
-            sds((PLANE, 8, 128)),
-            sds((3, 8, 128)),
-            sds((NEAR, NY * NZ), jnp.int32),
-            sds((NZ, 8, 128)),
-            sds((544, 128), bf16),
-        ),
-        in_specs=[SM, SM, HB, HB, HB, HB],
-        out_specs=(VM,) * 5,
-        scratch_shapes=[pltpu.SMEM((3, NZ * NY * MEMBERS), f32), pltpu.VMEM((3, 128), f32), pltpu.SemaphoreType.DMA((4,))],
-        compiler_params=small,
-        cost_estimate=pl.CostEstimate(flops=10**9, bytes_accessed=12 * 10**6, transcendentals=0),
-        name="prep",
-    )(valid_count, step_sizes, hbm(leaf_centers), hbm(near_lists.T), boundary_data, target_points)
-    recv, tsend = lax.optimization_barrier((recv, tsend))
+    recv, tsend, step_sizes = lax.optimization_barrier((recv, tsend, step_sizes))
     targets = lax.all_to_all(tsend, plane, 0, 0, tiled=True)
     interp = sds((NZ * 32, 128), bf16)
-    a, ih, il, q, far, chunks, count = pl.pallas_call(
+    a, ih, il, q, held, far, chunks, count = pl.pallas_call(
         setup_kernel,
         out_shape=(
             sds((ZERO_BLOCK * 128, 128), bf16),
             interp,
             interp,
             sds((ZERO_BLOCK + 1, 16, 128), bf16),
+            sds((3, 8, 128)),
             sds((NY, FAR_SLOTS), jnp.int32),
             sds((CHUNK_SLOTS,), jnp.int32),
             sds((1,), jnp.int32),
         ),
-        in_specs=[SM, VM, VM, VM],
-        out_specs=(VM,) * 4 + (SM,) * 3,
-        scratch_shapes=[pltpu.VMEM((5, 16, 128), f32)],
+        in_specs=[SM, SM, HB, HB, HB, VM],
+        out_specs=(VM,) * 5 + (SM,) * 3,
+        scratch_shapes=[
+            pltpu.VMEM((5, 16, 128), f32),
+            pltpu.VMEM((544, 128), bf16),
+            pltpu.SMEM((3, NZ * NY * MEMBERS), f32),
+            pltpu.SMEM((NEAR, NY * NZ), jnp.int32),
+            pltpu.SemaphoreType.DMA((3,)),
+        ],
         compiler_params=params,
-        cost_estimate=pl.CostEstimate(flops=10**9, bytes_accessed=8 * 10**6, transcendentals=0),
+        cost_estimate=pl.CostEstimate(flops=10**9, bytes_accessed=12 * 10**6, transcendentals=0),
         name="setup",
-    )(near, centers, recv, proxies)
+    )(valid_count, step_sizes, hbm(leaf_centers), hbm(near_lists.T), hbm(boundary_data), recv)
     scale = 1.0 / math.sqrt(NY * NZ * MEMBERS * 128)
     half = pltpu.VMEM((PAIRS, TILES, 256, TILE), bf16)
     sums, *kernels = pl.pallas_call(

time: 99.4 us -> 99.3 us (level)
  blocking collectives: 39.3 us -> 65.9 us
  starting transfers between devices: 25.6 us -> 9.84 us
  waiting for transfers between devices: 14 us -> 3.74 us
  Pallas kernels: 18.3 us -> 17.2 us
    all_to_all x1 -> x2, blocking collectives: 14.8 us -> 42.5 us  [body(): recv = lax.all_to_all(zsend, 'z', 0, 0, tiled=True)]
    all_to_all x1 -> x0, starting transfers between devices: 15.7 us -> none  [body(): recv = lax.all_to_all(zsend, 'z', 0, 0, tiled=True)]
    all_to_all x1 -> x0, waiting for transfers between devices: 8.98 us -> none  [body(): recv = lax.all_to_all(zsend, 'z', 0, 0, tiled=True)]
    pallas_call x2 -> x1, Pallas kernels: 3.58 us -> 1.41 us  [body(): pl.pallas_call(prologue_kernel, out_shape=(sds((3 * NZ, 4, 128)), sds((PL...]
    all_to_all x1, waiting for transfers between devices: 5.01 us -> 3.74 us  [body(): targets = lax.all_to_all(tsend, plane, 0, 0, tiled=True)]
    all_to_all x2, blocking collectives: 24.4 us -> 23.3 us  [update(): lax.all_to_all(sums, plane, 0, 0, tiled=True)]
  transfers between devices with their start and end apart: 2 -> 1, of which waited for: 2 -> 1; matrix products, arithmetic and copies ran while one was open for 0% -> 0% of each run, Pallas kernels for 5% -> 3%
where the time goes in v8:
time: 99.3 us; the launch traced here: 98.6 us
  blocking collectives  65.9 us (66%)
  Pallas kernels  17.2 us (17%)
  starting transfers between devices  9.84 us (10%)
  waiting for transfers between devices  3.74 us (4%)
  between operations  1.33 us (1%)
    all_to_all x2, blocking collectives, body(): recv = lax.all_to_all(zsend, 'z', 0, 0, tiled=True)  42.5 us
    all_to_all x2, blocking collectives, update(): lax.all_to_all(sums, plane, 0, 0, tiled=True)  23.3 us
    all_to_all x1, starting transfers between devices, body(): targets = lax.all_to_all(tsend, plane, 0, 0, tiled=True)  9.84 us
    pallas_call x1, Pallas kernels, body(): pl.pallas_call(first_kernel, out_shape=(sds((PLANE, 8, 128)), half, half,...  6.83 us
    pallas_call x1, Pallas kernels, body(): pl.pallas_call(second_kernel, out_shape=sds((PLANE, 8, 128)), in_specs=[S...  5.1 us
    all_to_all x1, waiting for transfers between devices, body(): targets = lax.all_to_all(tsend, plane, 0, 0, tiled=True)  3.74 us
    pallas_call x1, Pallas kernels, body(): pl.pallas_call(setup_kernel, out_shape=(sds((ZERO_BLOCK * 128, 128), bf16...  3.2 us
  transfers between devices with their start and end apart: 1, of which 1 were waited for; matrix products, arithmetic and copies ran while one was open for 0% of the time, Pallas kernels for 3%

profile of v8, /device:TPU:1, one launch (start us, length us, event | category | flops | bytes accessed | tf_op | source)
XLA Modules:
  0.0 98.6 jit_solution(351548106018759594)
XLA Ops:
  1.3 1.4 %prologue.1 = (f32[48,4,128]{2,1,0:T(4,128)S(1)}, f32[32,8,128]{2,1,0:T(8,128)}, f32[8,128]{1,0:T(8,128)S(1)}) custom-call(s32[1]{0:T(128)S(6)} %copy.10.count_ref, f32[8,128]{1,0:T(8,128)} %charges_hbm.1, f32[3,128]{1,0:T(4,128)} %coords_hbm.1, f32[3,128]{1,0:T(4,128)} %targets_hbm.1), custom_call_target="tpu_custom_call" | custom-call | tf_op jit(solution)/shard_map/prologue/pallas_call | solution.py:366
  2.7 27.4 %all_to_all.25.recv_ref = f32[48,4,128]{2,1,0:T(4,128)S(1)} all-to-all(f32[48,4,128]{2,1,0:T(4,128)S(1)} %get-tuple-element.23), channel_id=1, replica_groups=mesh['y'=4,'z'=16,'x'=4,'core'=2] {'z'}, dimensions={0} | all-to-all | bytes 196608 | tf_op jit(solution)/shard_map/all_to_all | solution.py:375
  30.1 9.8 %all-to-all-start.1 = ((f32[32,8,128]{2,1,0:T(8,128)}), f32[32,8,128]{2,1,0:T(8,128)S(1)}, u32[]{:S(2)}, u32[]{:S(2)}) async-start(f32[32,8,128]{2,1,0:T(8,128)} %get-tuple-element.30), calls=%async_computation.1 | async-start | bytes 262144 | tf_op jit(solution)/shard_map/all_to_all | solution.py:377
  39.9 0.0 copy-start
  39.9 0.6 copy-done
  40.6 3.2 %setup.1 = (bf16[4096,128]{1,0:T(8,128)(2,1)S(1)}, bf16[512,128]{1,0:T(8,128)(2,1)S(1)}, bf16[512,128]{1,0:T(8,128)(2,1)S(1)}, bf16[33,16,128]{2,1,0:T(8,128)(2,...) custom-call(s32[1]{0:T(128)S(6)} %copy.10.count_ref, f32[8]{0:T(128)S(1)} %copy-done, ...), custom_call_target="tpu_custom_call" | custom-call | flops 1000000000 | bytes 12000000 | tf_op jit(solution)/shard_map/setup/pallas_call | solution.py:379
  43.8 3.7 %all-to-all-done.1.tgt_ref = f32[32,8,128]{2,1,0:T(8,128)S(1)} async-done(((f32[32,8,128]{2,1,0:T(8,128)}), f32[32,8,128]{2,1,0:T(8,128)S(1)}, u32[]{:S(2)}, u32[]{:S(2)}) %all-to-all-start.1) | async-done | bytes 131104 | tf_op jit(solution)/shard_map/all_to_all | solution.py:377
  47.5 6.8 %first.1 = (f32[32,8,128]{2,1,0:T(8,128)S(1)}, bf16[17,4,256,256]{3,2,1,0:T(8,128)(2,1)S(1)}, bf16[17,4,256,256]{3,2,1,0:T(8,128)(2,1)S(1)}, bf16[17,4,256,256]{...) custom-call(s32[128]{0:T(128)S(1)} %get-tuple-element.27.chunk_ref, s32[1]{0:T(128)} %get-tuple-element.28.count_ref, ...), custom_call_target="tpu_custom_call" | custom-call | tf_op jit(solution)/shard_map/first/pallas_call | solution.py:406
  54.4 10.8 %all_to_all.26.recv_ref = f32[32,8,128]{2,1,0:T(8,128)S(1)} all-to-all(f32[32,8,128]{2,1,0:T(8,128)S(1)} %get-tuple-element.33), channel_id=1, replica_groups=mesh['y'=4,'z'=16,'x'=4,'core'=2] {'y','x','core'}, dimensions={0} | all-to-all | bytes 262144 | tf_op jit(solution)/shard_map/all_to_all | solution.py:424
  65.2 15.1 %all_to_all.27.recv_ref = f32[16,8,128]{2,1,0:T(8,128)S(1)} all-to-all(f32[16,8,128]{2,1,0:T(8,128)S(1)} %get-tuple-element.36), channel_id=1, replica_groups=mesh['y'=4,'z'=16,'x'=4,'core'=2] {'z'}, dimensions={0} | all-to-all | bytes 131072 | tf_op jit(solution)/shard_map/all_to_all | solution.py:427
  80.3 5.1 %second.1 = f32[32,8,128]{2,1,0:T(8,128)S(1)} custom-call(s32[128]{0:T(128)S(1)} %get-tuple-element.27.chunk_ref, s32[1]{0:T(128)} %get-tuple-element.28.count_ref, s32[4,16]{1,0:T(4,128)S(1)} %get-tuple-element.29.far_ref, f32[16,8,128]{2,1,0:T(8,128)S(1)} %all_to_all.27.recv_ref, bf16[512,128]{1,0:T(8,128)(2,1)S(1)} %get-tuple-element.37.ih_ref, ...), custom_call_target="tpu_custom_call" | custom-call | tf_op jit(solution)/shard_map/second/pallas_call | solution.py:428
  85.5 12.5 %all_to_all.28.recv_ref = f32[32,8,128]{2,1,0:T(8,128)S(1)} all-to-all(f32[32,8,128]{2,1,0:T(8,128)S(1)} %second.1), channel_id=1, replica_groups=mesh['y'=4,'z'=16,'x'=4,'core'=2] {'y','x','core'}, dimensions={0} | all-to-all | bytes 262144 | tf_op jit(solution)/shard_map/all_to_all | solution.py:424
  98.0 0.6 update.3
  (1 shorter events, 0.0 us)
Async XLA Ops:
  30.1 17.4 %all-to-all-start.1 = ((f32[32,8,128]{2,1,0:T(8,128)}), f32[32,8,128]{2,1,0:T(8,128)S(1)}, u32[]{:S(2)}, u32[]{:S(2)}) async-start(f32[32,8,128]{2,1,0:T(8,128)} %get-tuple-element.30), calls=%async_computation.1 | async-start | bytes 262144 | tf_op jit(solution)/shard_map/all_to_all | solution.py:377
  39.9 0.7 copy-start

commit v9 on v8

--- a/solution.py
+++ b/solution.py
@@ -64,10 +64,8 @@
 
 
 def target_rows(pts):
-    row = iota(pts.shape, 0)
-    t = jnp.where(row < 3, pts - 0.5, 0.0)
-    norm = jnp.sum(t * t, axis=0, keepdims=True)
-    return jnp.where(row < 3, t, jnp.where(row == 3, 1.0, jnp.where(row == 4, norm, 0.0)))
+    t = pts - 0.5
+    return jnp.concatenate([t, jnp.sum(t * t, axis=0, keepdims=True)], 0)
 
 
 def column3(a, b, c, shape):
@@ -139,7 +137,7 @@
         zsend_ref[3 * k] = current[0:4]
         zsend_ref[3 * k + 1] = current[4:8]
         zsend_ref[3 * k + 2] = coords
-    rows = target_rows(jnp.concatenate([targets_ref[...], jnp.zeros((5, 128), f32)], 0))
+    rows = target_rows(targets_ref[...])
     for k in range(PLANE):
         tsend_ref[k] = rows
 
@@ -172,12 +170,12 @@
 
 
 def setup_kernel(
-    count_ref, steps_ref, centers_hbm, near_hbm, boundary_hbm, recv_ref,
+    count_ref, steps_hbm, centers_hbm, near_hbm, boundary_hbm, recv_ref,
     a_ref, ih_ref, il_ref, q_ref, held_ref, far_ref, chunk_ref, chunks_ref,
-    wide_ref, proxy_ref, centers_ref, near_ref, sem,
+    wide_ref, proxy_ref, centers_ref, near_ref, steps_ref, sem,
 ):
     y, z, member = here()
-    moves = ((near_hbm, near_ref), (centers_hbm, centers_ref), (boundary_hbm, held_ref.at[0]))
+    moves = ((near_hbm, near_ref), (centers_hbm, centers_ref), (boundary_hbm, held_ref.at[0]), (steps_hbm, steps_ref))
     copies = [pltpu.make_async_copy(source, target, sem.at[k]) for k, (source, target) in enumerate(moves)]
     for copy in copies:
         copy.start()
@@ -202,13 +200,13 @@
         pick(p >> 4, cheby_nodes(2)),
         jnp.where(row == 1, pick((p >> 2) & 3, cheby_nodes(4)), jnp.where(row == 2, pick(p & 3, cheby_nodes(4)), 0.0)),
     )
+    held_ref[2] = (lane < count_ref[0]).astype(f32)
+    for copy in copies:
+        copy.wait()
     steps = jnp.zeros((8, 128), f32)
     for k in range(8):
         steps = jnp.where(row == k, steps_ref[k], steps)
     held_ref[1] = steps
-    held_ref[2] = (lane < count_ref[0]).astype(f32)
-    for copy in copies:
-        copy.wait()
     make_lists(y, z, near_ref, far_ref, chunk_ref, chunks_ref)
     for block in range(4):
         center = jnp.zeros((8, 128), f32)
@@ -263,7 +261,9 @@
 
 def first_kernel(chunk_ref, count_ref, tgt_ref, a_ref, q_ref, out_ref, eh_ref, el_ref, oh_ref, ol_ref, b_ref, acc_ref):
     for other in range(NY):
-        h, m, low = split3(jnp.concatenate([tgt_ref[other * MEMBERS + k] for k in range(MEMBERS)], 1))
+        got = jnp.concatenate([tgt_ref[other * MEMBERS + k] for k in range(MEMBERS)], 1)
+        one, none = jnp.ones((1, MEMBERS * 128), f32), jnp.zeros((3, MEMBERS * 128), f32)
+        h, m, low = split3(jnp.concatenate([got[0:3], one, got[3:4], none], 0))
         b_ref[other] = jnp.concatenate([h, m, h, m, low, h], 0).astype(bf16)
     acc_ref[...] = jnp.zeros_like(acc_ref)
     count = count_ref[0]
@@ -365,7 +365,7 @@
     hbm = functools.partial(pltpu.with_memory_space_constraint, memory_space=pltpu.HBM)
     zsend, tsend, current = pl.pallas_call(
         prologue_kernel,
-        out_shape=(sds((3 * NZ, 4, 128)), sds((PLANE, 8, 128)), sds((8, 128))),
+        out_shape=(sds((3 * NZ, 4, 128)), sds((PLANE, 4, 128)), sds((8, 128))),
         in_specs=[SM, HB, HB, HB],
         out_specs=(VM,) * 3,
         scratch_shapes=[pltpu.VMEM((3, 128), f32), pltpu.VMEM((3, 128), f32), pltpu.SemaphoreType.DMA((3,))],
@@ -373,7 +373,7 @@
         name="prologue",
     )(valid_count, hbm(charges), hbm(source_coords), hbm(target_points))
     recv = lax.all_to_all(zsend, "z", 0, 0, tiled=True)
-    recv, tsend, step_sizes = lax.optimization_barrier((recv, tsend, step_sizes))
+    recv, tsend = lax.optimization_barrier((recv, tsend))
     targets = lax.all_to_all(tsend, plane, 0, 0, tiled=True)
     interp = sds((NZ * 32, 128), bf16)
     a, ih, il, q, held, far, chunks, count = pl.pallas_call(
@@ -388,19 +388,20 @@
             sds((CHUNK_SLOTS,), jnp.int32),
             sds((1,), jnp.int32),
         ),
-        in_specs=[SM, SM, HB, HB, HB, VM],
+        in_specs=[SM, HB, HB, HB, HB, VM],
         out_specs=(VM,) * 5 + (SM,) * 3,
         scratch_shapes=[
             pltpu.VMEM((5, 16, 128), f32),
             pltpu.VMEM((544, 128), bf16),
             pltpu.SMEM((3, NZ * NY * MEMBERS), f32),
             pltpu.SMEM((NEAR, NY * NZ), jnp.int32),
-            pltpu.SemaphoreType.DMA((3,)),
+            pltpu.SMEM((8,), f32),
+            pltpu.SemaphoreType.DMA((4,)),
         ],
         compiler_params=params,
         cost_estimate=pl.CostEstimate(flops=10**9, bytes_accessed=12 * 10**6, transcendentals=0),
         name="setup",
-    )(valid_count, step_sizes, hbm(leaf_centers), hbm(near_lists.T), hbm(boundary_data), recv)
+    )(valid_count, hbm(step_sizes), hbm(leaf_centers), hbm(near_lists.T), hbm(boundary_data), recv)
     scale = 1.0 / math.sqrt(NY * NZ * MEMBERS * 128)
     half = pltpu.VMEM((PAIRS, TILES, 256, TILE), bf16)
     sums, *kernels = pl.pallas_call(

time: 99.3 us -> 99 us (level)
  Pallas kernels: 17.2 us -> 16 us
  blocking collectives: 65.9 us -> 67 us
where the time goes in v9:
time: 99 us; the launch traced here: 98.8 us
  blocking collectives  67 us (68%)
  Pallas kernels  16 us (16%)
  starting transfers between devices  9.84 us (10%)
  waiting for transfers between devices  4.51 us (5%)
  between operations  1.32 us (1%)
    all_to_all x2, blocking collectives, body(): recv = lax.all_to_all(zsend, 'z', 0, 0, tiled=True)  42.7 us
    all_to_all x2, blocking collectives, update(): lax.all_to_all(sums, plane, 0, 0, tiled=True)  24.3 us
    all_to_all x1, starting transfers between devices, body(): targets = lax.all_to_all(tsend, plane, 0, 0, tiled=True)  9.84 us
    pallas_call x1, Pallas kernels, body(): pl.pallas_call(first_kernel, out_shape=(sds((PLANE, 8, 128)), half, half,...  6.4 us
    pallas_call x1, Pallas kernels, body(): pl.pallas_call(second_kernel, out_shape=sds((PLANE, 8, 128)), in_specs=[S...  4.82 us
    all_to_all x1, waiting for transfers between devices, body(): targets = lax.all_to_all(tsend, plane, 0, 0, tiled=True)  4.51 us
    pallas_call x1, Pallas kernels, body(): pl.pallas_call(setup_kernel, out_shape=(sds((ZERO_BLOCK * 128, 128), bf16...  2.8 us
  transfers between devices with their start and end apart: 1, of which 1 were waited for; matrix products, arithmetic and copies ran while one was open for 0% of the time, Pallas kernels for 3%

profile of v9, /device:TPU:1, one launch (start us, length us, event | category | flops | bytes accessed | tf_op | source)
XLA Modules:
  0.0 98.8 jit_solution(14817876029798872455)
XLA Ops:
  1.3 1.4 %prologue.1 = (f32[48,4,128]{2,1,0:T(4,128)S(1)}, f32[32,4,128]{2,1,0:T(4,128)}, f32[8,128]{1,0:T(8,128)S(1)}) custom-call(s32[1]{0:T(128)S(6)} %copy.10.count_ref, f32[8,128]{1,0:T(8,128)} %charges_hbm.1, f32[3,128]{1,0:T(4,128)} %coords_hbm.1, f32[3,128]{1,0:T(4,128)} %targets_hbm.1), custom_call_target="tpu_custom_call" | custom-call | tf_op jit(solution)/shard_map/prologue/pallas_call | solution.py:366
  2.7 27.4 %all_to_all.25.recv_ref = f32[48,4,128]{2,1,0:T(4,128)S(1)} all-to-all(f32[48,4,128]{2,1,0:T(4,128)S(1)} %get-tuple-element.22), channel_id=1, replica_groups=mesh['y'=4,'z'=16,'x'=4,'core'=2] {'z'}, dimensions={0} | all-to-all | bytes 196608 | tf_op jit(solution)/shard_map/all_to_all | solution.py:375
  30.0 9.8 %all-to-all-start.1 = ((f32[32,4,128]{2,1,0:T(4,128)}), f32[32,4,128]{2,1,0:T(4,128)S(1)}, u32[]{:S(2)}, u32[]{:S(2)}) async-start(f32[32,4,128]{2,1,0:T(4,128)} %get-tuple-element.28), calls=%async_computation.1 | async-start | bytes 131072 | tf_op jit(solution)/shard_map/all_to_all | solution.py:377
  39.9 2.8 %setup.1 = (bf16[4096,128]{1,0:T(8,128)(2,1)S(1)}, bf16[512,128]{1,0:T(8,128)(2,1)S(1)}, bf16[512,128]{1,0:T(8,128)(2,1)S(1)}, bf16[33,16,128]{2,1,0:T(8,128)(2,...) custom-call(s32[1]{0:T(128)S(6)} %copy.10.count_ref, f32[8]{0:T(128)} %steps_hbm.1, ...), custom_call_target="tpu_custom_call" | custom-call | flops 1000000000 | bytes 12000000 | tf_op jit(solution)/shard_map/setup/pallas_call | solution.py:379
  42.7 4.5 %all-to-all-done.1.tgt_ref = f32[32,4,128]{2,1,0:T(4,128)S(1)} async-done(((f32[32,4,128]{2,1,0:T(4,128)}), f32[32,4,128]{2,1,0:T(4,128)S(1)}, u32[]{:S(2)}, u32[]{:S(2)}) %all-to-all-start.1) | async-done | bytes 65568 | tf_op jit(solution)/shard_map/all_to_all | solution.py:377
  47.2 6.4 %first.1 = (f32[32,8,128]{2,1,0:T(8,128)S(1)}, bf16[17,4,256,256]{3,2,1,0:T(8,128)(2,1)S(1)}, bf16[17,4,256,256]{3,2,1,0:T(8,128)(2,1)S(1)}, bf16[17,4,256,256]{...) custom-call(s32[128]{0:T(128)S(1)} %get-tuple-element.25.chunk_ref, s32[1]{0:T(128)} %get-tuple-element.26.count_ref, ...), custom_call_target="tpu_custom_call" | custom-call | tf_op jit(solution)/shard_map/first/pallas_call | solution.py:407
  53.6 11.4 %all_to_all.26.recv_ref = f32[32,8,128]{2,1,0:T(8,128)S(1)} all-to-all(f32[32,8,128]{2,1,0:T(8,128)S(1)} %get-tuple-element.31), channel_id=1, replica_groups=mesh['y'=4,'z'=16,'x'=4,'core'=2] {'y','x','core'}, dimensions={0} | all-to-all | bytes 262144 | tf_op jit(solution)/shard_map/all_to_all | solution.py:425
  65.1 15.4 %all_to_all.27.recv_ref = f32[16,8,128]{2,1,0:T(8,128)S(1)} all-to-all(f32[16,8,128]{2,1,0:T(8,128)S(1)} %get-tuple-element.34), channel_id=1, replica_groups=mesh['y'=4,'z'=16,'x'=4,'core'=2] {'z'}, dimensions={0} | all-to-all | bytes 131072 | tf_op jit(solution)/shard_map/all_to_all | solution.py:428
  80.4 4.8 %second.1 = f32[32,8,128]{2,1,0:T(8,128)S(1)} custom-call(s32[128]{0:T(128)S(1)} %get-tuple-element.25.chunk_ref, s32[1]{0:T(128)} %get-tuple-element.26.count_ref, s32[4,16]{1,0:T(4,128)S(1)} %get-tuple-element.27.far_ref, f32[16,8,128]{2,1,0:T(8,128)S(1)} %all_to_all.27.recv_ref, bf16[512,128]{1,0:T(8,128)(2,1)S(1)} %get-tuple-element.35.ih_ref, ...), custom_call_target="tpu_custom_call" | custom-call | tf_op jit(solution)/shard_map/second/pallas_call | solution.py:429
  85.3 12.9 %all_to_all.28.recv_ref = f32[32,8,128]{2,1,0:T(8,128)S(1)} all-to-all(f32[32,8,128]{2,1,0:T(8,128)S(1)} %second.1), channel_id=1, replica_groups=mesh['y'=4,'z'=16,'x'=4,'core'=2] {'y','x','core'}, dimensions={0} | all-to-all | bytes 262144 | tf_op jit(solution)/shard_map/all_to_all | solution.py:425
  98.1 0.6 update.3
  (1 shorter events, 0.0 us)
Async XLA Ops:
  30.0 17.2 %all-to-all-start.1 = ((f32[32,4,128]{2,1,0:T(4,128)}), f32[32,4,128]{2,1,0:T(4,128)S(1)}, u32[]{:S(2)}, u32[]{:S(2)}) async-start(f32[32,4,128]{2,1,0:T(4,128)} %get-tuple-element.28), calls=%async_computation.1 | async-start | bytes 131072 | tf_op jit(solution)/shard_map/all_to_all | solution.py:377

commit v10 on v9

--- a/solution.py
+++ b/solution.py
@@ -143,22 +143,27 @@
 
 
 def charge_blocks(charges, ih_ref, il_ref, far_ref, q_ref, wide_ref):
-    far = []
     nt = (((1,), (1,)), ((), ()))
-    for k in range(NZ):
-        hi, lo = split2(charges(k))
-        q = jnp.concatenate([hi.astype(f32), lo.astype(f32)], 0).astype(bf16)
-        q_ref[k] = q
-        both = lax.dot_general(q, ih_ref[k * 32 : (k + 1) * 32], nt, preferred_element_type=f32)
-        both = both + lax.dot_general(q, il_ref[k * 32 : (k + 1) * 32], nt, preferred_element_type=f32)
-        far.append(both[0:8] + both[8:16])
-    for k in range(4):
-        wide = jnp.concatenate(far[4 * k : 4 * k + 4], 1)
+    group = iota((16, 128), 1) >> 5
+    for block in range(4):
+        rows = []
+        for k in range(4 * block, 4 * block + 4):
+            hi, lo = split2(charges(k))
+            q = jnp.concatenate([hi.astype(f32), lo.astype(f32)], 0).astype(bf16)
+            q_ref[k] = q
+            rows.append(q)
+        rows = jnp.concatenate(rows, 0)
+        part = slice(block * 128, (block + 1) * 128)
+        both = lax.dot_general(rows, ih_ref[part], nt, preferred_element_type=f32)
+        both = both + lax.dot_general(rows, il_ref[part], nt, preferred_element_type=f32)
+        own = both[0:16]
+        for k in range(1, 4):
+            own = jnp.where(group == k, both[16 * k : 16 * k + 16], own)
+        wide = own[0:8] + own[8:16]
         hi = wide.astype(bf16).astype(f32)
-        wide_ref[k] = jnp.concatenate([hi, wide - hi], 0)
+        wide_ref[block] = jnp.concatenate([hi, wide - hi], 0)
     wide_ref[4] = jnp.zeros((16, 128), f32)
     q_ref[ZERO_BLOCK] = jnp.zeros((16, 128), bf16)
-    group = iota((16, 128), 1) >> 5
     for other in range(NY):
         for block in range(4):
             out = None

time: 99 us -> 99 us (level)
  no operation moved by 1% of the time
where the time goes in v10:
time: 99 us; the launch traced here: 98.9 us
  blocking collectives  66.5 us (67%)
  Pallas kernels  16.8 us (17%)
  starting transfers between devices  9.84 us (10%)
  waiting for transfers between devices  4.49 us (5%)
  between operations  1.32 us (1%)
    all_to_all x2, blocking collectives, body(): recv = lax.all_to_all(zsend, 'z', 0, 0, tiled=True)  42.6 us
    all_to_all x2, blocking collectives, update(): lax.all_to_all(sums, plane, 0, 0, tiled=True)  23.9 us
    all_to_all x1, starting transfers between devices, body(): targets = lax.all_to_all(tsend, plane, 0, 0, tiled=True)  9.84 us
    pallas_call x1, Pallas kernels, body(): pl.pallas_call(first_kernel, out_shape=(sds((PLANE, 8, 128)), half, half,...  6.85 us
    pallas_call x1, Pallas kernels, body(): pl.pallas_call(second_kernel, out_shape=sds((PLANE, 8, 128)), in_specs=[S...  5.06 us
    all_to_all x1, waiting for transfers between devices, body(): targets = lax.all_to_all(tsend, plane, 0, 0, tiled=True)  4.49 us
    pallas_call x1, Pallas kernels, body(): pl.pallas_call(setup_kernel, out_shape=(sds((ZERO_BLOCK * 128, 128), bf16...  2.82 us
  transfers between devices with their start and end apart: 1, of which 1 were waited for; matrix products, arithmetic and copies ran while one was open for 0% of the time, Pallas kernels for 3%

profile of v10, /device:TPU:1, one launch (start us, length us, event | category | flops | bytes accessed | tf_op | source)
XLA Modules:
  0.0 98.9 jit_solution(12652347337970031147)
XLA Ops:
  1.3 1.4 %prologue.1 = (f32[48,4,128]{2,1,0:T(4,128)S(1)}, f32[32,4,128]{2,1,0:T(4,128)}, f32[8,128]{1,0:T(8,128)S(1)}) custom-call(s32[1]{0:T(128)S(6)} %copy.10.count_ref, f32[8,128]{1,0:T(8,128)} %charges_hbm.1, f32[3,128]{1,0:T(4,128)} %coords_hbm.1, f32[3,128]{1,0:T(4,128)} %targets_hbm.1), custom_call_target="tpu_custom_call" | custom-call | tf_op jit(solution)/shard_map/prologue/pallas_call | solution.py:371
  2.7 27.4 %all_to_all.25.recv_ref = f32[48,4,128]{2,1,0:T(4,128)S(1)} all-to-all(f32[48,4,128]{2,1,0:T(4,128)S(1)} %get-tuple-element.22), channel_id=1, replica_groups=mesh['y'=4,'z'=16,'x'=4,'core'=2] {'z'}, dimensions={0} | all-to-all | bytes 196608 | tf_op jit(solution)/shard_map/all_to_all | solution.py:380
  30.0 9.8 %all-to-all-start.1 = ((f32[32,4,128]{2,1,0:T(4,128)}), f32[32,4,128]{2,1,0:T(4,128)S(1)}, u32[]{:S(2)}, u32[]{:S(2)}) async-start(f32[32,4,128]{2,1,0:T(4,128)} %get-tuple-element.28), calls=%async_computation.1 | async-start | bytes 131072 | tf_op jit(solution)/shard_map/all_to_all | solution.py:382
  39.9 2.8 %setup.1 = (bf16[4096,128]{1,0:T(8,128)(2,1)S(1)}, bf16[512,128]{1,0:T(8,128)(2,1)S(1)}, bf16[512,128]{1,0:T(8,128)(2,1)S(1)}, bf16[33,16,128]{2,1,0:T(8,128)(2,...) custom-call(s32[1]{0:T(128)S(6)} %copy.10.count_ref, f32[8]{0:T(128)} %steps_hbm.1, ...), custom_call_target="tpu_custom_call" | custom-call | flops 1000000000 | bytes 12000000 | tf_op jit(solution)/shard_map/setup/pallas_call | solution.py:384
  42.7 4.5 %all-to-all-done.1.tgt_ref = f32[32,4,128]{2,1,0:T(4,128)S(1)} async-done(((f32[32,4,128]{2,1,0:T(4,128)}), f32[32,4,128]{2,1,0:T(4,128)S(1)}, u32[]{:S(2)}, u32[]{:S(2)}) %all-to-all-start.1) | async-done | bytes 65568 | tf_op jit(solution)/shard_map/all_to_all | solution.py:382
  47.2 6.9 %first.1 = (f32[32,8,128]{2,1,0:T(8,128)S(1)}, bf16[17,4,256,256]{3,2,1,0:T(8,128)(2,1)S(1)}, bf16[17,4,256,256]{3,2,1,0:T(8,128)(2,1)S(1)}, bf16[17,4,256,256]{...) custom-call(s32[128]{0:T(128)S(1)} %get-tuple-element.25.chunk_ref, s32[1]{0:T(128)} %get-tuple-element.26.count_ref, ...), custom_call_target="tpu_custom_call" | custom-call | tf_op jit(solution)/shard_map/first/pallas_call | solution.py:412
  54.1 11.2 %all_to_all.26.recv_ref = f32[32,8,128]{2,1,0:T(8,128)S(1)} all-to-all(f32[32,8,128]{2,1,0:T(8,128)S(1)} %get-tuple-element.31), channel_id=1, replica_groups=mesh['y'=4,'z'=16,'x'=4,'core'=2] {'y','x','core'}, dimensions={0} | all-to-all | bytes 262144 | tf_op jit(solution)/shard_map/all_to_all | solution.py:430
  65.3 15.2 %all_to_all.27.recv_ref = f32[16,8,128]{2,1,0:T(8,128)S(1)} all-to-all(f32[16,8,128]{2,1,0:T(8,128)S(1)} %get-tuple-element.34), channel_id=1, replica_groups=mesh['y'=4,'z'=16,'x'=4,'core'=2] {'z'}, dimensions={0} | all-to-all | bytes 131072 | tf_op jit(solution)/shard_map/all_to_all | solution.py:433
  80.5 5.1 %second.1 = f32[32,8,128]{2,1,0:T(8,128)S(1)} custom-call(s32[128]{0:T(128)S(1)} %get-tuple-element.25.chunk_ref, s32[1]{0:T(128)} %get-tuple-element.26.count_ref, s32[4,16]{1,0:T(4,128)S(1)} %get-tuple-element.27.far_ref, f32[16,8,128]{2,1,0:T(8,128)S(1)} %all_to_all.27.recv_ref, bf16[512,128]{1,0:T(8,128)(2,1)S(1)} %get-tuple-element.35.ih_ref, ...), custom_call_target="tpu_custom_call" | custom-call | tf_op jit(solution)/shard_map/second/pallas_call | solution.py:434
  85.5 12.8 %all_to_all.28.recv_ref = f32[32,8,128]{2,1,0:T(8,128)S(1)} all-to-all(f32[32,8,128]{2,1,0:T(8,128)S(1)} %second.1), channel_id=1, replica_groups=mesh['y'=4,'z'=16,'x'=4,'core'=2] {'y','x','core'}, dimensions={0} | all-to-all | bytes 262144 | tf_op jit(solution)/shard_map/all_to_all | solution.py:430
  98.3 0.6 update.3
  (1 shorter events, 0.0 us)
Async XLA Ops:
  30.0 17.2 %all-to-all-start.1 = ((f32[32,4,128]{2,1,0:T(4,128)}), f32[32,4,128]{2,1,0:T(4,128)S(1)}, u32[]{:S(2)}, u32[]{:S(2)}) async-start(f32[32,4,128]{2,1,0:T(4,128)} %get-tuple-element.28), calls=%async_computation.1 | async-start | bytes 131072 | tf_op jit(solution)/shard_map/all_to_all | solution.py:382

commit v11 on v10

--- a/solution.py
+++ b/solution.py
@@ -239,22 +239,23 @@
     acc_ref[rows, cols] = acc_ref[rows, cols] + jnp.dot(jnp.concatenate([q, q], 1), both, preferred_element_type=f32)
 
 
-def in_steps(number, work):
-    def four(j, carry):
-        for k in range(4):
-            work(4 * j + k)
+def in_steps(number, work, most=4):
+    def many(j, carry):
+        for k in range(most):
+            work(most * j + k)
         return carry
 
-    lax.fori_loop(0, number >> 2, four, 0)
-
-    @pl.when((number & 2) == 2)
-    def _():
-        work((number >> 2) * 4)
-        work((number >> 2) * 4 + 1)
-
-    @pl.when((number & 1) == 1)
-    def _():
-        work(number - 1)
+    lax.fori_loop(0, number // most, many, 0)
+    size = most // 2
+    while size:
+
+        @pl.when((number & size) == size)
+        def _(size=size):
+            start = number // (2 * size) * (2 * size)
+            for k in range(size):
+                work(start + k)
+
+        size //= 2
 
 
 def write_sums(acc_ref, out_ref):
@@ -329,7 +330,7 @@
             mul(2 * j, eh_ref, el_ref, j, t)
             mul(2 * j + 1, oh_ref, ol_ref, j, t)
 
-    in_steps(count >> 1, pair)
+    in_steps(count >> 1, pair, 8)
 
     @pl.when((count & 1) == 1)
     def _():

time: 99 us -> 98.8 us (level)
  Pallas kernels: 16.8 us -> 15.3 us
where the time goes in v11:
time: 98.8 us; the launch traced here: 98.2 us
  blocking collectives  67.2 us (68%)
  Pallas kernels  15.3 us (15%)
  starting transfers between devices  9.84 us (10%)
  waiting for transfers between devices  4.49 us (5%)
  between operations  1.32 us (1%)
    all_to_all x2, blocking collectives, body(): recv = lax.all_to_all(zsend, 'z', 0, 0, tiled=True)  42.3 us
    all_to_all x2, blocking collectives, update(): lax.all_to_all(sums, plane, 0, 0, tiled=True)  24.9 us
    all_to_all x1, starting transfers between devices, body(): targets = lax.all_to_all(tsend, plane, 0, 0, tiled=True)  9.84 us
    pallas_call x1, Pallas kernels, body(): pl.pallas_call(first_kernel, out_shape=(sds((PLANE, 8, 128)), half, half,...  6.08 us
    all_to_all x1, waiting for transfers between devices, body(): targets = lax.all_to_all(tsend, plane, 0, 0, tiled=True)  4.49 us
    pallas_call x1, Pallas kernels, body(): pl.pallas_call(second_kernel, out_shape=sds((PLANE, 8, 128)), in_specs=[S...  4.42 us
    pallas_call x1, Pallas kernels, body(): pl.pallas_call(setup_kernel, out_shape=(sds((ZERO_BLOCK * 128, 128), bf16...  2.82 us
  transfers between devices with their start and end apart: 1, of which 1 were waited for; matrix products, arithmetic and copies ran while one was open for 0% of the time, Pallas kernels for 3%

profile of v11, /device:TPU:1, one launch (start us, length us, event | category | flops | bytes accessed | tf_op | source)
XLA Modules:
  0.0 98.2 jit_solution(13192175443500344530)
XLA Ops:
  1.3 1.4 %prologue.1 = (f32[48,4,128]{2,1,0:T(4,128)S(1)}, f32[32,4,128]{2,1,0:T(4,128)}, f32[8,128]{1,0:T(8,128)S(1)}) custom-call(s32[1]{0:T(128)S(6)} %copy.10.count_ref, f32[8,128]{1,0:T(8,128)} %charges_hbm.1, f32[3,128]{1,0:T(4,128)} %coords_hbm.1, f32[3,128]{1,0:T(4,128)} %targets_hbm.1), custom_call_target="tpu_custom_call" | custom-call | tf_op jit(solution)/shard_map/prologue/pallas_call | solution.py:372
  2.7 27.4 %all_to_all.25.recv_ref = f32[48,4,128]{2,1,0:T(4,128)S(1)} all-to-all(f32[48,4,128]{2,1,0:T(4,128)S(1)} %get-tuple-element.22), channel_id=1, replica_groups=mesh['y'=4,'z'=16,'x'=4,'core'=2] {'z'}, dimensions={0} | all-to-all | bytes 196608 | tf_op jit(solution)/shard_map/all_to_all | solution.py:381
  30.0 9.8 %all-to-all-start.1 = ((f32[32,4,128]{2,1,0:T(4,128)}), f32[32,4,128]{2,1,0:T(4,128)S(1)}, u32[]{:S(2)}, u32[]{:S(2)}) async-start(f32[32,4,128]{2,1,0:T(4,128)} %get-tuple-element.28), calls=%async_computation.1 | async-start | bytes 131072 | tf_op jit(solution)/shard_map/all_to_all | solution.py:383
  39.9 2.8 %setup.1 = (bf16[4096,128]{1,0:T(8,128)(2,1)S(1)}, bf16[512,128]{1,0:T(8,128)(2,1)S(1)}, bf16[512,128]{1,0:T(8,128)(2,1)S(1)}, bf16[33,16,128]{2,1,0:T(8,128)(2,...) custom-call(s32[1]{0:T(128)S(6)} %copy.10.count_ref, f32[8]{0:T(128)} %steps_hbm.1, ...), custom_call_target="tpu_custom_call" | custom-call | flops 1000000000 | bytes 12000000 | tf_op jit(solution)/shard_map/setup/pallas_call | solution.py:385
  42.7 4.5 %all-to-all-done.1.tgt_ref = f32[32,4,128]{2,1,0:T(4,128)S(1)} async-done(((f32[32,4,128]{2,1,0:T(4,128)}), f32[32,4,128]{2,1,0:T(4,128)S(1)}, u32[]{:S(2)}, u32[]{:S(2)}) %all-to-all-start.1) | async-done | bytes 65568 | tf_op jit(solution)/shard_map/all_to_all | solution.py:383
  47.2 6.1 %first.1 = (f32[32,8,128]{2,1,0:T(8,128)S(1)}, bf16[17,4,256,256]{3,2,1,0:T(8,128)(2,1)S(1)}, bf16[17,4,256,256]{3,2,1,0:T(8,128)(2,1)S(1)}, bf16[17,4,256,256]{...) custom-call(s32[128]{0:T(128)S(1)} %get-tuple-element.25.chunk_ref, s32[1]{0:T(128)} %get-tuple-element.26.count_ref, ...), custom_call_target="tpu_custom_call" | custom-call | tf_op jit(solution)/shard_map/first/pallas_call | solution.py:413
  53.3 11.8 %all_to_all.26.recv_ref = f32[32,8,128]{2,1,0:T(8,128)S(1)} all-to-all(f32[32,8,128]{2,1,0:T(8,128)S(1)} %get-tuple-element.31), channel_id=1, replica_groups=mesh['y'=4,'z'=16,'x'=4,'core'=2] {'y','x','core'}, dimensions={0} | all-to-all | bytes 262144 | tf_op jit(solution)/shard_map/all_to_all | solution.py:431
  65.1 14.9 %all_to_all.27.recv_ref = f32[16,8,128]{2,1,0:T(8,128)S(1)} all-to-all(f32[16,8,128]{2,1,0:T(8,128)S(1)} %get-tuple-element.34), channel_id=1, replica_groups=mesh['y'=4,'z'=16,'x'=4,'core'=2] {'z'}, dimensions={0} | all-to-all | bytes 131072 | tf_op jit(solution)/shard_map/all_to_all | solution.py:434
  80.0 4.4 %second.1 = f32[32,8,128]{2,1,0:T(8,128)S(1)} custom-call(s32[128]{0:T(128)S(1)} %get-tuple-element.25.chunk_ref, s32[1]{0:T(128)} %get-tuple-element.26.count_ref, s32[4,16]{1,0:T(4,128)S(1)} %get-tuple-element.27.far_ref, f32[16,8,128]{2,1,0:T(8,128)S(1)} %all_to_all.27.recv_ref, bf16[512,128]{1,0:T(8,128)(2,1)S(1)} %get-tuple-element.35.ih_ref, ...), custom_call_target="tpu_custom_call" | custom-call | tf_op jit(solution)/shard_map/second/pallas_call | solution.py:435
  84.4 13.1 %all_to_all.28.recv_ref = f32[32,8,128]{2,1,0:T(8,128)S(1)} all-to-all(f32[32,8,128]{2,1,0:T(8,128)S(1)} %second.1), channel_id=1, replica_groups=mesh['y'=4,'z'=16,'x'=4,'core'=2] {'y','x','core'}, dimensions={0} | all-to-all | bytes 262144 | tf_op jit(solution)/shard_map/all_to_all | solution.py:431
  97.6 0.6 update.3
  (1 shorter events, 0.0 us)
Async XLA Ops:
  30.0 17.2 %all-to-all-start.1 = ((f32[32,4,128]{2,1,0:T(4,128)}), f32[32,4,128]{2,1,0:T(4,128)S(1)}, u32[]{:S(2)}, u32[]{:S(2)}) async-start(f32[32,4,128]{2,1,0:T(4,128)} %get-tuple-element.28), calls=%async_computation.1 | async-start | bytes 131072 | tf_op jit(solution)/shard_map/all_to_all | solution.py:383
